TPU v7x, 128 devices: a whole 4x4x4 slice. The times are simulated.
128 devices in a mesh: dp: 16 (over x, y), expert: 8 (over z, core).
Axes of the slice: x: 4, y: 4, z: 4, core: 2. Of those that a mesh axis runs over, the one named last changes fastest.
Arguments:
- tokens: bfloat16 [2048, 4096], P('dp', 'expert'), may hold values from -6 to 6
- output_gradient: bfloat16 [2048, 4096], P('dp', 'expert'), may hold values from -6 to 6
- routing: int32 [2048, 2], P('dp'), may hold values from 0 to 7, all different within a row; in each aligned block of 128 rows (0 to 127, 128 to 255, ...) at most 96 rows name the same one
- router_gate_values: float32 [2048, 2], P('dp'), may hold values from 0.1 to 0.9
- gate_weight: bfloat16 [8, 7168, 4096], P('expert', 'dp'), may hold values from -0.09375 to 0.09375
- up_weight: bfloat16 [8, 7168, 4096], P('expert', 'dp'), may hold values from -0.09375 to 0.09375
- down_weight: bfloat16 [8, 7168, 4096], P('expert', 'dp'), may hold values from -0.0625 to 0.0625
- adapter_lower_gate: bfloat16 [8, 16, 4096], P('expert'), may hold values from -0.09375 to 0.09375
- adapter_upper_gate: bfloat16 [8, 7168, 16], P('expert', 'dp'), may hold values from -0.375 to 0.375
- adapter_lower_up: bfloat16 [8, 16, 4096], P('expert'), may hold values from -0.09375 to 0.09375
- adapter_upper_up: bfloat16 [8, 7168, 16], P('expert', 'dp'), may hold values from -0.375 to 0.375
- adapter_lower_down: bfloat16 [8, 16, 7168], P('expert', None, 'dp'), may hold values from -0.0625 to 0.0625
- adapter_upper_down: bfloat16 [8, 4096, 16], P('expert'), may hold values from -0.375 to 0.375
Outputs:
- grad_x: bfloat16 [2048, 4096], P('dp', 'expert')
- grad_lora_a_gate: float32 [8, 16, 4096], P('expert')
- grad_lora_b_gate: float32 [8, 7168, 16], P('expert', 'dp')
- grad_lora_a_up: float32 [8, 16, 4096], P('expert')
- grad_lora_b_up: float32 [8, 7168, 16], P('expert', 'dp')
- grad_lora_a_down: float32 [8, 16, 7168], P('expert', None, 'dp')
- grad_lora_b_down: float32 [8, 4096, 16], P('expert')
Inputs may be any that keep to these rules, and one draw needn't show every extreme that they name: `routing`: each row names two different experts. In the rows of one dp shard (aligned blocks of 128 rows) no expert is named by more than 96 rows, and in some blocks one expert is named by exactly 96 rows.
All inputs are finite; a program needn't handle non-finite values.
Results may differ from a plain program's by a relative error of at most 0.015.
Values may be sent and summed in bfloat16 or wider, within the bound.
A program may use at most 256 MiB of HBM per device.

v0:
```python
import jax
import jax.numpy as jnp
from jax import lax
from jax.sharding import PartitionSpec as P

ADAPTER_SCALE = 2.0


def contract_pair(left, right, left_axis, right_axis):
    return lax.dot_general(
        left, right, (((left_axis,), (right_axis,)), ((), ())), preferred_element_type=jnp.float32
    )


def slot_numbers(route_rows, experts):
    picked = (route_rows[:, :, None] == jnp.arange(experts, dtype=jnp.int32)[None, None, :]).astype(
        jnp.int32
    )
    per_token = jnp.sum(picked, axis=1)
    earlier = jnp.cumsum(per_token, axis=0) - per_token
    return jnp.sum(earlier[:, None, :] * picked, axis=2)


def slot_sources(route_rows, positions, experts, capacity):
    tokens_here, choose = route_rows.shape
    target = (route_rows * capacity + positions).reshape(-1)
    owners = jnp.repeat(jnp.arange(tokens_here, dtype=jnp.int32), choose)
    member_ids = jnp.tile(jnp.arange(choose, dtype=jnp.int32), tokens_here)
    source = jnp.full((experts * capacity,), tokens_here, jnp.int32).at[target].set(owners)
    member = jnp.zeros((experts * capacity,), jnp.int32).at[target].set(member_ids)
    return (source, member)


def rows_backward_pass(input_rows, output_gradient_rows, params):
    (
        gate_weight,
        up_weight,
        down_weight,
        a_gate,
        gate_adapter_upper,
        a_up,
        up_adapter_upper,
        down_adapter_lower,
        b_down,
    ) = params
    gate_projected_lower = contract_pair(a_gate, input_rows, 1, 1).astype(jnp.bfloat16)
    up_projected_lower = contract_pair(a_up, input_rows, 1, 1).astype(jnp.bfloat16)
    gate_preactivation = contract_pair(
        gate_weight, input_rows, 1, 1
    ) + ADAPTER_SCALE * contract_pair(gate_adapter_upper, gate_projected_lower, 1, 0)
    up_preactivation = contract_pair(up_weight, input_rows, 1, 1) + ADAPTER_SCALE * contract_pair(
        up_adapter_upper, up_projected_lower, 1, 0
    )
    sigmoid_gate = jax.nn.sigmoid(gate_preactivation)
    silu_gate = gate_preactivation * sigmoid_gate
    hidden_units = (silu_gate * up_preactivation).astype(jnp.bfloat16)
    down_projected_lower = contract_pair(b_down, output_gradient_rows, 0, 1).astype(jnp.bfloat16)
    hidden_gradient = contract_pair(
        down_weight, output_gradient_rows, 1, 1
    ) + ADAPTER_SCALE * contract_pair(down_adapter_lower, down_projected_lower, 0, 0)
    gate_gradient = (
        hidden_gradient
        * up_preactivation
        * sigmoid_gate
        * (1.0 + gate_preactivation * (1.0 - sigmoid_gate))
    ).astype(jnp.bfloat16)
    up_gradient = (hidden_gradient * silu_gate).astype(jnp.bfloat16)
    gate_partial = contract_pair(gate_adapter_upper, gate_gradient, 0, 0).astype(jnp.bfloat16)
    up_partial = contract_pair(up_adapter_upper, up_gradient, 0, 0).astype(jnp.bfloat16)
    down_partial = contract_pair(down_adapter_lower, hidden_units, 1, 0).astype(jnp.bfloat16)
    paired_partials = jnp.concatenate([gate_partial, up_partial], 0)
    paired_factors = jnp.concatenate([a_gate, a_up], 0)
    gradient_rows_out = (
        contract_pair(gate_gradient, gate_weight, 0, 0)
        + contract_pair(up_gradient, up_weight, 0, 0)
        + ADAPTER_SCALE * contract_pair(paired_partials, paired_factors, 0, 0)
    )
    shared_slice = (
        ADAPTER_SCALE * contract_pair(gate_partial, input_rows, 1, 0),
        ADAPTER_SCALE * contract_pair(up_partial, input_rows, 1, 0),
        ADAPTER_SCALE * contract_pair(output_gradient_rows, down_partial, 0, 1),
    )
    owned_slice = (
        ADAPTER_SCALE * contract_pair(gate_gradient, gate_projected_lower, 1, 1),
        ADAPTER_SCALE * contract_pair(up_gradient, up_projected_lower, 1, 1),
        ADAPTER_SCALE * contract_pair(down_projected_lower, hidden_units, 1, 1),
    )
    return (gradient_rows_out, shared_slice, owned_slice)


def local(
    tokens,
    output_gradient,
    routing,
    router_gate_values,
    gate_weight,
    up_weight,
    down_weight,
    adapter_lower_gate,
    adapter_upper_gate,
    adapter_lower_up,
    adapter_upper_up,
    adapter_lower_down,
    adapter_upper_down,
):
    experts = lax.axis_size("expert")
    shards = lax.axis_size("dp")
    tok_local, feat_local = tokens.shape
    choose = routing.shape[1]
    complete_width = feat_local * experts
    capacity = min(tok_local, 6 * tok_local // experts)
    hidden_units_local = gate_weight.shape[1]
    adapter_rank = adapter_lower_gate.shape[1]
    params = (
        gate_weight[0],
        up_weight[0],
        down_weight[0],
        adapter_lower_gate[0],
        adapter_upper_gate[0],
        adapter_lower_up[0],
        adapter_upper_up[0],
        adapter_lower_down[0],
        adapter_upper_down[0],
    )
    positions = slot_numbers(routing, experts)
    zero_row = jnp.zeros((1, feat_local), jnp.bfloat16)
    initial = (
        jnp.zeros((shards * capacity, complete_width), jnp.float32),
        (
            jnp.zeros((adapter_rank, complete_width), jnp.float32),
            jnp.zeros((adapter_rank, complete_width), jnp.float32),
            jnp.zeros((complete_width, adapter_rank), jnp.float32),
        ),
        (
            jnp.zeros((hidden_units_local, adapter_rank), jnp.float32),
            jnp.zeros((hidden_units_local, adapter_rank), jnp.float32),
            jnp.zeros((adapter_rank, hidden_units_local), jnp.float32),
        ),
    )
    source, member = slot_sources(routing, positions, experts, capacity)
    clamped = jnp.minimum(source, tok_local - 1)
    slot_gate = jnp.where(
        source < tok_local, router_gate_values.reshape(-1)[clamped * choose + member], 0.0
    )
    send_x = jnp.concatenate([tokens, zero_row], 0)[source].reshape(experts, capacity, feat_local)
    send_dy = (
        (
            slot_gate[:, None]
            * jnp.concatenate([output_gradient, zero_row], 0)[source].astype(jnp.float32)
        )
        .astype(jnp.bfloat16)
        .reshape(experts, capacity, feat_local)
    )
    recv_x, recv_dy = (
        lax.all_to_all(send_x, "expert", split_axis=0, concat_axis=2, tiled=True),
        lax.all_to_all(send_dy, "expert", split_axis=0, concat_axis=2, tiled=True),
    )
    gradient_rows_out, shared_slice, owned_slice = rows_backward_pass(
        lax.all_gather(recv_x[0], "dp", axis=0, tiled=True),
        lax.all_gather(recv_dy[0], "dp", axis=0, tiled=True),
        params,
    )
    rows_part = gradient_rows_out
    totals = (
        rows_part,
        jax.tree.map(jnp.add, initial[1], shared_slice),
        jax.tree.map(jnp.add, initial[2], owned_slice),
    )
    rows_part, shared_slice, owned_slice = totals
    summed = lax.psum_scatter(
        rows_part.astype(jnp.bfloat16), "dp", scatter_dimension=0, tiled=True
    ).astype(jnp.float32)
    returned_rows = lax.all_to_all(
        summed.reshape(capacity, experts, feat_local).astype(jnp.bfloat16),
        "expert",
        split_axis=1,
        concat_axis=1,
        tiled=True,
    ).astype(jnp.float32)
    lookup = positions * experts + routing
    grad_x = jnp.sum(returned_rows.reshape(capacity * experts, feat_local)[lookup], axis=1).astype(
        jnp.bfloat16
    )
    grad_a_gate, grad_a_up, grad_b_down = (
        lax.psum(shared_slice[0].astype(jnp.bfloat16), "dp").astype(jnp.float32),
        lax.psum(shared_slice[1].astype(jnp.bfloat16), "dp").astype(jnp.float32),
        lax.psum(shared_slice[2].astype(jnp.bfloat16), "dp").astype(jnp.float32),
    )
    return (
        grad_x,
        grad_a_gate[None],
        owned_slice[0][None],
        grad_a_up[None],
        owned_slice[1][None],
        owned_slice[2][None],
        grad_b_down[None],
    )


def solution(mesh):
    return jax.shard_map(
        local,
        mesh=mesh,
        in_specs=(
            P("dp", "expert"),
            P("dp", "expert"),
            P("dp", None),
            P("dp", None),
            P("expert", "dp", None),
            P("expert", "dp", None),
            P("expert", "dp", None),
            P("expert", None, None),
            P("expert", "dp", None),
            P("expert", None, None),
            P("expert", "dp", None),
            P("expert", None, "dp"),
            P("expert", None, None),
        ),
        out_specs=(
            P("dp", "expert"),
            P("expert", None, None),
            P("expert", "dp", None),
            P("expert", None, None),
            P("expert", "dp", None),
            P("expert", None, "dp"),
            P("expert", None, None),
        ),
        check_vma=False,
    )
```

profile of v0, /device:TPU:1, one launch (start us, length us, event | category | flops | bytes accessed | tf_op | source)
XLA Modules:
  0.0 501.6 jit_solution(6191401442853904213)
XLA Ops:
  7.2 0.0 all-gather.5.cloned.1.call-start
  7.2 0.7 convert_reduce_fusion
  7.9 0.1 copy.42
  8.1 0.2 reduce_window_sum.11
  8.3 0.7 select_reduce_fusion
  9.0 0.7 compare_select_fusion.3
  9.7 0.1 copy.45
  9.8 0.1 reshape.84
  10.0 0.1 reshape.137
  10.1 0.1 reshape.129
  10.3 1.4 scatter_custom_fusion.1
  11.7 1.4 scatter_custom_fusion
  13.1 0.9 concatenate.13
  14.0 2.7 gather_fusion.2
  16.7 18.8 %all_to_all.35 = bf16[8,96,512]{2,1,0:T(8,128)(2,1)S(1)} all-to-all(bf16[8,96,512]{2,1,0:T(8,128)(2,1)S(1)} %bitcast.118), channel_id=1, replica_groups=mesh['dp'=16,'expert'=8] {'expert'}, dimensions={0} | all-to-all | bytes 1572864 | tf_op jit(solution)/shard_map/all_to_all | solution.py:155
  35.6 1.0 copy.54
  36.6 0.0 all-gather.3.cloned.1.call-start
  36.6 0.1 copy.46
  36.7 0.1 reshape.86
  36.9 5.0 gather_fusion
  41.9 0.1 mul.106
  42.0 2.7 gather_fusion.1
  44.7 0.2 fusion.23
  44.9 15.7 %all_to_all.36 = bf16[8,96,512]{2,1,0:T(8,128)(2,1)S(1)} all-to-all(bf16[8,96,512]{2,1,0:T(8,128)(2,1)S(1)} %fusion.23), channel_id=1, replica_groups=mesh['dp'=16,'expert'=8] {'expert'}, dimensions={0} | all-to-all | bytes 1572864 | tf_op jit(solution)/shard_map/all_to_all | solution.py:156
  60.6 1.0 copy.53
  61.6 0.6 reduce-scatter.2.cloned.1.call-start
  62.2 64.3 %all-gather.5.cloned.1.call-done = bf16[1536,4096]{1,0:T(8,128)(2,1)} async-done(((bf16[96,4096]{1,0:T(8,128)(2,1)}), bf16[1536,4096]{1,0:T(8,128)(2,1)}) %all-gather.5.cloned.1.call-update) | async-done | bytes 12582928 | tf_op jit(solution)/shard_map/all_gather | solution.py:159
  126.5 8.1 %convolution_convert_fusion.3 = bf16[1536,16]{0,1:T(8,128)(2,1)S(1)} fusion(bf16[1536,4096]{1,0:T(8,128)(2,1)} %all-gather.5.cloned.1.call-done, bf16[1,16,4096]{2,1,0:T(8,128)(2,1)S(1)} %copy-done.5), kind=kOutput, calls=%fused_computation.43 | convolution fusion | flops 201351168 | bytes 12763136 | tf_op jit(solution)/shard_map/dot_general | solution.py:10
  134.5 0.1 copy-done.2
  134.6 8.0 %fusion.8 = f32[1536,448]{0,1:T(8,128)S(1)} fusion(bf16[1536,4096]{1,0:T(8,128)(2,1)S(1)} %copy-done.2, bf16[1,448,4096]{2,1,0:T(8,128)(2,1)} %param.17), kind=kOutput, calls=%fused_computation.18 | convolution fusion | flops 5637144576 | bytes 19005440 | tf_op jit(solution)/shard_map/dot_general | solution.py:10
  142.6 2.1 fusion.21
  144.7 73.6 %all-gather.3.cloned.1.call-done = bf16[1536,4096]{1,0:T(8,128)(2,1)} async-done(((bf16[96,4096]{1,0:T(8,128)(2,1)}), bf16[1536,4096]{1,0:T(8,128)(2,1)}) %all-gather.3.cloned.1.call-update) | async-done | bytes 12582928 | tf_op jit(solution)/shard_map/all_gather | solution.py:160
  218.3 8.1 %convolution_convert_fusion.5 = bf16[1536,16]{0,1:T(8,128)(2,1)S(1)} fusion(bf16[1536,4096]{1,0:T(8,128)(2,1)} %all-gather.3.cloned.1.call-done, bf16[1,4096,16]{1,2,0:T(8,128)(2,1)S(1)} %copy-done), kind=kOutput, calls=%fused_computation.45 | convolution fusion | flops 201351168 | bytes 12763136 | tf_op jit(solution)/shard_map/dot_general | solution.py:10
  226.4 9.3 %fusion.14 = f32[1536,448]{0,1:T(8,128)S(1)} fusion(bf16[1536,4096]{1,0:T(8,128)(2,1)} %all-gather.3.cloned.1.call-done, bf16[1,448,4096]{2,1,0:T(8,128)(2,1)S(1)} %copy-done.12), kind=kOutput, calls=%fused_computation.24 | convolution fusion | flops 5637144576 | bytes 19005440 | tf_op jit(solution)/shard_map/dot_general | solution.py:10
  235.7 0.6 fusion.19
  236.3 0.3 copy-done.6
  236.6 3.3 convolution_convert_fusion.4
  239.9 5.9 %fusion.12 = f32[1536,448]{0,1:T(8,128)S(1)} fusion(bf16[1536,4096]{1,0:T(8,128)(2,1)S(1)} %bitcast.115, bf16[1,448,4096]{2,1,0:T(8,128)(2,1)S(1)} %copy-done.13), kind=kOutput, calls=%fused_computation.22 | convolution fusion | flops 5637144576 | bytes 19005440 | tf_op jit(solution)/shard_map/dot_general | solution.py:10
  245.9 2.7 multiply_convert_fusion
  248.6 0.3 convolution_convert_fusion.1
  248.9 12.0 %fusion.10 = f32[1536,4096]{1,0:T(8,128)} fusion(bf16[448,1536]{1,0:T(8,128)(2,1)S(1)} %get-tuple-element.12, bf16[1,448,4096]{2,1,0:T(8,128)(2,1)S(1)} %copy-done.13), kind=kOutput, calls=%fused_computation.20 | convolution fusion | flops 5637144576 | bytes 30212096 | tf_op jit(solution)/shard_map/dot_general | solution.py:10
  260.8 0.3 convolution_convert_fusion.2
  261.1 11.7 %fusion.6 = f32[1536,4096]{1,0:T(8,128)} fusion(bf16[448,1536]{1,0:T(8,128)(2,1)S(1)} %get-tuple-element.11, bf16[1,448,4096]{2,1,0:T(8,128)(2,1)S(1)} %copy-done.14), kind=kOutput, calls=%fused_computation.16 | convolution fusion | flops 5637144576 | bytes 30212096 | tf_op jit(solution)/shard_map/dot_general | solution.py:10
  272.8 21.9 %add_convert_fusion = bf16[1536,4096]{1,0:T(8,128)(2,1)} fusion(f32[1536,4096]{1,0:T(8,128)} %fusion.6, f32[1536,4096]{1,0:T(8,128)} %fusion.10, bf16[16,4096]{1,0:T(8,128)(2,1)S(1)} %bitcast.128, bf16[16,4096]{1,0:T(8,128)(2,1)S(1)} %bitcast.127, bf16[16,1536]{1,0:T(8,128)(2,1)S(1)} %bitcast.126, bf16[16,1536]{1,0:T(8,128)(2,1)S(1)} %bitcast.125), kind=kOutput, calls=%fused_computation.6 | convolution fusion | flops 428539904 | bytes 63275008 | tf_op jit(solution)/shard_map/dot_general | solution.py:10
  294.7 0.1 copy.51
  294.9 0.1 reshape.119
  295.0 7.0 %fusion.4 = bf16[1,16,4096]{2,1,0:T(8,128)(2,1)} fusion(bf16[1536,16]{0,1:T(8,128)(2,1)S(1)} %convolution_convert_fusion.1, bf16[1536,4096]{1,0:T(8,128)(2,1)} %all-gather.5.cloned.1.call-done), kind=kOutput, calls=%fused_computation.14 | convolution fusion | flops 201457664 | bytes 12763136 | tf_op jit(solution)/shard_map/dot_general | solution.py:10
  302.0 8.2 %fusion.3 = bf16[1,4096,16]{1,2,0:T(8,128)(2,1)} fusion(bf16[1536,4096]{1,0:T(8,128)(2,1)} %all-gather.3.cloned.1.call-done, bf16[448,1536]{1,0:T(8,128)(2,1)} %get-tuple-element.10, bf16[1,16,448]{2,1,0:T(8,128)(2,1)S(1)} %copy-done.9), kind=kOutput, calls=%fused_computation.13 | convolution fusion | flops 223502336 | bytes 14104576 | tf_op jit(solution)/shard_map/dot_general | solution.py:10
  310.2 78.6 %reduce-scatter.2.cloned.1.call-done = bf16[96,4096]{1,0:T(8,128)(2,1)} async-done(((bf16[1536,4096]{1,0:T(8,128)(2,1)}), bf16[96,4096]{1,0:T(8,128)(2,1)}) %reduce-scatter.2.cloned.1.call-update) | async-done | bytes 786448 | tf_op jit(solution)/shard_map/reduce_scatter | solution.py:170
  388.8 2.1 copy.60
  390.9 5.3 %all-to-all-start.2 = ((bf16[96,8,512]{2,0,1:T(8,128)(2,1)}), bf16[96,8,512]{2,0,1:T(8,128)(2,1)}, u32[]{:S(2)}, u32[]{:S(2)}) async-start(bf16[96,8,512]{2,0,1:T(8,128)(2,1)} %bitcast.119), calls=%async_computation.3 | async-start | bytes 1572864 | tf_op jit(solution)/shard_map/all_to_all | solution.py:173
  396.2 0.2 all-reduce.5.cloned.1.call-start
  396.5 7.0 %fusion.5 = bf16[1,16,4096]{2,1,0:T(8,128)(2,1)} fusion(bf16[1536,16]{0,1:T(8,128)(2,1)S(1)} %convolution_convert_fusion.2, bf16[1536,4096]{1,0:T(8,128)(2,1)} %all-gather.5.cloned.1.call-done), kind=kOutput, calls=%fused_computation.15 | convolution fusion | flops 201457664 | bytes 12763136 | tf_op jit(solution)/shard_map/dot_general | solution.py:10
  403.5 1.1 fusion.25
  404.6 1.1 fusion.26
  405.7 1.1 fusion.24
  406.8 78.9 %all-reduce.5.cloned.1.call-done = (bf16[1,16,4096]{2,1,0:T(8,128)(2,1)}, bf16[1,16,4096]{2,1,0:T(8,128)(2,1)}, bf16[1,4096,16]{1,2,0:T(8,128)(2,1)}) async-done(((bf16[1,16,4096]{2,1,0:T(8,128)(2,1)}, bf16[1,16,4096]{2,1,0:T(8,128)(2,1)}, bf16[1,4096,16]{1,2,0:T(8,128)(2,1)}), (bf16[1,16,4096]{2,1,0:T(8,128)(2,1)}, bf16[1,16,4096]{2,1,0:T(8,128)(2,1)}, ...) | async-done | bytes 393232 | tf_op jit(solution)/shard_map/psum | solution.py:185
  485.7 1.6 broadcast_in_dim.57
  487.3 1.6 broadcast_in_dim.60
  489.0 1.6 broadcast_in_dim.64
  490.6 1.6 copy.59
  492.2 1.0 gather_fusion.3
  493.2 0.3 reshape.122
  493.5 1.3 reduce_sum.29
  (50 shorter events, 0.3 us)
Async XLA Ops:
  7.2 211.1 %copy-start = (bf16[1,4096,16]{1,2,0:T(8,128)(2,1)S(1)}, bf16[1,4096,16]{1,2,0:T(8,128)(2,1)}, u32[]{:S(2)}) copy-start(bf16[1,4096,16]{1,2,0:T(8,128)(2,1)} %param.25) | copy-start | bytes 393220
  7.2 119.3 %all-gather.5.cloned.1.call-start = ((), (), s32[]{:S(2)}) async-start(), calls=%async_computation.5 | async-start | bytes 13369344 | tf_op jit(solution)/shard_map/all_gather | solution.py:159
  16.7 19.9 %copy-start.11 = (f32[128,2]{0,1:T(2,128)S(1)}, f32[128,2]{0,1:T(2,128)}, u32[]{:S(2)}) copy-start(f32[128,2]{0,1:T(2,128)} %param.16) | copy-start | bytes 3076
  36.5 5.4 %copy-start.7 = (bf16[128,512]{1,0:T(8,128)(2,1)S(1)}, bf16[128,512]{1,0:T(8,128)(2,1)}, u32[]{:S(2)}) copy-start(bf16[128,512]{1,0:T(8,128)(2,1)} %param.14) | copy-start | bytes 393220
  36.6 181.7 %all-gather.3.cloned.1.call-start = ((), (), s32[]{:S(2)}) async-start(), calls=%async_computation.4 | async-start | bytes 13369344 | tf_op jit(solution)/shard_map/all_gather | solution.py:160
  44.7 81.8 %copy-start.5 = (bf16[1,16,4096]{2,1,0:T(8,128)(2,1)S(1)}, bf16[1,16,4096]{2,1,0:T(8,128)(2,1)}, u32[]{:S(2)}) copy-start(bf16[1,16,4096]{2,1,0:T(8,128)(2,1)} %param.20) | copy-start | bytes 393220
  61.6 327.2 %reduce-scatter.2.cloned.1.call-start = ((), (), s32[]{:S(2)}) async-start(), calls=%async_computation.6 | async-start | bytes 13369344 | tf_op jit(solution)/shard_map/reduce_scatter | solution.py:170
  126.5 8.2 %copy-start.2 = (bf16[1536,4096]{1,0:T(8,128)(2,1)S(1)}, bf16[1536,4096]{1,0:T(8,128)(2,1)}, u32[]{:S(2)}) copy-start(bf16[1536,4096]{1,0:T(8,128)(2,1)} %all-gather.5.cloned.1.call-done) | copy-start | bytes 37748740
  134.6 8.0 %copy-start.8 = (bf16[1,448,16]{1,2,0:T(8,128)(2,1)S(1)}, bf16[1,448,16]{1,2,0:T(8,128)(2,1)}, u32[]{:S(2)}) copy-start(bf16[1,448,16]{1,2,0:T(8,128)(2,1)} %param.21) | copy-start | bytes 43012
  218.3 8.1 %copy-start.12 = (bf16[1,448,4096]{2,1,0:T(8,128)(2,1)S(1)}, bf16[1,448,4096]{2,1,0:T(8,128)(2,1)}, u32[]{:S(2)}) copy-start(bf16[1,448,4096]{2,1,0:T(8,128)(2,1)} %param.19) | copy-start | bytes 11010052
  218.3 18.0 %slice-start = ((s8[12582912]{0:T(1024)(128)(4,1)}), s8[4194304]{0:T(1024)(128)(4,1)S(1)}, s32[]{:S(2)}) async-start(s8[12582912]{0:T(1024)(128)(4,1)} %bitcast.114), calls=%async_computation.8 | async-start | bytes 8388608
  226.3 9.3 %copy-start.9 = (bf16[1,16,448]{2,1,0:T(8,128)(2,1)S(1)}, bf16[1,16,448]{2,1,0:T(8,128)(2,1)}, u32[]{:S(2)}) copy-start(bf16[1,16,448]{2,1,0:T(8,128)(2,1)} %param.24) | copy-start | bytes 43012
  226.3 9.9 %slice-start.1 = ((s8[12582912]{0:T(1024)(128)(4,1)}), s8[4194304]{0:T(1024)(128)(4,1)S(1)}, s32[]{:S(2)}) async-start(s8[12582912]{0:T(1024)(128)(4,1)} %bitcast.114), calls=%async_computation.9 | async-start | bytes 8388608
  226.4 9.9 %slice-start.2 = ((s8[12582912]{0:T(1024)(128)(4,1)}), s8[4194304]{0:T(1024)(128)(4,1)S(1)}, s32[]{:S(2)}) async-start(s8[12582912]{0:T(1024)(128)(4,1)} %bitcast.114), calls=%async_computation.10 | async-start | bytes 8388608
  235.7 0.9 copy-start.6
  236.6 3.3 copy-start.13
  239.9 5.9 %copy-start.4 = (f32[448,1536]{1,0:T(8,128)S(1)}, f32[448,1536]{1,0:T(8,128)}, u32[]{:S(2)}) copy-start(f32[448,1536]{1,0:T(8,128)} %fusion.21) | copy-start | bytes 8257540
  239.9 5.9 %copy-start.10 = (bf16[1,448,16]{1,2,0:T(8,128)(2,1)S(1)}, bf16[1,448,16]{1,2,0:T(8,128)(2,1)}, u32[]{:S(2)}) copy-start(bf16[1,448,16]{1,2,0:T(8,128)(2,1)} %param.23) | copy-start | bytes 43012
  248.9 12.2 %copy-start.14 = (bf16[1,448,4096]{2,1,0:T(8,128)(2,1)S(1)}, bf16[1,448,4096]{2,1,0:T(8,128)(2,1)}, u32[]{:S(2)}) copy-start(bf16[1,448,4096]{2,1,0:T(8,128)(2,1)} %param.17) | copy-start | bytes 11010052
  390.9 99.7 %all-to-all-start.2 = ((bf16[96,8,512]{2,0,1:T(8,128)(2,1)}), bf16[96,8,512]{2,0,1:T(8,128)(2,1)}, u32[]{:S(2)}, u32[]{:S(2)}) async-start(bf16[96,8,512]{2,0,1:T(8,128)(2,1)} %bitcast.119), calls=%async_computation.3 | async-start | bytes 1572864 | tf_op jit(solution)/shard_map/all_to_all | solution.py:173
  396.2 89.5 %all-reduce.5.cloned.1.call-start = ((), (), s32[]{:S(2)}) async-start(), calls=%async_computation.7 | async-start | bytes 786432 | tf_op jit(solution)/shard_map/psum | solution.py:185
  403.5 2.2 copy-start.3
  492.2 2.6 copy-start.1
Sparse Core Ops, SparseCore 0:
  36.7 89.7 all-gather.4
  128.6 89.5 all-gather.2
  294.9 93.8 reduce-scatter.1
  403.6 82.0 all-reduce.4
where the time goes:
time: 507 us; the launch traced here: 502 us
  waiting for transfers between devices  295 us (58%)
  matrix products  120 us (24%)
  blocking collectives  34.5 us (7%)
  local copies, waits for them, and re-layouts  22.7 us (4%)
  between operations  14.4 us (3%)
  other arithmetic  8.74 us (2%)
  starting transfers between devices  6.21 us (1%)
    dot_general x20, matrix products, contract_pair(): lax.dot_general(left, right, (((left_axis,), (right_axis,)), ((), ())), p...  120 us
    psum x1, waiting for transfers between devices, local(): lax.psum(shared_slice[0].astype(jnp.bfloat16), 'dp').astype(jnp.float32)  78.9 us
    reduce_scatter x1, waiting for transfers between devices, local(): lax.psum_scatter(rows_part.astype(jnp.bfloat16), 'dp', scatter_dimension=...  78.6 us
    all_gather x1, waiting for transfers between devices, local(): lax.all_gather(recv_dy[0], 'dp', axis=0, tiled=True)  73.6 us
    all_gather x1, waiting for transfers between devices, local(): lax.all_gather(recv_x[0], 'dp', axis=0, tiled=True)  64.3 us
    all_to_all x1, blocking collectives, local(): lax.all_to_all(send_x, 'expert', split_axis=0, concat_axis=2, tiled=True)  18.8 us
    all_to_all x1, blocking collectives, local(): lax.all_to_all(send_dy, 'expert', split_axis=0, concat_axis=2, tiled=True)  15.7 us
  transfers between devices with their start and end apart: 5, of which 4 were waited for; matrix products, arithmetic and copies ran while one was open for 12% of the time, Pallas kernels for 0%

commit v1 on v0

--- a/solution.py
+++ b/solution.py
@@ -4,6 +4,7 @@
 from jax.sharding import PartitionSpec as P
 
 ADAPTER_SCALE = 2.0
+NUM_CHUNKS = 2
 
 
 def contract_pair(left, right, left_axis, right_axis):
@@ -109,8 +110,9 @@
     choose = routing.shape[1]
     complete_width = feat_local * experts
     capacity = min(tok_local, 6 * tok_local // experts)
-    hidden_units_local = gate_weight.shape[1]
     adapter_rank = adapter_lower_gate.shape[1]
+    chunks = NUM_CHUNKS
+    piece = capacity // chunks
     params = (
         gate_weight[0],
         up_weight[0],
@@ -124,19 +126,6 @@
     )
     positions = slot_numbers(routing, experts)
     zero_row = jnp.zeros((1, feat_local), jnp.bfloat16)
-    initial = (
-        jnp.zeros((shards * capacity, complete_width), jnp.float32),
-        (
-            jnp.zeros((adapter_rank, complete_width), jnp.float32),
-            jnp.zeros((adapter_rank, complete_width), jnp.float32),
-            jnp.zeros((complete_width, adapter_rank), jnp.float32),
-        ),
-        (
-            jnp.zeros((hidden_units_local, adapter_rank), jnp.float32),
-            jnp.zeros((hidden_units_local, adapter_rank), jnp.float32),
-            jnp.zeros((adapter_rank, hidden_units_local), jnp.float32),
-        ),
-    )
     source, member = slot_sources(routing, positions, experts, capacity)
     clamped = jnp.minimum(source, tok_local - 1)
     slot_gate = jnp.where(
@@ -151,27 +140,44 @@
         .astype(jnp.bfloat16)
         .reshape(experts, capacity, feat_local)
     )
-    recv_x, recv_dy = (
-        lax.all_to_all(send_x, "expert", split_axis=0, concat_axis=2, tiled=True),
-        lax.all_to_all(send_dy, "expert", split_axis=0, concat_axis=2, tiled=True),
-    )
-    gradient_rows_out, shared_slice, owned_slice = rows_backward_pass(
-        lax.all_gather(recv_x[0], "dp", axis=0, tiled=True),
-        lax.all_gather(recv_dy[0], "dp", axis=0, tiled=True),
-        params,
-    )
-    rows_part = gradient_rows_out
-    totals = (
-        rows_part,
-        jax.tree.map(jnp.add, initial[1], shared_slice),
-        jax.tree.map(jnp.add, initial[2], owned_slice),
-    )
-    rows_part, shared_slice, owned_slice = totals
-    summed = lax.psum_scatter(
-        rows_part.astype(jnp.bfloat16), "dp", scatter_dimension=0, tiled=True
-    ).astype(jnp.float32)
+    send_both = jnp.concatenate([send_x, send_dy], axis=2)
+    recv_both = lax.all_to_all(send_both, "expert", split_axis=0, concat_axis=2, tiled=True)[0]
+    recv_both = recv_both.reshape(capacity, experts, 2, feat_local).transpose(0, 2, 1, 3)
+    recv_both = recv_both.reshape(capacity, 2 * complete_width)
+
+    rows_pieces = []
+    shared_total = None
+    owned_total = None
+    for c in range(chunks):
+        part = recv_both[c * piece:(c + 1) * piece]
+        gathered = lax.all_gather(part, "dp", axis=0, tiled=True)
+        x_rows = gathered[:, :complete_width]
+        dy_rows = gathered[:, complete_width:]
+        rows_out, shared_slice, owned_slice = rows_backward_pass(x_rows, dy_rows, params)
+        if c == 0:
+            shared_total, owned_total = shared_slice, owned_slice
+        else:
+            shared_total = jax.tree.map(jnp.add, shared_total, shared_slice)
+            owned_total = jax.tree.map(jnp.add, owned_total, owned_slice)
+        rows_bf = rows_out.astype(jnp.bfloat16).reshape(shards, piece, complete_width)
+        summed = lax.psum_scatter(rows_bf, "dp", scatter_dimension=0, tiled=True)[0]
+        rows_pieces.append(summed)
+    lora = jnp.concatenate(
+        [shared_total[0], shared_total[1], shared_total[2].T], 0
+    ).astype(jnp.bfloat16)
+    lora_shape = lora.shape
+    lora_part = lax.psum_scatter(
+        lora.reshape(shards * 8, -1), "dp", scatter_dimension=0, tiled=True
+    )
+    summed = jnp.concatenate(rows_pieces, 0)
+    lora_part = lax.optimization_barrier(lora_part)
+    lora_sum = lax.all_gather(lora_part, "dp", axis=0, tiled=True).astype(jnp.float32)
+    lora_sum = lora_sum.reshape(lora_shape)
+    grad_a_gate = lora_sum[:adapter_rank]
+    grad_a_up = lora_sum[adapter_rank:2 * adapter_rank]
+    grad_b_down = lora_sum[2 * adapter_rank:].T
     returned_rows = lax.all_to_all(
-        summed.reshape(capacity, experts, feat_local).astype(jnp.bfloat16),
+        summed.reshape(capacity, experts, feat_local),
         "expert",
         split_axis=1,
         concat_axis=1,
@@ -181,18 +187,13 @@
     grad_x = jnp.sum(returned_rows.reshape(capacity * experts, feat_local)[lookup], axis=1).astype(
         jnp.bfloat16
     )
-    grad_a_gate, grad_a_up, grad_b_down = (
-        lax.psum(shared_slice[0].astype(jnp.bfloat16), "dp").astype(jnp.float32),
-        lax.psum(shared_slice[1].astype(jnp.bfloat16), "dp").astype(jnp.float32),
-        lax.psum(shared_slice[2].astype(jnp.bfloat16), "dp").astype(jnp.float32),
-    )
     return (
         grad_x,
         grad_a_gate[None],
-        owned_slice[0][None],
+        owned_total[0][None],
         grad_a_up[None],
-        owned_slice[1][None],
-        owned_slice[2][None],
+        owned_total[1][None],
+        owned_total[2][None],
         grad_b_down[None],
     )
 

time: 507 us -> 576 us (1.14)
  waiting for transfers between devices: 295 us -> 324 us
  matrix products: 120 us -> 136 us
  blocking collectives: 34.5 us -> 45.7 us
  local copies, waits for them, and re-layouts: 22.7 us -> 33 us
    unnamed x4 -> x8, waiting for transfers between devices: 0.07 us -> 182 us
    psum x1 -> x0, waiting for transfers between devices: 78.9 us -> none  [local(): lax.psum(shared_slice[0].astype(jnp.bfloat16), 'dp').astype(jnp.float32)]
    reduce_scatter x1 -> x0, waiting for transfers between devices: 78.6 us -> none  [local(): lax.psum_scatter(rows_part.astype(jnp.bfloat16), 'dp', scatter_dimension=...]
    all_gather x0 -> x1, blocking collectives: none -> 18.3 us  [local(): lax.all_gather(lora_part, 'dp', axis=0, tiled=True).astype(jnp.float32)]
    dot_general x20 -> x40, matrix products: 120 us -> 136 us  [contract_pair(): lax.dot_general(left, right, (((left_axis,), (right_axis,)), ((), ())), p...]
    all_to_all x1, waiting for transfers between devices: 0.01 us -> 11.4 us  [local(): lax.all_to_all(summed.reshape(capacity, experts, feat_local), 'expert', s...]
    all_to_all x2 -> x1, blocking collectives: 34.5 us -> 27.4 us  [local(): lax.all_to_all(send_both, 'expert', split_axis=0, concat_axis=2, tiled=True)]
    unnamed x39 -> x99, local copies, waits for them, and re-layouts: 2.55 us -> 9.66 us
  transfers between devices with their start and end apart: 5 -> 6, of which waited for: 4 -> 6; matrix products, arithmetic and copies ran while one was open for 12% -> 17% of each run, Pallas kernels for 0% -> 0%
where the time goes in v1:
time: 576 us; the launch traced here: 568 us
  waiting for transfers between devices  324 us (56%)
  matrix products  136 us (24%)
  blocking collectives  45.7 us (8%)
  local copies, waits for them, and re-layouts  33 us (6%)
  between operations  15.6 us (3%)
  other arithmetic  6.67 us (1%)
  starting transfers between devices  6.65 us (1%)
    unnamed x8, waiting for transfers between devices  182 us
    dot_general x40, matrix products, contract_pair(): lax.dot_general(left, right, (((left_axis,), (right_axis,)), ((), ())), p...  136 us
    all_gather x2, waiting for transfers between devices, local(): gathered = lax.all_gather(part, 'dp', axis=0, tiled=True)  131 us
    all_to_all x1, blocking collectives, local(): lax.all_to_all(send_both, 'expert', split_axis=0, concat_axis=2, tiled=True)  27.4 us
    all_gather x1, blocking collectives, local(): lax.all_gather(lora_part, 'dp', axis=0, tiled=True).astype(jnp.float32)  18.3 us
  transfers between devices with their start and end apart: 6, of which 6 were waited for; matrix products, arithmetic and copies ran while one was open for 17% of the time, Pallas kernels for 0%

profile of v1, /device:TPU:1, one launch (start us, length us, event | category | flops | bytes accessed | tf_op | source)
XLA Modules:
  0.0 568.4 jit_solution(9020184322485059997)
XLA Ops:
  7.2 0.8 convert_reduce_fusion
  8.4 0.7 select_reduce_fusion
  9.1 1.3 compare_select_fusion.3
  10.9 0.8 copy.56
  11.8 1.4 scatter_custom_fusion.1
  13.3 1.4 scatter_custom_fusion
  14.7 5.0 gather_fusion.1
  19.8 2.7 gather_fusion.2
  22.5 2.7 gather_fusion
  25.7 27.4 %all_to_all.20 = bf16[8,96,1024]{2,1,0:T(8,128)(2,1)S(1)} all-to-all(bf16[8,96,1024]{2,1,0:T(8,128)(2,1)S(1)} %pad_maximum_fusion), channel_id=1, replica_groups=mesh['dp'=16,'expert'=8] {'expert'}, dimensions={0} | all-to-all | bytes 3145728 | tf_op jit(solution)/shard_map/all_to_all | solution.py:144
  53.0 1.2 reshape.172
  54.2 1.7 copy.71
  56.0 1.3 fusion.132
  57.5 1.3 copy.65
  59.0 1.3 copy.67
  60.7 88.0 %all-gather.3.cloned.1.call-done = bf16[768,8192]{1,0:T(8,128)(2,1)} async-done(((bf16[48,8192]{1,0:T(8,128)(2,1)}), bf16[768,8192]{1,0:T(8,128)(2,1)}) %all-gather.3.cloned.1.call-update) | async-done | bytes 12582928 | tf_op jit(solution)/shard_map/all_gather | solution.py:153
  148.7 4.7 fusion.79
  153.4 6.0 %fusion.31 = f32[768,448]{0,1:T(8,128)S(1)} fusion(bf16[1,448,4096]{2,1,0:T(8,128)(2,1)S(1)} %copy-done.2, bf16[768,8192]{1,0:T(8,128)(2,1)} %all-gather.3.cloned.1.call-done), kind=kOutput, calls=%fused_computation.35 | convolution fusion | flops 2818572288 | bytes 11337728 | tf_op jit(solution)/shard_map/dot_general | solution.py:11
  159.9 1.7 fusion.88
  161.6 0.7 copy-done.34
  162.3 3.1 fusion.10
  165.8 1.7 fusion.76
  167.9 14.7 %fusion.39 = f32[768,448]{0,1:T(8,128)S(1)} fusion(bf16[1,448,4096]{2,1,0:T(8,128)(2,1)S(1)} %copy-done.4, bf16[768,8192]{1,0:T(8,128)(2,1)S(1)} %bitcast.166), kind=kOutput, calls=%fused_computation.43 | convolution fusion | flops 2818572288 | bytes 11337728 | tf_op jit(solution)/shard_map/dot_general | solution.py:11
  182.6 1.8 multiply_convert_fusion.1
  184.8 6.6 %fusion.29 = f32[768,4096]{1,0:T(8,128)} fusion(bf16[448,768]{1,0:T(8,128)(2,1)S(1)} %get-tuple-element.8, bf16[1,448,4096]{2,1,0:T(8,128)(2,1)S(1)} %copy-done.2), kind=kOutput, calls=%fused_computation.33 | convolution fusion | flops 2818572288 | bytes 16941056 | tf_op jit(solution)/shard_map/dot_general | solution.py:11
  191.4 6.5 %fusion.37 = f32[768,4096]{1,0:T(8,128)} fusion(bf16[448,768]{1,0:T(8,128)(2,1)S(1)} %get-tuple-element.9, bf16[1,448,4096]{2,1,0:T(8,128)(2,1)S(1)} %copy-done.4), kind=kOutput, calls=%fused_computation.41 | convolution fusion | flops 2818572288 | bytes 16941056 | tf_op jit(solution)/shard_map/dot_general | solution.py:11
  197.9 42.7 %all-gather.5.cloned.1.call-done = bf16[768,8192]{1,0:T(8,128)(2,1)} async-done(((bf16[48,8192]{1,0:T(8,128)(2,1)}), bf16[768,8192]{1,0:T(8,128)(2,1)}) %all-gather.5.cloned.1.call-update) | async-done | bytes 12582928 | tf_op jit(solution)/shard_map/all_gather | solution.py:153
  240.5 4.7 fusion.91
  245.2 6.0 %fusion.4 = f32[768,448]{0,1:T(8,128)S(1)} fusion(bf16[768,8192]{1,0:T(8,128)(2,1)} %all-gather.5.cloned.1.call-done, bf16[1,448,4096]{2,1,0:T(8,128)(2,1)S(1)} %copy-done.35), kind=kOutput, calls=%fused_computation.12 | convolution fusion | flops 2818572288 | bytes 11337728 | tf_op jit(solution)/shard_map/dot_general | solution.py:11
  251.7 1.7 fusion.85
  253.7 3.1 fusion.27
  257.2 1.7 fusion.82
  259.2 3.3 fusion.35
  262.5 1.8 multiply_convert_fusion
  265.0 1.6 fusion.53
  266.6 0.9 fusion.51
  267.6 4.1 fusion
  271.7 4.4 fusion.23
  276.0 4.4 fusion.24
  280.4 4.1 fusion.20
  284.5 1.0 pad_maximum_fusion.2
  285.5 1.2 convert_element_type.133
  286.9 12.2 %add_convert_fusion.1 = bf16[768,4096]{1,0:T(8,128)(2,1)} fusion(f32[768,4096]{1,0:T(8,128)} %fusion.29, f32[768,4096]{1,0:T(8,128)} %fusion.37, bf16[16,4096]{1,0:T(8,128)(2,1)S(1)} %bitcast.186, bf16[16,4096]{1,0:T(8,128)(2,1)S(1)} %bitcast.184, bf16[16,768]{1,0:T(8,128)(2,1)} %bitcast.191, bf16[16,768]{1,0:T(8,128)(2,1)} %bitcast.190), kind=kOutput, calls=%fused_computation.7 | convolution fusion | flops 214532096 | bytes 31768576 | tf_op jit(solution)/shard_map/dot_general | solution.py:11
  299.2 8.9 %fusion.25 = f32[768,4096]{1,0:T(8,128)} fusion(bf16[448,768]{1,0:T(8,128)(2,1)S(1)} %get-tuple-element.11, bf16[1,448,4096]{2,1,0:T(8,128)(2,1)} %param.17), kind=kOutput, calls=%fused_computation.29 | convolution fusion | flops 2818572288 | bytes 16941056 | tf_op jit(solution)/shard_map/dot_general | solution.py:11
  308.1 6.4 %fusion.33 = f32[768,4096]{1,0:T(8,128)} fusion(bf16[448,768]{1,0:T(8,128)(2,1)S(1)} %get-tuple-element.12, bf16[1,448,4096]{2,1,0:T(8,128)(2,1)S(1)} %copy-done.6), kind=kOutput, calls=%fused_computation.37 | convolution fusion | flops 2818572288 | bytes 16941056 | tf_op jit(solution)/shard_map/dot_general | solution.py:11
  314.5 12.1 %add_convert_fusion = bf16[768,4096]{1,0:T(8,128)(2,1)} fusion(f32[768,4096]{1,0:T(8,128)} %fusion.25, f32[768,4096]{1,0:T(8,128)} %fusion.33, bf16[16,4096]{1,0:T(8,128)(2,1)S(1)} %bitcast.187, bf16[16,4096]{1,0:T(8,128)(2,1)S(1)} %bitcast.185, bf16[16,768]{1,0:T(8,128)(2,1)S(1)} %bitcast.193, bf16[16,768]{1,0:T(8,128)(2,1)S(1)} %bitcast.192), kind=kOutput, calls=%fused_computation.6 | convolution fusion | flops 214532096 | bytes 31768576 | tf_op jit(solution)/shard_map/dot_general | solution.py:11
  327.6 0.6 dynamic-slice
  328.8 1.4 fusion.135
  330.2 2.1 fusion.95
  332.6 1.0 fusion.97
  333.8 1.0 fusion.99
  334.8 34.6 %all-reduce.7.cloned.1.call-done = bf16[128,1536]{1,0:T(8,128)(2,1)} async-done(((bf16[128,1536]{1,0:T(8,128)(2,1)}), bf16[128,1536]{1,0:T(8,128)(2,1)}) %all-reduce.7.cloned.1.call-update) | async-done | bytes 393232
  369.4 0.7 constant_dynamic-slice_fusion
  370.1 18.3 %all_gather.11 = bf16[128,1536]{1,0:T(8,128)(2,1)S(1)} all-gather(bf16[8,1536]{1,0:T(8,128)(2,1)S(1)} %constant_dynamic-slice_fusion), channel_id=1, replica_groups=mesh['dp'=16,'expert'=8] {'dp'}, dimensions={0}, use_global_device_ids=true | all-gather | bytes 417792 | tf_op jit(solution)/shard_map/all_gather | solution.py:174
  388.9 65.0 %reduce-scatter.7.cloned.1.call-done = bf16[1,48,4096]{2,1,0:T(8,128)(2,1)} async-done(((bf16[16,48,4096]{2,1,0:T(8,128)(2,1)}), bf16[1,48,4096]{2,1,0:T(8,128)(2,1)}) %reduce-scatter.7.cloned.1.call-update) | async-done | bytes 393232
  453.9 1.1 copy.66
  455.1 82.5 %reduce-scatter.9.cloned.1.call-done = bf16[1,48,4096]{2,1,0:T(8,128)(2,1)} async-done(((bf16[16,48,4096]{2,1,0:T(8,128)(2,1)}), bf16[1,48,4096]{2,1,0:T(8,128)(2,1)}) %reduce-scatter.9.cloned.1.call-update) | async-done | bytes 393232
  537.7 1.1 copy.68
  538.9 1.0 pad_maximum_fusion.1
  539.9 6.2 %all-to-all-start.1 = ((bf16[96,8,512]{2,0,1:T(8,128)(2,1)}), bf16[96,8,512]{2,0,1:T(8,128)(2,1)S(1)}, u32[]{:S(2)}, u32[]{:S(2)}) async-start(bf16[96,8,512]{2,0,1:T(8,128)(2,1)} %pad_maximum_fusion.1), calls=%async_computation.1 | async-start | bytes 1572864 | tf_op jit(solution)/shard_map/all_to_all | solution.py:179
  546.1 0.9 slice_bitcast_fusion
  547.0 11.4 %all-to-all-done.1 = bf16[96,8,512]{2,0,1:T(8,128)(2,1)S(1)} async-done(((bf16[96,8,512]{2,0,1:T(8,128)(2,1)}), bf16[96,8,512]{2,0,1:T(8,128)(2,1)S(1)}, u32[]{:S(2)}, u32[]{:S(2)}) %all-to-all-start.1) | async-done | bytes 786464 | tf_op jit(solution)/shard_map/all_to_all | solution.py:179
  558.8 1.0 gather_fusion.3
  560.1 1.3 reduce_sum.29
  (144 shorter events, 9.0 us)
Async XLA Ops:
  7.2 152.7 %copy-start = (bf16[1,4096,16]{1,2,0:T(8,128)(2,1)S(1)}, bf16[1,4096,16]{1,2,0:T(8,128)(2,1)}, u32[]{:S(2)}) copy-start(bf16[1,4096,16]{1,2,0:T(8,128)(2,1)} %param.25) | copy-start | bytes 393220
  7.2 12.6 %copy-start.18 = (bf16[128,512]{1,0:T(8,128)(2,1)S(1)}, bf16[128,512]{1,0:T(8,128)(2,1)}, u32[]{:S(2)}) copy-start(bf16[128,512]{1,0:T(8,128)(2,1)} %param.14) | copy-start | bytes 393220
  7.2 12.6 %copy-start.19 = (bf16[128,512]{1,0:T(8,128)(2,1)S(1)}, bf16[128,512]{1,0:T(8,128)(2,1)}, u32[]{:S(2)}) copy-start(bf16[128,512]{1,0:T(8,128)(2,1)} %param.13) | copy-start | bytes 393220
  7.2 141.5 %all-gather.3.cloned.1.call-start = ((), (), s32[]{:S(2)}) async-start(), calls=%async_computation.4 | async-start | bytes 13369344 | tf_op jit(solution)/shard_map/all_gather | solution.py:153
  57.3 91.4 %copy-start.7 = (bf16[1,16,4096]{2,1,0:T(8,128)(2,1)S(1)}, bf16[1,16,4096]{2,1,0:T(8,128)(2,1)}, u32[]{:S(2)}) copy-start(bf16[1,16,4096]{2,1,0:T(8,128)(2,1)} %param.20) | copy-start | bytes 393220
  58.8 181.7 %all-gather.5.cloned.1.call-start = ((), (), s32[]{:S(2)}) async-start(), calls=%async_computation.5 | async-start | bytes 13369344 | tf_op jit(solution)/shard_map/all_gather | solution.py:153
  60.4 309.0 %all-reduce.7.cloned.1.call-start = ((), (), s32[]{:S(2)}) async-start(), calls=%async_computation.6 | async-start | bytes 786432
  148.7 4.7 copy-start.2
  148.7 11.1 %slice-start = ((s8[12582912]{0:T(1024)(128)(4,1)}), s8[4194304]{0:T(1024)(128)(4,1)S(1)}, s32[]{:S(2)}) async-start(s8[12582912]{0:T(1024)(128)(4,1)} %bitcast.165), calls=%async_computation.9 | async-start | bytes 8388608
  153.4 6.0 %copy-start.20 = (bf16[768,16]{0,1:T(8,128)(2,1)}, bf16[768,16]{0,1:T(8,128)(2,1)S(1)}, u32[]{:S(2)}) copy-start(bf16[768,16]{0,1:T(8,128)(2,1)S(1)} %fusion.79) | copy-start | bytes 73732
  153.4 6.0 %copy-start.11 = (bf16[1,448,16]{1,2,0:T(8,128)(2,1)S(1)}, bf16[1,448,16]{1,2,0:T(8,128)(2,1)}, u32[]{:S(2)}) copy-start(bf16[1,448,16]{1,2,0:T(8,128)(2,1)} %param.21) | copy-start | bytes 43012
  153.4 6.4 %slice-start.1 = ((s8[12582912]{0:T(1024)(128)(4,1)}), s8[4194304]{0:T(1024)(128)(4,1)S(1)}, s32[]{:S(2)}) async-start(s8[12582912]{0:T(1024)(128)(4,1)} %bitcast.165), calls=%async_computation.10 | async-start | bytes 8388608
  153.4 6.4 %slice-start.2 = ((s8[12582912]{0:T(1024)(128)(4,1)}), s8[4194304]{0:T(1024)(128)(4,1)S(1)}, s32[]{:S(2)}) async-start(s8[12582912]{0:T(1024)(128)(4,1)} %bitcast.165), calls=%async_computation.11 | async-start | bytes 8388608
  159.9 2.4 copy-start.34
  162.3 3.1 copy-start.22
  162.3 3.1 copy-start.10
  162.3 3.5 copy-start.8
  165.8 2.1 copy-start.4
  167.9 14.7 %copy-start.29 = (bf16[768,16]{0,1:T(8,128)(2,1)}, bf16[768,16]{0,1:T(8,128)(2,1)S(1)}, u32[]{:S(2)}) copy-start(bf16[768,16]{0,1:T(8,128)(2,1)S(1)} %fusion.76) | copy-start | bytes 73732
  167.9 14.7 %copy-start.28 = (bf16[1,448,16]{1,2,0:T(8,128)(2,1)S(1)}, bf16[1,448,16]{1,2,0:T(8,128)(2,1)}, u32[]{:S(2)}) copy-start(bf16[1,448,16]{1,2,0:T(8,128)(2,1)} %param.23) | copy-start | bytes 43012
  184.6 80.2 %copy-start.12 = (bf16[768,16]{0,1:T(8,128)(2,1)}, bf16[768,16]{0,1:T(8,128)(2,1)S(1)}, u32[]{:S(2)}) copy-start(bf16[768,16]{0,1:T(8,128)(2,1)S(1)} %convolution_convert_fusion.5) | copy-start | bytes 73732
  184.8 81.9 %copy-start.13 = (bf16[768,16]{0,1:T(8,128)(2,1)}, bf16[768,16]{0,1:T(8,128)(2,1)S(1)}, u32[]{:S(2)}) copy-start(bf16[768,16]{0,1:T(8,128)(2,1)S(1)} %convolution_convert_fusion.4) | copy-start | bytes 73732
  240.5 4.7 copy-start.35
  240.5 11.1 %slice-start.6 = ((s8[12582912]{0:T(1024)(128)(4,1)}), s8[4194304]{0:T(1024)(128)(4,1)S(1)}, s32[]{:S(2)}) async-start(s8[12582912]{0:T(1024)(128)(4,1)} %bitcast.169), calls=%async_computation.15 | async-start | bytes 8388608
  245.2 6.0 %copy-start.26 = (bf16[768,16]{0,1:T(8,128)(2,1)}, bf16[768,16]{0,1:T(8,128)(2,1)S(1)}, u32[]{:S(2)}) copy-start(bf16[768,16]{0,1:T(8,128)(2,1)S(1)} %fusion.91) | copy-start | bytes 73732
  245.2 6.4 %slice-start.7 = ((s8[12582912]{0:T(1024)(128)(4,1)}), s8[4194304]{0:T(1024)(128)(4,1)S(1)}, s32[]{:S(2)}) async-start(s8[12582912]{0:T(1024)(128)(4,1)} %bitcast.169), calls=%async_computation.16 | async-start | bytes 8388608
  245.2 6.4 %slice-start.8 = ((s8[12582912]{0:T(1024)(128)(4,1)}), s8[4194304]{0:T(1024)(128)(4,1)S(1)}, s32[]{:S(2)}) async-start(s8[12582912]{0:T(1024)(128)(4,1)} %bitcast.169), calls=%async_computation.17 | async-start | bytes 8388608
  251.6 2.0 copy-start.3
  253.7 3.1 copy-start.24
  257.2 2.0 copy-start.5
  259.2 3.3 copy-start.31
  259.2 5.5 slice-start.3
  259.2 5.6 slice-start.4
  262.5 2.5 slice-start.5
  264.5 7.1 %copy-start.14 = (bf16[768,16]{0,1:T(8,128)(2,1)}, bf16[768,16]{0,1:T(8,128)(2,1)S(1)}, u32[]{:S(2)}) copy-start(bf16[768,16]{0,1:T(8,128)(2,1)S(1)} %convolution_convert_fusion.3) | copy-start | bytes 73732
  265.0 11.1 %copy-start.16 = (bf16[768,16]{0,1:T(8,128)(2,1)}, bf16[768,16]{0,1:T(8,128)(2,1)S(1)}, u32[]{:S(2)}) copy-start(bf16[768,16]{0,1:T(8,128)(2,1)S(1)} %convolution_convert_fusion.2) | copy-start | bytes 73732
  280.4 6.4 %copy-start.9 = (bf16[1,16,4096]{2,1,0:T(8,128)(2,1)S(1)}, bf16[1,16,4096]{2,1,0:T(8,128)(2,1)}, u32[]{:S(2)}) copy-start(bf16[1,16,4096]{2,1,0:T(8,128)(2,1)} %param.22) | copy-start | bytes 393220
  286.8 167.1 %reduce-scatter.7.cloned.1.call-start = ((), (), s32[]{:S(2)}) async-start(), calls=%async_computation.7 | async-start | bytes 6684672
  299.1 238.5 %reduce-scatter.9.cloned.1.call-start = ((), (), s32[]{:S(2)}) async-start(), calls=%async_computation.8 | async-start | bytes 6684672
  299.2 8.9 %copy-start.6 = (bf16[1,448,4096]{2,1,0:T(8,128)(2,1)S(1)}, bf16[1,448,4096]{2,1,0:T(8,128)(2,1)}, u32[]{:S(2)}) copy-start(bf16[1,448,4096]{2,1,0:T(8,128)(2,1)} %param.18) | copy-start | bytes 11010052
  308.1 6.4 %copy-start.15 = (bf16[768,16]{0,1:T(8,128)(2,1)S(1)}, bf16[768,16]{0,1:T(8,128)(2,1)}, u32[]{:S(2)}) copy-start(bf16[768,16]{0,1:T(8,128)(2,1)} %copy-done.14) | copy-start | bytes 73732
  308.1 6.4 %copy-start.17 = (bf16[768,16]{0,1:T(8,128)(2,1)S(1)}, bf16[768,16]{0,1:T(8,128)(2,1)}, u32[]{:S(2)}) copy-start(bf16[768,16]{0,1:T(8,128)(2,1)} %copy-done.16) | copy-start | bytes 73732
  326.6 0.7 copy-start.33
  326.6 0.9 copy-start.36
  326.6 2.2 copy-start.23
  326.6 3.6 copy-start.27
  326.7 5.6 copy-start.30
  326.7 5.9 %copy-start.32 = (bf16[768,16]{0,1:T(8,128)(2,1)S(1)}, bf16[768,16]{0,1:T(8,128)(2,1)}, u32[]{:S(2)}) copy-start(bf16[768,16]{0,1:T(8,128)(2,1)} %copy-done.31) | copy-start | bytes 73732
  326.7 6.9 %copy-start.21 = (bf16[768,16]{0,1:T(8,128)(2,1)S(1)}, bf16[768,16]{0,1:T(8,128)(2,1)}, u32[]{:S(2)}) copy-start(bf16[768,16]{0,1:T(8,128)(2,1)} %copy-done.20) | copy-start | bytes 73732
  326.7 7.2 %copy-start.25 = (bf16[768,16]{0,1:T(8,128)(2,1)S(1)}, bf16[768,16]{0,1:T(8,128)(2,1)}, u32[]{:S(2)}) copy-start(bf16[768,16]{0,1:T(8,128)(2,1)} %copy-done.24) | copy-start | bytes 73732
  539.9 18.5 %all-to-all-start.1 = ((bf16[96,8,512]{2,0,1:T(8,128)(2,1)}), bf16[96,8,512]{2,0,1:T(8,128)(2,1)S(1)}, u32[]{:S(2)}, u32[]{:S(2)}) async-start(bf16[96,8,512]{2,0,1:T(8,128)(2,1)} %pad_maximum_fusion.1), calls=%async_computation.1 | async-start | bytes 1572864 | tf_op jit(solution)/shard_map/all_to_all | solution.py:179
  558.4 3.1 copy-start.1
Sparse Core Ops, SparseCore 0:
  58.9 89.7 all-gather.2
  150.9 89.5 all-gather.4
  286.9 82.4 all-reduce.6
  372.7 81.1 reduce-scatter.6
  457.2 80.4 reduce-scatter.8

commit v2 on v1

--- a/solution.py
+++ b/solution.py
@@ -5,6 +5,7 @@
 
 ADAPTER_SCALE = 2.0
 NUM_CHUNKS = 2
+PART_COLS = 128
 
 
 def contract_pair(left, right, left_axis, right_axis):
@@ -87,6 +88,59 @@
         ADAPTER_SCALE * contract_pair(down_projected_lower, hidden_units, 1, 1),
     )
     return (gradient_rows_out, shared_slice, owned_slice)
+
+
+def rows_backward_parts(input_rows, output_gradient_rows, params):
+    (
+        gate_weight,
+        up_weight,
+        down_weight,
+        a_gate,
+        gate_adapter_upper,
+        a_up,
+        up_adapter_upper,
+        down_adapter_lower,
+        b_down,
+    ) = params
+    gate_projected_lower = contract_pair(a_gate, input_rows, 1, 1).astype(jnp.bfloat16)
+    up_projected_lower = contract_pair(a_up, input_rows, 1, 1).astype(jnp.bfloat16)
+    gate_preactivation = contract_pair(
+        gate_weight, input_rows, 1, 1
+    ) + ADAPTER_SCALE * contract_pair(gate_adapter_upper, gate_projected_lower, 1, 0)
+    up_preactivation = contract_pair(up_weight, input_rows, 1, 1) + ADAPTER_SCALE * contract_pair(
+        up_adapter_upper, up_projected_lower, 1, 0
+    )
+    sigmoid_gate = jax.nn.sigmoid(gate_preactivation)
+    silu_gate = gate_preactivation * sigmoid_gate
+    hidden_units = (silu_gate * up_preactivation).astype(jnp.bfloat16)
+    down_projected_lower = contract_pair(b_down, output_gradient_rows, 0, 1).astype(jnp.bfloat16)
+    hidden_gradient = contract_pair(
+        down_weight, output_gradient_rows, 1, 1
+    ) + ADAPTER_SCALE * contract_pair(down_adapter_lower, down_projected_lower, 0, 0)
+    gate_gradient = (
+        hidden_gradient
+        * up_preactivation
+        * sigmoid_gate
+        * (1.0 + gate_preactivation * (1.0 - sigmoid_gate))
+    ).astype(jnp.bfloat16)
+    up_gradient = (hidden_gradient * silu_gate).astype(jnp.bfloat16)
+    gate_partial = contract_pair(gate_gradient, gate_adapter_upper, 0, 0).astype(jnp.bfloat16)
+    up_partial = contract_pair(up_gradient, up_adapter_upper, 0, 0).astype(jnp.bfloat16)
+    down_partial = contract_pair(hidden_units, down_adapter_lower, 0, 1).astype(jnp.bfloat16)
+    paired_partials = jnp.concatenate([gate_partial, up_partial], 1)
+    paired_factors = jnp.concatenate([a_gate, a_up], 0)
+    gradient_rows_out = (
+        contract_pair(gate_gradient, gate_weight, 0, 0)
+        + contract_pair(up_gradient, up_weight, 0, 0)
+        + ADAPTER_SCALE * contract_pair(paired_partials, paired_factors, 1, 0)
+    )
+    parts = jnp.concatenate([gate_partial, up_partial, down_partial], 1)
+    owned_slice = (
+        ADAPTER_SCALE * contract_pair(gate_gradient, gate_projected_lower, 1, 1),
+        ADAPTER_SCALE * contract_pair(up_gradient, up_projected_lower, 1, 1),
+        ADAPTER_SCALE * contract_pair(down_projected_lower, hidden_units, 1, 1),
+    )
+    return (gradient_rows_out, parts, owned_slice)
 
 
 def local(
@@ -145,37 +199,42 @@
     recv_both = recv_both.reshape(capacity, experts, 2, feat_local).transpose(0, 2, 1, 3)
     recv_both = recv_both.reshape(capacity, 2 * complete_width)
 
-    rows_pieces = []
-    shared_total = None
+    rows_chunks = []
+    part_chunks = []
+    x_chunks = []
+    dy_chunks = []
     owned_total = None
     for c in range(chunks):
         part = recv_both[c * piece:(c + 1) * piece]
         gathered = lax.all_gather(part, "dp", axis=0, tiled=True)
         x_rows = gathered[:, :complete_width]
         dy_rows = gathered[:, complete_width:]
-        rows_out, shared_slice, owned_slice = rows_backward_pass(x_rows, dy_rows, params)
+        rows_out, parts, owned_slice = rows_backward_parts(x_rows, dy_rows, params)
         if c == 0:
-            shared_total, owned_total = shared_slice, owned_slice
+            owned_total = owned_slice
         else:
-            shared_total = jax.tree.map(jnp.add, shared_total, shared_slice)
             owned_total = jax.tree.map(jnp.add, owned_total, owned_slice)
-        rows_bf = rows_out.astype(jnp.bfloat16).reshape(shards, piece, complete_width)
-        summed = lax.psum_scatter(rows_bf, "dp", scatter_dimension=0, tiled=True)[0]
-        rows_pieces.append(summed)
-    lora = jnp.concatenate(
-        [shared_total[0], shared_total[1], shared_total[2].T], 0
-    ).astype(jnp.bfloat16)
-    lora_shape = lora.shape
-    lora_part = lax.psum_scatter(
-        lora.reshape(shards * 8, -1), "dp", scatter_dimension=0, tiled=True
-    )
-    summed = jnp.concatenate(rows_pieces, 0)
-    lora_part = lax.optimization_barrier(lora_part)
-    lora_sum = lax.all_gather(lora_part, "dp", axis=0, tiled=True).astype(jnp.float32)
-    lora_sum = lora_sum.reshape(lora_shape)
-    grad_a_gate = lora_sum[:adapter_rank]
-    grad_a_up = lora_sum[adapter_rank:2 * adapter_rank]
-    grad_b_down = lora_sum[2 * adapter_rank:].T
+        rows_chunks.append(rows_out.astype(jnp.bfloat16).reshape(shards, piece, complete_width))
+        part_chunks.append(parts.reshape(shards, piece, 3 * adapter_rank))
+        x_chunks.append(x_rows.reshape(shards, piece, complete_width))
+        dy_chunks.append(dy_rows.reshape(shards, piece, complete_width))
+    rows_all = jnp.concatenate(rows_chunks, 1)
+    parts_all = jnp.concatenate(part_chunks, 1)
+    parts_all = jnp.pad(parts_all, ((0, 0), (0, 0), (0, PART_COLS - 3 * adapter_rank)))
+    packed = jnp.concatenate([rows_all, parts_all], 2)
+    summed_packed = lax.psum_scatter(packed, "dp", scatter_dimension=0, tiled=True)[0]
+    summed = summed_packed[:, :complete_width]
+    parts_mine = summed_packed[:, complete_width:complete_width + 3 * adapter_rank]
+    parts_sum = lax.all_gather(parts_mine, "dp", axis=0, tiled=True)
+    parts_sum = parts_sum.reshape(shards, capacity, 3 * adapter_rank)
+    x_all = jnp.concatenate(x_chunks, 1).reshape(shards * capacity, complete_width)
+    dy_all = jnp.concatenate(dy_chunks, 1).reshape(shards * capacity, complete_width)
+    parts_sum = parts_sum.reshape(shards * capacity, 3 * adapter_rank)
+    grad_a_gate = ADAPTER_SCALE * contract_pair(parts_sum[:, :adapter_rank], x_all, 0, 0)
+    grad_a_up = ADAPTER_SCALE * contract_pair(
+        parts_sum[:, adapter_rank:2 * adapter_rank], x_all, 0, 0
+    )
+    grad_b_down = ADAPTER_SCALE * contract_pair(dy_all, parts_sum[:, 2 * adapter_rank:], 0, 0)
     returned_rows = lax.all_to_all(
         summed.reshape(capacity, experts, feat_local),
         "expert",

time: 576 us -> 477 us (0.83)
  waiting for transfers between devices: 324 us -> 207 us
  other arithmetic: 6.67 us -> 32 us
  matrix products: 136 us -> 117 us
  local copies, waits for them, and re-layouts: 33 us -> 42.5 us
    unnamed x8 -> x4, waiting for transfers between devices: 182 us -> 60 us
    concatenate x2 -> x6, other arithmetic: 1.96 us -> 27.9 us  [the longest x1 10.4 us: local(): packed = jnp.concatenate([rows_all, parts_all], 2)]
    dot_general x40 -> x39, matrix products: 136 us -> 117 us  [contract_pair(): lax.dot_general(left, right, (((left_axis,), (right_axis,)), ((), ())), p...]
    slice x0 -> x3, local copies, waits for them, and re-layouts: none -> 12.7 us  [the longest x2 11.6 us: local(): dy_rows = gathered[:, complete_width:]]
    all_gather x2, waiting for transfers between devices: 131 us -> 142 us  [local(): gathered = lax.all_gather(part, 'dp', axis=0, tiled=True)]
    all_to_all x1, waiting for transfers between devices: 11.4 us -> 5.27 us  [local(): lax.all_to_all(summed.reshape(capacity, experts, feat_local), 'expert', s...]
  transfers between devices with their start and end apart: 6 -> 4, of which waited for: 6 -> 4; matrix products, arithmetic and copies ran while one was open for 17% -> 17% of each run, Pallas kernels for 0% -> 0%
where the time goes in v2:
time: 477 us; the launch traced here: 470 us
  waiting for transfers between devices  207 us (43%)
  matrix products  117 us (25%)
  blocking collectives  44.1 us (9%)
  local copies, waits for them, and re-layouts  42.5 us (9%)
  other arithmetic  32 us (7%)
  between operations  14.6 us (3%)
  starting transfers between devices  12 us (3%)
    all_gather x2, waiting for transfers between devices, local(): gathered = lax.all_gather(part, 'dp', axis=0, tiled=True)  142 us
    dot_general x39, matrix products, contract_pair(): lax.dot_general(left, right, (((left_axis,), (right_axis,)), ((), ())), p...  117 us
    unnamed x4, waiting for transfers between devices  60 us
    all_to_all x1, blocking collectives, local(): lax.all_to_all(send_both, 'expert', split_axis=0, concat_axis=2, tiled=True)  27.4 us
    all_gather x1, blocking collectives, local(): parts_sum = lax.all_gather(parts_mine, 'dp', axis=0, tiled=True)  16.7 us
    slice x2, local copies, waits for them, and re-layouts, local(): dy_rows = gathered[:, complete_width:]  11.6 us
    all_to_all x1, starting transfers between devices, local(): lax.all_to_all(summed.reshape(capacity, experts, feat_local), 'expert', s...  11.4 us
    concatenate x1, other arithmetic, local(): packed = jnp.concatenate([rows_all, parts_all], 2)  10.4 us
  transfers between devices with their start and end apart: 4, of which 4 were waited for; matrix products, arithmetic and copies ran while one was open for 17% of the time, Pallas kernels for 0%

profile of v2, /device:TPU:1, one launch (start us, length us, event | category | flops | bytes accessed | tf_op | source)
XLA Modules:
  0.0 469.6 jit_solution(13800577406468424391)
XLA Ops:
  7.2 0.8 convert_reduce_fusion
  8.4 0.7 select_reduce_fusion
  9.1 0.7 compare_select_fusion.3
  10.0 0.8 copy.79
  11.3 1.4 scatter_custom_fusion.1
  12.7 1.4 scatter_custom_fusion
  14.1 5.0 %gather_fusion.1 = f32[768]{0:T(1024)S(1)} fusion(f32[256]{0:T(256)S(1)} %reshape.120, s32[1024]{0:T(1024)S(1)} %get-tuple-element.23), kind=kCustom, calls=%fused_computation.1 | custom fusion | bytes 9216 | tf_op jit(solution)/shard_map/gather | solution.py:186
  19.2 2.7 gather_fusion.2
  21.9 2.7 gather_fusion
  25.1 27.4 %all_to_all.20 = bf16[8,96,1024]{2,1,0:T(8,128)(2,1)S(1)} all-to-all(bf16[8,96,1024]{2,1,0:T(8,128)(2,1)S(1)} %pad_maximum_fusion.3), channel_id=1, replica_groups=mesh['dp'=16,'expert'=8] {'expert'}, dimensions={0} | all-to-all | bytes 3145728 | tf_op jit(solution)/shard_map/all_to_all | solution.py:198
  52.5 1.2 reshape.192
  53.6 1.7 copy.99
  55.4 1.3 fusion.94
  56.9 1.4 copy.94
  58.4 1.3 copy.95
  59.8 0.5 reduce-scatter.4.cloned.1.call-start
  60.3 87.8 %all-gather.4.cloned.1.call-done = bf16[768,8192]{1,0:T(8,128)(2,1)} async-done(((bf16[48,8192]{1,0:T(8,128)(2,1)}), bf16[768,8192]{1,0:T(8,128)(2,1)}) %all-gather.4.cloned.1.call-update) | async-done | bytes 12582928 | tf_op jit(solution)/shard_map/all_gather | solution.py:209
  148.2 4.7 convolution_convert_fusion.11
  152.9 6.0 %fusion.21 = f32[768,448]{0,1:T(8,128)S(1)} fusion(bf16[1,448,4096]{2,1,0:T(8,128)(2,1)S(1)} %copy-done.29, bf16[768,8192]{1,0:T(8,128)(2,1)} %all-gather.4.cloned.1.call-done), kind=kOutput, calls=%fused_computation.35 | convolution fusion | flops 2818572288 | bytes 11337728 | tf_op jit(solution)/shard_map/dot_general | solution.py:12
  159.4 1.7 convolution_convert_fusion.10
  161.1 0.7 copy-done.3
  161.7 3.1 fusion.17
  165.2 1.7 convolution_convert_fusion.9
  167.3 3.3 fusion.9
  170.6 1.9 multiply_convert_fusion.5
  172.9 6.4 %fusion.15 = f32[768,4096]{1,0:T(8,128)} fusion(bf16[448,768]{1,0:T(8,128)(2,1)S(1)} %get-tuple-element.13, bf16[1,448,4096]{2,1,0:T(8,128)(2,1)S(1)} %copy-done.3), kind=kOutput, calls=%fused_computation.29 | convolution fusion | flops 2818572288 | bytes 16941056 | tf_op jit(solution)/shard_map/dot_general | solution.py:12
  179.3 6.3 %fusion.7 = f32[768,4096]{1,0:T(8,128)} fusion(bf16[448,768]{1,0:T(8,128)(2,1)S(1)} %get-tuple-element.11, bf16[1,448,4096]{2,1,0:T(8,128)(2,1)S(1)} %copy-done.5), kind=kOutput, calls=%fused_computation.21 | convolution fusion | flops 2818572288 | bytes 16941056 | tf_op jit(solution)/shard_map/dot_general | solution.py:12
  185.6 54.4 %all-gather.6.cloned.1.call-done = bf16[768,8192]{1,0:T(8,128)(2,1)} async-done(((bf16[48,8192]{1,0:T(8,128)(2,1)}), bf16[768,8192]{1,0:T(8,128)(2,1)}) %all-gather.6.cloned.1.call-update) | async-done | bytes 12582928 | tf_op jit(solution)/shard_map/all_gather | solution.py:209
  240.0 4.7 convolution_convert_fusion.8
  244.7 6.0 %fusion.19 = f32[768,448]{0,1:T(8,128)S(1)} fusion(bf16[1,448,4096]{2,1,0:T(8,128)(2,1)S(1)} %copy-done.30, bf16[768,8192]{1,0:T(8,128)(2,1)} %all-gather.6.cloned.1.call-done), kind=kOutput, calls=%fused_computation.33 | convolution fusion | flops 2818572288 | bytes 11337728 | tf_op jit(solution)/shard_map/dot_general | solution.py:12
  251.1 1.7 convolution_convert_fusion.7
  253.1 3.1 fusion.13
  256.6 1.7 convolution_convert_fusion.6
  258.7 3.5 fusion.5
  262.1 1.0 multiply_convert_fusion.3
  263.3 6.3 %fusion.11 = f32[768,4096]{1,0:T(8,128)} fusion(bf16[448,768]{1,0:T(8,128)(2,1)S(1)} %get-tuple-element.16, bf16[1,448,4096]{2,1,0:T(8,128)(2,1)S(1)} %copy-done.4), kind=kOutput, calls=%fused_computation.25 | convolution fusion | flops 2818572288 | bytes 16941056 | tf_op jit(solution)/shard_map/dot_general | solution.py:12
  269.9 6.3 %fusion.3 = f32[768,4096]{1,0:T(8,128)} fusion(bf16[448,768]{1,0:T(8,128)(2,1)S(1)} %get-tuple-element.14, bf16[1,448,4096]{2,1,0:T(8,128)(2,1)S(1)} %copy-done.6), kind=kOutput, calls=%fused_computation.17 | convolution fusion | flops 2818572288 | bytes 16941056 | tf_op jit(solution)/shard_map/dot_general | solution.py:12
  276.6 1.3 convolution_convert_fusion.1
  278.3 9.3 %add_convert_fusion.1 = bf16[768,4096]{1,0:T(8,128)(2,1)S(1)} fusion(f32[768,4096]{1,0:T(8,128)} %fusion.7, f32[768,4096]{1,0:T(8,128)} %fusion.15, bf16[16,4096]{1,0:T(8,128)(2,1)S(1)} %bitcast.196, bf16[16,4096]{1,0:T(8,128)(2,1)S(1)} %bitcast.198, bf16[768,16]{0,1:T(8,128)(2,1)} %copy-done.13, bf16[768,16]{0,1:T(8,128)(2,1)} %copy-done.12), kind=kOutput, calls=%fused_computation.10 | convolution fusion | flops 214532096 | bytes 31768576 | tf_op jit(solution)/shard_map/dot_general | solution.py:12
  287.5 12.0 %add_convert_fusion = bf16[768,4096]{1,0:T(8,128)(2,1)} fusion(f32[768,4096]{1,0:T(8,128)} %fusion.3, f32[768,4096]{1,0:T(8,128)} %fusion.11, bf16[16,4096]{1,0:T(8,128)(2,1)S(1)} %bitcast.197, bf16[16,4096]{1,0:T(8,128)(2,1)S(1)} %bitcast.199, bf16[768,16]{0,1:T(8,128)(2,1)S(1)} %convolution_convert_fusion.2, bf16[768,16]{0,1:T(8,128)(2,1)S(1)} %convolution_convert_fusion.3), kind=kOutput, calls=%fused_computation.9 | convolution fusion | flops 214532096 | bytes 31768576 | tf_op jit(solution)/shard_map/dot_general | solution.py:12
  299.5 10.4 %pad_maximum_fusion = bf16[16,96,4224]{2,1,0:T(8,128)(2,1)} fusion(bf16[16,96,128]{2,1,0:T(8,128)(2,1)S(1)} %fusion.46, bf16[16,48,4096]{2,1,0:T(8,128)(2,1)} %bitcast.176, bf16[16,48,4096]{2,1,0:T(8,128)(2,1)S(1)} %bitcast.172), kind=kLoop, calls=%fused_computation.6 | loop fusion | flops 38928384 | bytes 25952256 | tf_op jit(solution)/shard_map/concatenate | solution.py:224
  310.3 0.4 copy-done.19
  310.7 1.4 fusion.97
  312.1 2.1 fusion.39
  314.4 1.0 fusion.43
  315.7 1.0 fusion.41
  316.6 5.9 %fusion.93 = (bf16[768,4096]{1,0:T(8,128)(2,1)S(1)}, bf16[768,4096]{1,0:T(8,128)(2,1)S(1)}) fusion(bf16[768,8192]{1,0:T(8,128)(2,1)} %all-gather.6.cloned.1.call-done), kind=kLoop, calls=%fused_computation.158 | loop fusion | bytes 25165824 | tf_op jit(solution)/shard_map/slice | solution.py:211
  322.5 5.7 %fusion.92 = (bf16[768,4096]{1,0:T(8,128)(2,1)S(1)}, bf16[768,4096]{1,0:T(8,128)(2,1)S(1)}) fusion(bf16[768,8192]{1,0:T(8,128)(2,1)} %all-gather.4.cloned.1.call-done), kind=kLoop, calls=%fused_computation.157 | loop fusion | bytes 25165824 | tf_op jit(solution)/shard_map/slice | solution.py:211
  328.2 8.7 %pad_maximum_fusion.2 = bf16[16,96,4096]{2,1,0:T(8,128)(2,1)} fusion(bf16[16,48,4096]{2,1,0:T(8,128)(2,1)S(1)} %bitcast.174, bf16[16,48,4096]{2,1,0:T(8,128)(2,1)S(1)} %bitcast.177), kind=kLoop, calls=%fused_computation.8 | loop fusion | flops 25165824 | bytes 25165824 | tf_op jit(solution)/shard_map/concatenate | solution.py:231
  336.9 8.6 %pad_maximum_fusion.1 = bf16[16,96,4096]{2,1,0:T(8,128)(2,1)} fusion(bf16[16,48,4096]{2,1,0:T(8,128)(2,1)S(1)} %bitcast.173, bf16[16,48,4096]{2,1,0:T(8,128)(2,1)S(1)} %bitcast.175), kind=kLoop, calls=%fused_computation.7 | loop fusion | flops 25165824 | bytes 25165824 | tf_op jit(solution)/shard_map/concatenate | solution.py:230
  345.5 60.0 %reduce-scatter.4.cloned.1.call-done = bf16[1,96,4224]{2,1,0:T(8,128)(2,1)} async-done(((bf16[16,96,4224]{2,1,0:T(8,128)(2,1)}), bf16[1,96,4224]{2,1,0:T(8,128)(2,1)}) %reduce-scatter.4.cloned.1.call-update) | async-done | bytes 811024
  405.5 0.7 slice_bitcast_fusion
  406.3 1.2 slice.66
  407.5 16.7 %all-gather = bf16[16,96,48]{1,2,0:T(8,128)(2,1)S(1)} all-gather(bf16[1,96,48]{1,2,0:T(8,128)(2,1)S(1)} %copy.88), channel_id=1, replica_groups=mesh['dp'=16,'expert'=8] {'dp'}, dimensions={0}, use_global_device_ids=true | all-gather | bytes 156672 | tf_op jit(solution)/shard_map/all_gather | solution.py:228
  424.5 7.2 %fusion.1 = f32[1,16,4096]{2,1,0:T(8,128)} fusion(bf16[1536,4096]{1,0:T(8,128)(2,1)} %bitcast.169, bf16[1536,48]{0,1:T(8,128)(2,1)S(1)} %reshape.191), kind=kOutput, calls=%fused_computation.14 | convolution fusion | flops 201392128 | bytes 12894208 | tf_op jit(solution)/shard_map/dot_general | solution.py:12
  431.7 1.1 copy-done.2
  432.7 2.4 fusion.2
  435.2 1.0 copy.101
  436.2 11.4 %all-to-all-start.1 = ((bf16[96,8,512]{2,0,1:T(8,128)(2,1)}), bf16[96,8,512]{2,0,1:T(8,128)(2,1)S(1)}, u32[]{:S(2)}, u32[]{:S(2)}) async-start(bf16[96,8,512]{2,0,1:T(8,128)(2,1)} %bitcast.166), calls=%async_computation.1 | async-start | bytes 1572864 | tf_op jit(solution)/shard_map/all_to_all | solution.py:238
  447.6 7.0 %fusion = f32[1,4096,16]{1,2,0:T(8,128)} fusion(bf16[1536,4096]{1,0:T(8,128)(2,1)} %bitcast.171, bf16[1536,48]{0,1:T(8,128)(2,1)S(1)} %reshape.191), kind=kOutput, calls=%fused_computation.12 | convolution fusion | flops 201392128 | bytes 12894208 | tf_op jit(solution)/shard_map/dot_general | solution.py:12
  454.6 5.3 %all-to-all-done.1 = bf16[96,8,512]{2,0,1:T(8,128)(2,1)S(1)} async-done(((bf16[96,8,512]{2,0,1:T(8,128)(2,1)}), bf16[96,8,512]{2,0,1:T(8,128)(2,1)S(1)}, u32[]{:S(2)}, u32[]{:S(2)}) %all-to-all-start.1) | async-done | bytes 786464 | tf_op jit(solution)/shard_map/all_to_all | solution.py:238
  459.9 0.5 copy.100
  460.3 1.0 gather_fusion.3
  461.6 1.3 reduce_sum.29
  (123 shorter events, 7.5 us)
Async XLA Ops:
  7.2 141.0 %copy-start = (bf16[1,4096,16]{1,2,0:T(8,128)(2,1)S(1)}, bf16[1,4096,16]{1,2,0:T(8,128)(2,1)}, u32[]{:S(2)}) copy-start(bf16[1,4096,16]{1,2,0:T(8,128)(2,1)} %param.25) | copy-start | bytes 393220
  7.2 12.0 %copy-start.14 = (bf16[128,512]{1,0:T(8,128)(2,1)S(1)}, bf16[128,512]{1,0:T(8,128)(2,1)}, u32[]{:S(2)}) copy-start(bf16[128,512]{1,0:T(8,128)(2,1)} %param.13) | copy-start | bytes 393220
  7.2 12.0 %copy-start.15 = (bf16[128,512]{1,0:T(8,128)(2,1)S(1)}, bf16[128,512]{1,0:T(8,128)(2,1)}, u32[]{:S(2)}) copy-start(bf16[128,512]{1,0:T(8,128)(2,1)} %param.14) | copy-start | bytes 393220
  7.2 141.0 %all-gather.4.cloned.1.call-start = ((), (), s32[]{:S(2)}) async-start(), calls=%async_computation.3 | async-start | bytes 13369344 | tf_op jit(solution)/shard_map/all_gather | solution.py:209
  58.3 181.7 %all-gather.6.cloned.1.call-start = ((), (), s32[]{:S(2)}) async-start(), calls=%async_computation.4 | async-start | bytes 13369344 | tf_op jit(solution)/shard_map/all_gather | solution.py:209
  59.8 345.7 %reduce-scatter.4.cloned.1.call-start = ((), (), s32[]{:S(2)}) async-start(), calls=%async_computation.5 | async-start | bytes 13787136
  148.2 4.7 copy-start.29
  148.2 11.1 %slice-start = ((s8[12582912]{0:T(1024)(128)(4,1)}), s8[4194304]{0:T(1024)(128)(4,1)S(1)}, s32[]{:S(2)}) async-start(s8[12582912]{0:T(1024)(128)(4,1)} %bitcast.179), calls=%async_computation.6 | async-start | bytes 8388608
  152.8 6.0 %copy-start.18 = (bf16[768,16]{0,1:T(8,128)(2,1)}, bf16[768,16]{0,1:T(8,128)(2,1)S(1)}, u32[]{:S(2)}) copy-start(bf16[768,16]{0,1:T(8,128)(2,1)S(1)} %convolution_convert_fusion.11) | copy-start | bytes 73732
  152.8 6.0 %copy-start.11 = (bf16[1,16,448]{2,1,0:T(8,128)(2,1)S(1)}, bf16[1,16,448]{2,1,0:T(8,128)(2,1)}, u32[]{:S(2)}) copy-start(bf16[1,16,448]{2,1,0:T(8,128)(2,1)} %param.24) | copy-start | bytes 43012
  152.9 6.4 %slice-start.1 = ((s8[12582912]{0:T(1024)(128)(4,1)}), s8[4194304]{0:T(1024)(128)(4,1)S(1)}, s32[]{:S(2)}) async-start(s8[12582912]{0:T(1024)(128)(4,1)} %bitcast.179), calls=%async_computation.7 | async-start | bytes 8388608
  152.9 6.4 %slice-start.2 = ((s8[12582912]{0:T(1024)(128)(4,1)}), s8[4194304]{0:T(1024)(128)(4,1)S(1)}, s32[]{:S(2)}) async-start(s8[12582912]{0:T(1024)(128)(4,1)} %bitcast.179), calls=%async_computation.8 | async-start | bytes 8388608
  152.9 6.4 %copy-start.8 = (bf16[1,16,4096]{2,1,0:T(8,128)(2,1)S(1)}, bf16[1,16,4096]{2,1,0:T(8,128)(2,1)}, u32[]{:S(2)}) copy-start(bf16[1,16,4096]{2,1,0:T(8,128)(2,1)} %param.22) | copy-start | bytes 393220
  159.3 2.4 copy-start.3
  161.7 3.1 copy-start.16
  161.7 3.1 copy-start.10
  161.7 3.5 copy-start.9
  165.2 2.1 copy-start.5
  167.3 3.3 copy-start.25
  167.3 3.3 copy-start.24
  172.7 105.2 %copy-start.12 = (bf16[768,16]{0,1:T(8,128)(2,1)}, bf16[768,16]{0,1:T(8,128)(2,1)S(1)}, u32[]{:S(2)}) copy-start(bf16[768,16]{0,1:T(8,128)(2,1)S(1)} %convolution_convert_fusion.5) | copy-start | bytes 73732
  172.9 105.0 %copy-start.13 = (bf16[768,16]{0,1:T(8,128)(2,1)}, bf16[768,16]{0,1:T(8,128)(2,1)S(1)}, u32[]{:S(2)}) copy-start(bf16[768,16]{0,1:T(8,128)(2,1)S(1)} %convolution_convert_fusion.4) | copy-start | bytes 73732
  240.0 4.7 copy-start.30
  240.0 11.1 %slice-start.3 = ((s8[12582912]{0:T(1024)(128)(4,1)}), s8[4194304]{0:T(1024)(128)(4,1)S(1)}, s32[]{:S(2)}) async-start(s8[12582912]{0:T(1024)(128)(4,1)} %bitcast.181), calls=%async_computation.9 | async-start | bytes 8388608
  244.6 6.0 %copy-start.22 = (bf16[768,16]{0,1:T(8,128)(2,1)}, bf16[768,16]{0,1:T(8,128)(2,1)S(1)}, u32[]{:S(2)}) copy-start(bf16[768,16]{0,1:T(8,128)(2,1)S(1)} %convolution_convert_fusion.8) | copy-start | bytes 73732
  244.6 6.4 %slice-start.4 = ((s8[12582912]{0:T(1024)(128)(4,1)}), s8[4194304]{0:T(1024)(128)(4,1)S(1)}, s32[]{:S(2)}) async-start(s8[12582912]{0:T(1024)(128)(4,1)} %bitcast.181), calls=%async_computation.10 | async-start | bytes 8388608
  244.7 6.4 %slice-start.5 = ((s8[12582912]{0:T(1024)(128)(4,1)}), s8[4194304]{0:T(1024)(128)(4,1)S(1)}, s32[]{:S(2)}) async-start(s8[12582912]{0:T(1024)(128)(4,1)} %bitcast.181), calls=%async_computation.11 | async-start | bytes 8388608
  251.1 2.0 copy-start.4
  253.1 3.1 copy-start.20
  256.6 2.0 copy-start.6
  258.7 3.5 copy-start.27
  263.1 13.1 %copy-start.7 = (bf16[448,768]{1,0:T(8,128)(2,1)}, bf16[448,768]{1,0:T(8,128)(2,1)S(1)}, u32[]{:S(2)}) copy-start(bf16[448,768]{1,0:T(8,128)(2,1)S(1)} %get-tuple-element.15) | copy-start | bytes 2064388
  309.9 0.7 copy-start.19
  309.9 2.1 copy-start.23
  309.9 4.2 copy-start.26
  309.9 4.5 copy-start.28
  309.9 5.4 %copy-start.17 = (bf16[768,16]{0,1:T(8,128)(2,1)S(1)}, bf16[768,16]{0,1:T(8,128)(2,1)}, u32[]{:S(2)}) copy-start(bf16[768,16]{0,1:T(8,128)(2,1)} %copy-done.16) | copy-start | bytes 73732
  310.0 5.7 %copy-start.21 = (bf16[768,16]{0,1:T(8,128)(2,1)S(1)}, bf16[768,16]{0,1:T(8,128)(2,1)}, u32[]{:S(2)}) copy-start(bf16[768,16]{0,1:T(8,128)(2,1)} %copy-done.20) | copy-start | bytes 73732
  424.5 8.3 %copy-start.2 = (bf16[16,96,4096]{2,1,0:T(8,128)(2,1)S(1)}, bf16[16,96,4096]{2,1,0:T(8,128)(2,1)}, u32[]{:S(2)}) copy-start(bf16[16,96,4096]{2,1,0:T(8,128)(2,1)} %pad_maximum_fusion.1) | copy-start | bytes 37748740
  436.2 23.7 %all-to-all-start.1 = ((bf16[96,8,512]{2,0,1:T(8,128)(2,1)}), bf16[96,8,512]{2,0,1:T(8,128)(2,1)S(1)}, u32[]{:S(2)}, u32[]{:S(2)}) async-start(bf16[96,8,512]{2,0,1:T(8,128)(2,1)} %bitcast.166), calls=%async_computation.1 | async-start | bytes 1572864 | tf_op jit(solution)/shard_map/all_to_all | solution.py:238
  459.9 3.1 copy-start.1
Sparse Core Ops, SparseCore 0:
  58.4 89.7 all-gather.3
  150.3 89.5 all-gather.5
  310.1 95.3 reduce-scatter.3

commit v3 on v2

--- a/solution.py
+++ b/solution.py
@@ -1,7 +1,13 @@
+import functools
+
 import jax
 import jax.numpy as jnp
 from jax import lax
+from jax.experimental import pallas as pl
+from jax.experimental.pallas import tpu as pltpu
 from jax.sharding import PartitionSpec as P
+
+MESH = pl.DeviceIdType.MESH
 
 ADAPTER_SCALE = 2.0
 NUM_CHUNKS = 2
@@ -141,6 +147,43 @@
         ADAPTER_SCALE * contract_pair(down_projected_lower, hidden_units, 1, 1),
     )
     return (gradient_rows_out, parts, owned_slice)
+
+
+def gather_dp_kernel(n, src_ref, out_ref, send_sem, recv_sem):
+    me = lax.axis_index("dp")
+    ex = lax.axis_index("expert")
+    barrier = pltpu.get_barrier_semaphore()
+    for k in range(1, n):
+        peer = lax.rem(me + k, n)
+        pl.semaphore_signal(barrier, inc=1, device_id=(peer, ex), device_id_type=MESH)
+    pl.semaphore_wait(barrier, n - 1)
+    copies = []
+    for k in range(1, n):
+        peer = lax.rem(me + k, n)
+        cp = pltpu.make_async_remote_copy(
+            src_ref,
+            out_ref.at[me],
+            send_sem.at[k],
+            recv_sem.at[k],
+            device_id=(peer, ex),
+            device_id_type=MESH,
+        )
+        cp.start()
+        copies.append(cp)
+    out_ref[me] = src_ref[...]
+    for cp in copies:
+        cp.wait()
+
+
+def gather_dp(block, n):
+    return pl.pallas_call(
+        functools.partial(gather_dp_kernel, n),
+        out_shape=jax.ShapeDtypeStruct((n,) + block.shape, block.dtype),
+        in_specs=[pl.BlockSpec(memory_space=pltpu.VMEM)],
+        out_specs=pl.BlockSpec(memory_space=pltpu.VMEM),
+        scratch_shapes=[pltpu.SemaphoreType.DMA((n,)), pltpu.SemaphoreType.DMA((n,))],
+        compiler_params=pltpu.CompilerParams(collective_id=0, has_side_effects=True),
+    )(block)
 
 
 def local(
@@ -196,8 +239,8 @@
     )
     send_both = jnp.concatenate([send_x, send_dy], axis=2)
     recv_both = lax.all_to_all(send_both, "expert", split_axis=0, concat_axis=2, tiled=True)[0]
-    recv_both = recv_both.reshape(capacity, experts, 2, feat_local).transpose(0, 2, 1, 3)
-    recv_both = recv_both.reshape(capacity, 2 * complete_width)
+    recv_both = recv_both.reshape(capacity, experts, 2, feat_local).transpose(2, 0, 1, 3)
+    recv_both = recv_both.reshape(2, capacity, complete_width)
 
     rows_chunks = []
     part_chunks = []
@@ -205,10 +248,10 @@
     dy_chunks = []
     owned_total = None
     for c in range(chunks):
-        part = recv_both[c * piece:(c + 1) * piece]
-        gathered = lax.all_gather(part, "dp", axis=0, tiled=True)
-        x_rows = gathered[:, :complete_width]
-        dy_rows = gathered[:, complete_width:]
+        part = recv_both[:, c * piece:(c + 1) * piece]
+        gathered = lax.all_gather(part, "dp", axis=1, tiled=True)
+        x_rows = gathered[0]
+        dy_rows = gathered[1]
         rows_out, parts, owned_slice = rows_backward_parts(x_rows, dy_rows, params)
         if c == 0:
             owned_total = owned_slice
@@ -216,25 +259,31 @@
             owned_total = jax.tree.map(jnp.add, owned_total, owned_slice)
         rows_chunks.append(rows_out.astype(jnp.bfloat16).reshape(shards, piece, complete_width))
         part_chunks.append(parts.reshape(shards, piece, 3 * adapter_rank))
-        x_chunks.append(x_rows.reshape(shards, piece, complete_width))
-        dy_chunks.append(dy_rows.reshape(shards, piece, complete_width))
+        x_chunks.append(x_rows)
+        dy_chunks.append(dy_rows)
     rows_all = jnp.concatenate(rows_chunks, 1)
     parts_all = jnp.concatenate(part_chunks, 1)
     parts_all = jnp.pad(parts_all, ((0, 0), (0, 0), (0, PART_COLS - 3 * adapter_rank)))
     packed = jnp.concatenate([rows_all, parts_all], 2)
     summed_packed = lax.psum_scatter(packed, "dp", scatter_dimension=0, tiled=True)[0]
     summed = summed_packed[:, :complete_width]
-    parts_mine = summed_packed[:, complete_width:complete_width + 3 * adapter_rank]
-    parts_sum = lax.all_gather(parts_mine, "dp", axis=0, tiled=True)
-    parts_sum = parts_sum.reshape(shards, capacity, 3 * adapter_rank)
-    x_all = jnp.concatenate(x_chunks, 1).reshape(shards * capacity, complete_width)
-    dy_all = jnp.concatenate(dy_chunks, 1).reshape(shards * capacity, complete_width)
-    parts_sum = parts_sum.reshape(shards * capacity, 3 * adapter_rank)
-    grad_a_gate = ADAPTER_SCALE * contract_pair(parts_sum[:, :adapter_rank], x_all, 0, 0)
-    grad_a_up = ADAPTER_SCALE * contract_pair(
-        parts_sum[:, adapter_rank:2 * adapter_rank], x_all, 0, 0
-    )
-    grad_b_down = ADAPTER_SCALE * contract_pair(dy_all, parts_sum[:, 2 * adapter_rank:], 0, 0)
+    parts_mine = summed_packed[:, complete_width:]
+    parts_sum = gather_dp(parts_mine, shards).reshape(shards, chunks, piece, PART_COLS)
+    grad_a_gate = None
+    for c in range(chunks):
+        parts_c = parts_sum[:, c].reshape(shards * piece, PART_COLS)
+        a_gate_c = contract_pair(parts_c[:, :adapter_rank], x_chunks[c], 0, 0)
+        a_up_c = contract_pair(parts_c[:, adapter_rank:2 * adapter_rank], x_chunks[c], 0, 0)
+        b_down_c = contract_pair(dy_chunks[c], parts_c[:, 2 * adapter_rank:3 * adapter_rank], 0, 0)
+        if grad_a_gate is None:
+            grad_a_gate, grad_a_up, grad_b_down = a_gate_c, a_up_c, b_down_c
+        else:
+            grad_a_gate = grad_a_gate + a_gate_c
+            grad_a_up = grad_a_up + a_up_c
+            grad_b_down = grad_b_down + b_down_c
+    grad_a_gate = ADAPTER_SCALE * grad_a_gate
+    grad_a_up = ADAPTER_SCALE * grad_a_up
+    grad_b_down = ADAPTER_SCALE * grad_b_down
     returned_rows = lax.all_to_all(
         summed.reshape(capacity, experts, feat_local),
         "expert",

time: 477 us -> 461 us (0.966)
  waiting for transfers between devices: 207 us -> 233 us
  other arithmetic: 32 us -> 14.7 us
  blocking collectives: 44.1 us -> 27.4 us
  local copies, waits for them, and re-layouts: 42.5 us -> 31 us
  Pallas kernels: 0 us -> 10.8 us
  starting transfers between devices: 12 us -> 6.3 us
    unnamed x4, waiting for transfers between devices: 60 us -> 89.6 us
    concatenate x2 -> x0, other arithmetic: 17.3 us -> none  [the longest x1 8.69 us: local(): jnp.concatenate(dy_chunks, 1).reshape(shards * capacity, complete_width)]
    all_gather x1 -> x0, blocking collectives: 16.7 us -> none  [local(): parts_sum = lax.all_gather(parts_mine, 'dp', axis=0, tiled=True)]
    pallas_call x0 -> x1, Pallas kernels: none -> 10.8 us  [gather_dp(): pl.pallas_call(functools.partial(gather_dp_kernel, n), out_shape=jax.Shap...]
    slice x5 -> x3, local copies, waits for them, and re-layouts: 13.1 us -> 3.66 us  [the longest x1 1.35 us: local(): parts_mine = summed_packed[:, complete_width:]]
    all_to_all x1, starting transfers between devices: 11.4 us -> 5.66 us  [local(): lax.all_to_all(summed.reshape(capacity, experts, feat_local), 'expert', s...]
    all_to_all x1, waiting for transfers between devices: 5.27 us -> 0.01 us  [local(): lax.all_to_all(summed.reshape(capacity, experts, feat_local), 'expert', s...]
    unnamed x80 -> x79, local copies, waits for them, and re-layouts: 7.78 us -> 3 us
  transfers between devices with their start and end apart: 4 -> 4, of which waited for: 4 -> 3; matrix products, arithmetic and copies ran while one was open for 17% -> 13% of each run, Pallas kernels for 0% -> 2%
where the time goes in v3:
time: 461 us; the launch traced here: 455 us
  waiting for transfers between devices  233 us (51%)
  matrix products  117 us (25%)
  local copies, waits for them, and re-layouts  31 us (7%)
  blocking collectives  27.4 us (6%)
  between operations  14.9 us (3%)
  other arithmetic  14.7 us (3%)
  Pallas kernels  10.8 us (2%)
  starting transfers between devices  6.3 us (1%)
    all_gather x2, waiting for transfers between devices, local(): gathered = lax.all_gather(part, 'dp', axis=1, tiled=True)  143 us
    dot_general x42, matrix products, contract_pair(): lax.dot_general(left, right, (((left_axis,), (right_axis,)), ((), ())), p...  117 us
    unnamed x4, waiting for transfers between devices  89.6 us
    all_to_all x1, blocking collectives, local(): lax.all_to_all(send_both, 'expert', split_axis=0, concat_axis=2, tiled=True)  27.4 us
    pallas_call x1, Pallas kernels, gather_dp(): pl.pallas_call(functools.partial(gather_dp_kernel, n), out_shape=jax.Shap...  10.8 us
    concatenate x1, other arithmetic, local(): packed = jnp.concatenate([rows_all, parts_all], 2)  10.4 us
  transfers between devices with their start and end apart: 4, of which 3 were waited for; matrix products, arithmetic and copies ran while one was open for 13% of the time, Pallas kernels for 2%

profile of v3, /device:TPU:1, one launch (start us, length us, event | category | flops | bytes accessed | tf_op | source)
XLA Modules:
  0.0 454.5 jit_solution(13208695054183338585)
XLA Ops:
  7.2 0.8 convert_reduce_fusion
  8.4 0.7 select_reduce_fusion
  9.1 0.7 compare_select_fusion.3
  10.0 0.8 copy.62
  11.3 1.4 scatter_custom_fusion.1
  12.7 1.4 scatter_custom_fusion
  14.1 5.0 %gather_fusion.1 = f32[768]{0:T(1024)S(1)} fusion(f32[256]{0:T(256)S(1)} %reshape.105, s32[1024]{0:T(1024)S(1)} %get-tuple-element.21), kind=kCustom, calls=%fused_computation.1 | custom fusion | bytes 9216 | tf_op jit(solution)/shard_map/gather | solution.py:229
  19.2 2.7 gather_fusion.2
  21.9 2.7 gather_fusion
  25.1 27.4 %all_to_all.20 = bf16[8,96,1024]{2,1,0:T(8,128)(2,1)S(1)} all-to-all(bf16[8,96,1024]{2,1,0:T(8,128)(2,1)S(1)} %pad_maximum_fusion.1), channel_id=1, replica_groups=mesh['dp'=16,'expert'=8] {'expert'}, dimensions={0} | all-to-all | bytes 3145728 | tf_op jit(solution)/shard_map/all_to_all | solution.py:241
  52.5 1.2 reshape.171
  53.6 2.0 copy.64
  55.7 2.6 reshape.106
  58.3 1.3 fusion.103
  59.6 0.7 all-gather.5.cloned.1.call-update
  60.3 0.6 reduce-scatter.4.cloned.1.call-start
  60.9 88.6 %all-gather.3.cloned.1.call-done = bf16[2,768,4096]{2,1,0:T(8,128)(2,1)} async-done(((bf16[2,48,4096]{2,1,0:T(8,128)(2,1)}), bf16[2,768,4096]{2,1,0:T(8,128)(2,1)}) %all-gather.3.cloned.1.call-update) | async-done | bytes 12582928 | tf_op jit(solution)/shard_map/all_gather | solution.py:252
  149.5 4.7 %fusion.54 = bf16[768,16]{0,1:T(8,128)(2,1)S(1)} fusion(bf16[2,768,4096]{2,1,0:T(8,128)(2,1)} %all-gather.3.cloned.1.call-done, bf16[1,16,4096]{2,1,0:T(8,128)(2,1)S(1)} %copy-done.7), kind=kOutput, calls=%fused_computation.86 | convolution fusion | flops 100675584 | bytes 6447104 | tf_op jit(solution)/shard_map/dot_general | solution.py:18
  154.2 6.0 %fusion.27 = f32[768,448]{0,1:T(8,128)S(1)} fusion(bf16[1,448,4096]{2,1,0:T(8,128)(2,1)S(1)} %copy-done.2, bf16[2,768,4096]{2,1,0:T(8,128)(2,1)} %all-gather.3.cloned.1.call-done), kind=kOutput, calls=%fused_computation.42 | convolution fusion | flops 2818572288 | bytes 11337728 | tf_op jit(solution)/shard_map/dot_general | solution.py:18
  160.7 1.7 fusion.57
  162.4 0.7 copy-done.28
  163.1 3.1 fusion.2
  166.1 0.4 fusion.49
  166.6 1.7 fusion.55
  168.6 3.2 fusion.19
  171.9 1.9 multiply_convert_fusion.5
  174.2 6.4 %fusion.25 = f32[768,4096]{1,0:T(8,128)} fusion(bf16[448,768]{1,0:T(8,128)(2,1)S(1)} %get-tuple-element.9, bf16[1,448,4096]{2,1,0:T(8,128)(2,1)S(1)} %copy-done.2), kind=kOutput, calls=%fused_computation.40 | convolution fusion | flops 2818572288 | bytes 16941056 | tf_op jit(solution)/shard_map/dot_general | solution.py:18
  180.6 6.3 %fusion.17 = f32[768,4096]{1,0:T(8,128)} fusion(bf16[448,768]{1,0:T(8,128)(2,1)S(1)} %get-tuple-element.7, bf16[1,448,4096]{2,1,0:T(8,128)(2,1)S(1)} %copy-done.4), kind=kOutput, calls=%fused_computation.32 | convolution fusion | flops 2818572288 | bytes 16941056 | tf_op jit(solution)/shard_map/dot_general | solution.py:18
  186.8 54.4 %all-gather.5.cloned.1.call-done = bf16[2,768,4096]{2,1,0:T(8,128)(2,1)} async-done(((bf16[2,48,4096]{2,1,0:T(8,128)(2,1)}), bf16[2,768,4096]{2,1,0:T(8,128)(2,1)}) %all-gather.5.cloned.1.call-update) | async-done | bytes 12582928 | tf_op jit(solution)/shard_map/all_gather | solution.py:252
  241.3 4.7 %fusion.52 = bf16[768,16]{0,1:T(8,128)(2,1)S(1)} fusion(bf16[2,768,4096]{2,1,0:T(8,128)(2,1)} %all-gather.5.cloned.1.call-done, bf16[1,16,4096]{2,1,0:T(8,128)(2,1)S(1)} %copy-done.7), kind=kOutput, calls=%fused_computation.84 | convolution fusion | flops 100675584 | bytes 6447104 | tf_op jit(solution)/shard_map/dot_general | solution.py:18
  245.9 6.0 %fusion.23 = f32[768,448]{0,1:T(8,128)S(1)} fusion(bf16[1,448,4096]{2,1,0:T(8,128)(2,1)S(1)} %copy-done.3, bf16[2,768,4096]{2,1,0:T(8,128)(2,1)} %all-gather.5.cloned.1.call-done), kind=kOutput, calls=%fused_computation.38 | convolution fusion | flops 2818572288 | bytes 11337728 | tf_op jit(solution)/shard_map/dot_general | solution.py:18
  252.4 1.7 fusion.56
  254.4 3.1 fusion.5
  257.5 0.4 fusion.43
  257.9 1.7 fusion.53
  259.9 3.3 fusion.15
  263.2 1.0 multiply_convert_fusion.3
  264.4 6.3 %fusion.21 = f32[768,4096]{1,0:T(8,128)} fusion(bf16[448,768]{1,0:T(8,128)(2,1)S(1)} %get-tuple-element.12, bf16[1,448,4096]{2,1,0:T(8,128)(2,1)S(1)} %copy-done.3), kind=kOutput, calls=%fused_computation.36 | convolution fusion | flops 2818572288 | bytes 16941056 | tf_op jit(solution)/shard_map/dot_general | solution.py:18
  270.9 6.3 %fusion.13 = f32[768,4096]{1,0:T(8,128)} fusion(bf16[448,768]{1,0:T(8,128)(2,1)S(1)} %get-tuple-element.10, bf16[1,448,4096]{2,1,0:T(8,128)(2,1)S(1)} %copy-done.5), kind=kOutput, calls=%fused_computation.28 | convolution fusion | flops 2818572288 | bytes 16941056 | tf_op jit(solution)/shard_map/dot_general | solution.py:18
  277.6 1.3 convolution_convert_fusion.1
  279.3 9.3 %add_convert_fusion.1 = bf16[768,4096]{1,0:T(8,128)(2,1)S(1)} fusion(f32[768,4096]{1,0:T(8,128)} %fusion.17, f32[768,4096]{1,0:T(8,128)} %fusion.25, bf16[16,4096]{1,0:T(8,128)(2,1)S(1)} %bitcast.223, bf16[16,4096]{1,0:T(8,128)(2,1)S(1)} %bitcast.225, bf16[768,16]{0,1:T(8,128)(2,1)} %copy-done.12, bf16[768,16]{0,1:T(8,128)(2,1)} %copy-done.11), kind=kOutput, calls=%fused_computation.8 | convolution fusion | flops 214532096 | bytes 31768576 | tf_op jit(solution)/shard_map/dot_general | solution.py:18
  288.5 12.0 %add_convert_fusion = bf16[768,4096]{1,0:T(8,128)(2,1)} fusion(f32[768,4096]{1,0:T(8,128)} %fusion.13, f32[768,4096]{1,0:T(8,128)} %fusion.21, bf16[16,4096]{1,0:T(8,128)(2,1)S(1)} %bitcast.224, bf16[16,4096]{1,0:T(8,128)(2,1)S(1)} %bitcast.226, bf16[768,16]{0,1:T(8,128)(2,1)S(1)} %convolution_convert_fusion.2, bf16[768,16]{0,1:T(8,128)(2,1)S(1)} %convolution_convert_fusion.3), kind=kOutput, calls=%fused_computation.7 | convolution fusion | flops 214532096 | bytes 31768576 | tf_op jit(solution)/shard_map/dot_general | solution.py:18
  300.5 10.4 %pad_maximum_fusion = bf16[16,96,4224]{2,1,0:T(8,128)(2,1)} fusion(bf16[16,96,128]{2,1,0:T(8,128)(2,1)S(1)} %fusion.66, bf16[16,48,4096]{2,1,0:T(8,128)(2,1)} %bitcast.199, bf16[16,48,4096]{2,1,0:T(8,128)(2,1)S(1)} %bitcast.198), kind=kLoop, calls=%fused_computation.6 | loop fusion | flops 38928384 | bytes 25952256 | tf_op jit(solution)/shard_map/concatenate | solution.py:267
  311.3 0.4 copy-done.18
  311.7 1.4 fusion.107
  313.1 2.1 fusion.59
  315.4 1.0 fusion.63
  316.7 1.0 fusion.61
  317.7 88.8 %reduce-scatter.4.cloned.1.call-done = bf16[1,96,4224]{2,1,0:T(8,128)(2,1)} async-done(((bf16[16,96,4224]{2,1,0:T(8,128)(2,1)}), bf16[1,96,4224]{2,1,0:T(8,128)(2,1)}) %reduce-scatter.4.cloned.1.call-update) | async-done | bytes 811024
  406.5 1.3 slice.79.src_ref
  407.8 1.2 slice.78
  409.0 1.0 copy.78
  410.0 5.7 %all-to-all-start.1 = ((bf16[96,8,512]{2,0,1:T(8,128)(2,1)}), bf16[96,8,512]{2,0,1:T(8,128)(2,1)S(1)}, u32[]{:S(2)}, u32[]{:S(2)}) async-start(bf16[96,8,512]{2,0,1:T(8,128)(2,1)} %bitcast.195), calls=%async_computation.1 | async-start | bytes 1572864 | tf_op jit(solution)/shard_map/all_to_all | solution.py:287
  415.7 10.8 %shard_map.180 = bf16[16,96,128]{2,1,0:T(8,128)(2,1)} custom-call(bf16[96,128]{1,0:T(8,128)(2,1)} %slice.79.src_ref), custom_call_target="tpu_custom_call" | custom-call | tf_op jit(solution)/shard_map/pallas_call | solution.py:179
  426.5 1.1 fusion.104
  427.6 4.0 fusion
  431.5 4.1 fusion.31
  435.6 3.7 fusion.32
  439.4 1.7 fusion.9
  441.0 1.7 fusion.7
  442.8 1.7 fusion.12
  444.5 0.5 copy.77
  445.0 1.0 gather_fusion.3
  446.3 1.3 reduce_sum.29
  (122 shorter events, 6.2 us)
Async XLA Ops:
  7.2 153.4 %copy-start = (bf16[1,4096,16]{1,2,0:T(8,128)(2,1)S(1)}, bf16[1,4096,16]{1,2,0:T(8,128)(2,1)}, u32[]{:S(2)}) copy-start(bf16[1,4096,16]{1,2,0:T(8,128)(2,1)} %param.25) | copy-start | bytes 393220
  7.2 12.0 %copy-start.13 = (bf16[128,512]{1,0:T(8,128)(2,1)S(1)}, bf16[128,512]{1,0:T(8,128)(2,1)}, u32[]{:S(2)}) copy-start(bf16[128,512]{1,0:T(8,128)(2,1)} %param.13) | copy-start | bytes 393220
  7.2 12.0 %copy-start.14 = (bf16[128,512]{1,0:T(8,128)(2,1)S(1)}, bf16[128,512]{1,0:T(8,128)(2,1)}, u32[]{:S(2)}) copy-start(bf16[128,512]{1,0:T(8,128)(2,1)} %param.14) | copy-start | bytes 393220
  7.2 142.3 %all-gather.3.cloned.1.call-start = ((), (), s32[]{:S(2)}) async-start(), calls=%async_computation.3 | async-start | bytes 13369344 | tf_op jit(solution)/shard_map/all_gather | solution.py:252
  55.7 93.8 %copy-start.7 = (bf16[1,16,4096]{2,1,0:T(8,128)(2,1)S(1)}, bf16[1,16,4096]{2,1,0:T(8,128)(2,1)}, u32[]{:S(2)}) copy-start(bf16[1,16,4096]{2,1,0:T(8,128)(2,1)} %param.22) | copy-start | bytes 393220
  59.6 181.7 %all-gather.5.cloned.1.call-start = ((), (), s32[]{:S(2)}) async-start(), calls=%async_computation.4 | async-start | bytes 13369344 | tf_op jit(solution)/shard_map/all_gather | solution.py:252
  60.3 346.2 %reduce-scatter.4.cloned.1.call-start = ((), (), s32[]{:S(2)}) async-start(), calls=%async_computation.5 | async-start | bytes 13787136
  149.5 4.7 %copy-start.2 = (bf16[1,448,4096]{2,1,0:T(8,128)(2,1)S(1)}, bf16[1,448,4096]{2,1,0:T(8,128)(2,1)}, u32[]{:S(2)}) copy-start(bf16[1,448,4096]{2,1,0:T(8,128)(2,1)} %param.18) | copy-start | bytes 11010052
  149.5 11.1 %slice-start = ((s8[12582912]{0:T(1024)(128)(4,1)}), s8[4194304]{0:T(1024)(128)(4,1)S(1)}, s32[]{:S(2)}) async-start(s8[12582912]{0:T(1024)(128)(4,1)} %bitcast.201), calls=%async_computation.6 | async-start | bytes 8388608
  154.2 6.0 %copy-start.15 = (bf16[768,16]{0,1:T(8,128)(2,1)}, bf16[768,16]{0,1:T(8,128)(2,1)S(1)}, u32[]{:S(2)}) copy-start(bf16[768,16]{0,1:T(8,128)(2,1)S(1)} %fusion.54) | copy-start | bytes 73732
  154.2 6.0 %copy-start.9 = (bf16[1,448,16]{1,2,0:T(8,128)(2,1)S(1)}, bf16[1,448,16]{1,2,0:T(8,128)(2,1)}, u32[]{:S(2)}) copy-start(bf16[1,448,16]{1,2,0:T(8,128)(2,1)} %param.23) | copy-start | bytes 43012
  154.2 6.4 %slice-start.1 = ((s8[12582912]{0:T(1024)(128)(4,1)}), s8[4194304]{0:T(1024)(128)(4,1)S(1)}, s32[]{:S(2)}) async-start(s8[12582912]{0:T(1024)(128)(4,1)} %bitcast.201), calls=%async_computation.7 | async-start | bytes 8388608
  154.2 6.4 %slice-start.2 = ((s8[12582912]{0:T(1024)(128)(4,1)}), s8[4194304]{0:T(1024)(128)(4,1)S(1)}, s32[]{:S(2)}) async-start(s8[12582912]{0:T(1024)(128)(4,1)} %bitcast.201), calls=%async_computation.8 | async-start | bytes 8388608
  160.6 2.4 copy-start.28
  163.0 3.1 copy-start.17
  163.0 3.1 copy-start.10
  163.1 3.5 copy-start.8
  166.5 2.1 copy-start.4
  168.6 3.3 copy-start.24
  168.6 3.3 copy-start.23
  174.0 105.0 %copy-start.11 = (bf16[768,16]{0,1:T(8,128)(2,1)}, bf16[768,16]{0,1:T(8,128)(2,1)S(1)}, u32[]{:S(2)}) copy-start(bf16[768,16]{0,1:T(8,128)(2,1)S(1)} %convolution_convert_fusion.5) | copy-start | bytes 73732
  174.2 104.8 %copy-start.12 = (bf16[768,16]{0,1:T(8,128)(2,1)}, bf16[768,16]{0,1:T(8,128)(2,1)S(1)}, u32[]{:S(2)}) copy-start(bf16[768,16]{0,1:T(8,128)(2,1)S(1)} %convolution_convert_fusion.4) | copy-start | bytes 73732
  241.2 4.7 %copy-start.3 = (bf16[1,448,4096]{2,1,0:T(8,128)(2,1)S(1)}, bf16[1,448,4096]{2,1,0:T(8,128)(2,1)}, u32[]{:S(2)}) copy-start(bf16[1,448,4096]{2,1,0:T(8,128)(2,1)} %param.18) | copy-start | bytes 11010052
  241.2 11.1 %slice-start.3 = ((s8[12582912]{0:T(1024)(128)(4,1)}), s8[4194304]{0:T(1024)(128)(4,1)S(1)}, s32[]{:S(2)}) async-start(s8[12582912]{0:T(1024)(128)(4,1)} %bitcast.203), calls=%async_computation.9 | async-start | bytes 8388608
  245.9 6.0 %copy-start.19 = (bf16[768,16]{0,1:T(8,128)(2,1)}, bf16[768,16]{0,1:T(8,128)(2,1)S(1)}, u32[]{:S(2)}) copy-start(bf16[768,16]{0,1:T(8,128)(2,1)S(1)} %fusion.52) | copy-start | bytes 73732
  245.9 6.4 %slice-start.4 = ((s8[12582912]{0:T(1024)(128)(4,1)}), s8[4194304]{0:T(1024)(128)(4,1)S(1)}, s32[]{:S(2)}) async-start(s8[12582912]{0:T(1024)(128)(4,1)} %bitcast.203), calls=%async_computation.10 | async-start | bytes 8388608
  245.9 6.4 %slice-start.5 = ((s8[12582912]{0:T(1024)(128)(4,1)}), s8[4194304]{0:T(1024)(128)(4,1)S(1)}, s32[]{:S(2)}) async-start(s8[12582912]{0:T(1024)(128)(4,1)} %bitcast.203), calls=%async_computation.11 | async-start | bytes 8388608
  252.4 2.0 copy-start.29
  254.4 3.1 copy-start.21
  257.9 2.0 copy-start.5
  259.9 3.3 copy-start.26
  264.2 13.0 %copy-start.6 = (bf16[448,768]{1,0:T(8,128)(2,1)}, bf16[448,768]{1,0:T(8,128)(2,1)S(1)}, u32[]{:S(2)}) copy-start(bf16[448,768]{1,0:T(8,128)(2,1)S(1)} %get-tuple-element.11) | copy-start | bytes 2064388
  311.0 0.7 copy-start.18
  311.0 2.1 copy-start.22
  311.0 4.2 copy-start.25
  311.0 4.5 copy-start.27
  311.0 5.4 %copy-start.16 = (bf16[768,16]{0,1:T(8,128)(2,1)S(1)}, bf16[768,16]{0,1:T(8,128)(2,1)}, u32[]{:S(2)}) copy-start(bf16[768,16]{0,1:T(8,128)(2,1)} %copy-done.15) | copy-start | bytes 73732
  311.0 5.7 %copy-start.20 = (bf16[768,16]{0,1:T(8,128)(2,1)S(1)}, bf16[768,16]{0,1:T(8,128)(2,1)}, u32[]{:S(2)}) copy-start(bf16[768,16]{0,1:T(8,128)(2,1)} %copy-done.19) | copy-start | bytes 73732
  410.0 34.5 %all-to-all-start.1 = ((bf16[96,8,512]{2,0,1:T(8,128)(2,1)}), bf16[96,8,512]{2,0,1:T(8,128)(2,1)S(1)}, u32[]{:S(2)}, u32[]{:S(2)}) async-start(bf16[96,8,512]{2,0,1:T(8,128)(2,1)} %bitcast.195), calls=%async_computation.1 | async-start | bytes 1572864 | tf_op jit(solution)/shard_map/all_to_all | solution.py:287
  427.5 11.8 %slice-start.6 = ((s8[12582912]{0:T(1024)(128)(4,1)}), s8[4194304]{0:T(1024)(128)(4,1)S(1)}, s32[]{:S(2)}) async-start(s8[12582912]{0:T(1024)(128)(4,1)} %bitcast.205), calls=%async_computation.12 | async-start | bytes 8388608
  427.5 11.8 %slice-start.7 = ((s8[12582912]{0:T(1024)(128)(4,1)}), s8[4194304]{0:T(1024)(128)(4,1)S(1)}, s32[]{:S(2)}) async-start(s8[12582912]{0:T(1024)(128)(4,1)} %bitcast.205), calls=%async_computation.13 | async-start | bytes 8388608
  431.5 7.8 %slice-start.8 = ((s8[12582912]{0:T(1024)(128)(4,1)}), s8[4194304]{0:T(1024)(128)(4,1)S(1)}, s32[]{:S(2)}) async-start(s8[12582912]{0:T(1024)(128)(4,1)} %bitcast.205), calls=%async_computation.14 | async-start | bytes 8388608
  444.5 3.1 copy-start.1
Sparse Core Ops, SparseCore 0:
  59.7 89.7 all-gather.2
  151.6 89.5 all-gather.4
  311.1 95.3 reduce-scatter.3

commit v4 on v3

--- a/solution.py
+++ b/solution.py
@@ -10,7 +10,7 @@
 MESH = pl.DeviceIdType.MESH
 
 ADAPTER_SCALE = 2.0
-NUM_CHUNKS = 2
+NUM_CHUNKS = 3
 PART_COLS = 128
 
 

time: 461 us -> 490 us (1.063)
  matrix products: 117 us -> 127 us
  waiting for transfers between devices: 233 us -> 243 us
  local copies, waits for them, and re-layouts: 31 us -> 38.5 us
    all_gather x2 -> x3, waiting for transfers between devices: 143 us -> 154 us  [local(): gathered = lax.all_gather(part, 'dp', axis=1, tiled=True)]
    dot_general x42 -> x63, matrix products: 117 us -> 127 us  [contract_pair(): lax.dot_general(left, right, (((left_axis,), (right_axis,)), ((), ())), p...]
    unnamed x79 -> x114, local copies, waits for them, and re-layouts: 3 us -> 10.3 us
    unnamed x4 -> x5, waiting for transfers between devices: 89.6 us -> 88.8 us
  transfers between devices with their start and end apart: 4 -> 5, of which waited for: 3 -> 4; matrix products, arithmetic and copies ran while one was open for 13% -> 16% of each run, Pallas kernels for 2% -> 0%
where the time goes in v4:
time: 490 us; the launch traced here: 484 us
  waiting for transfers between devices  243 us (50%)
  matrix products  127 us (26%)
  local copies, waits for them, and re-layouts  38.5 us (8%)
  blocking collectives  27.4 us (6%)
  other arithmetic  16 us (3%)
  between operations  15.1 us (3%)
  Pallas kernels  9.56 us (2%)
  starting transfers between devices  7.61 us (2%)
    all_gather x3, waiting for transfers between devices, local(): gathered = lax.all_gather(part, 'dp', axis=1, tiled=True)  154 us
    dot_general x63, matrix products, contract_pair(): lax.dot_general(left, right, (((left_axis,), (right_axis,)), ((), ())), p...  127 us
    unnamed x5, waiting for transfers between devices  88.8 us
    all_to_all x1, blocking collectives, local(): lax.all_to_all(send_both, 'expert', split_axis=0, concat_axis=2, tiled=True)  27.4 us
    concatenate x1, other arithmetic, local(): packed = jnp.concatenate([rows_all, parts_all], 2)  11.1 us
    unnamed x114, local copies, waits for them, and re-layouts  10.3 us
  transfers between devices with their start and end apart: 5, of which 4 were waited for; matrix products, arithmetic and copies ran while one was open for 16% of the time, Pallas kernels for 0%

profile of v4, /device:TPU:1, one launch (start us, length us, event | category | flops | bytes accessed | tf_op | source)
XLA Modules:
  0.0 484.0 jit_solution(17627465251809866646)
XLA Ops:
  9.1 1.2 compare_select_fusion.3
  11.8 1.4 scatter_custom_fusion.1
  13.2 1.4 scatter_custom_fusion
  14.7 5.0 %gather_fusion.1 = f32[768]{0:T(1024)S(1)} fusion(f32[256]{0:T(256)S(1)} %reshape.111, s32[1024]{0:T(1024)S(1)} %get-tuple-element.26), kind=kCustom, calls=%fused_computation.1 | custom fusion | bytes 9216 | tf_op jit(solution)/shard_map/gather | solution.py:229
  19.8 2.7 gather_fusion.2
  22.5 2.7 gather_fusion
  25.6 27.4 %all_to_all.20 = bf16[8,96,1024]{2,1,0:T(8,128)(2,1)S(1)} all-to-all(bf16[8,96,1024]{2,1,0:T(8,128)(2,1)S(1)} %pad_maximum_fusion), channel_id=1, replica_groups=mesh['dp'=16,'expert'=8] {'expert'}, dimensions={0} | all-to-all | bytes 3145728 | tf_op jit(solution)/shard_map/all_to_all | solution.py:241
  53.0 1.2 reshape.179
  54.2 2.0 copy.78
  56.2 2.6 reshape.112
  58.8 1.2 fusion.139
  61.8 68.9 %all-gather.4.cloned.1.call-done = bf16[2,512,4096]{2,1,0:T(8,128)(2,1)} async-done(((bf16[2,32,4096]{2,1,0:T(8,128)(2,1)}), bf16[2,512,4096]{2,1,0:T(8,128)(2,1)}) %all-gather.4.cloned.1.call-update) | async-done | bytes 8388624 | tf_op jit(solution)/shard_map/all_gather | solution.py:252
  130.7 3.5 fusion.79
  134.2 4.6 fusion.30
  139.2 1.2 fusion.83
  141.3 2.1 fusion.36
  143.7 1.2 fusion.80
  145.8 2.1 fusion.18
  149.1 54.2 %all-gather.6.cloned.1.call-done = bf16[2,512,4096]{2,1,0:T(8,128)(2,1)} async-done(((bf16[2,32,4096]{2,1,0:T(8,128)(2,1)}), bf16[2,512,4096]{2,1,0:T(8,128)(2,1)}) %all-gather.6.cloned.1.call-update) | async-done | bytes 8388624 | tf_op jit(solution)/shard_map/all_gather | solution.py:252
  203.3 3.5 fusion.77
  206.8 5.0 %fusion.26 = f32[512,448]{0,1:T(8,128)S(1)} fusion(bf16[1,448,4096]{2,1,0:T(8,128)(2,1)S(1)} %copy-done.3, bf16[2,512,4096]{2,1,0:T(8,128)(2,1)} %all-gather.6.cloned.1.call-done), kind=kOutput, calls=%fused_computation.48 | convolution fusion | flops 1879048192 | bytes 8781824 | tf_op jit(solution)/shard_map/dot_general | solution.py:18
  212.2 1.2 fusion.82
  214.3 2.1 fusion.34
  216.7 1.2 fusion.78
  218.8 2.1 fusion.14
  222.0 5.7 %fusion.16 = f32[512,4096]{1,0:T(8,128)} fusion(bf16[448,512]{1,0:T(8,128)(2,1)S(1)} %get-tuple-element.7, bf16[1,448,4096]{2,1,0:T(8,128)(2,1)S(1)} %copy-done.6), kind=kOutput, calls=%fused_computation.38 | convolution fusion | flops 1879048192 | bytes 12517376 | tf_op jit(solution)/shard_map/dot_general | solution.py:18
  227.7 5.7 %fusion.28 = f32[512,4096]{1,0:T(8,128)} fusion(bf16[448,512]{1,0:T(8,128)(2,1)S(1)} %get-tuple-element.9, bf16[1,448,4096]{2,1,0:T(8,128)(2,1)S(1)} %copy-done.3), kind=kOutput, calls=%fused_computation.50 | convolution fusion | flops 1879048192 | bytes 12517376 | tf_op jit(solution)/shard_map/dot_general | solution.py:18
  233.4 5.9 %fusion.12 = f32[512,4096]{1,0:T(8,128)} fusion(bf16[448,512]{1,0:T(8,128)(2,1)S(1)} %get-tuple-element.10, bf16[1,448,4096]{2,1,0:T(8,128)(2,1)S(1)} %copy-done.6), kind=kOutput, calls=%fused_computation.34 | convolution fusion | flops 1879048192 | bytes 12517376 | tf_op jit(solution)/shard_map/dot_general | solution.py:18
  239.3 5.7 %fusion.24 = f32[512,4096]{1,0:T(8,128)} fusion(bf16[448,512]{1,0:T(8,128)(2,1)S(1)} %get-tuple-element.12, bf16[1,448,4096]{2,1,0:T(8,128)(2,1)S(1)} %copy-done.3), kind=kOutput, calls=%fused_computation.46 | convolution fusion | flops 1879048192 | bytes 12517376 | tf_op jit(solution)/shard_map/dot_general | solution.py:18
  245.0 31.1 %all-gather.8.cloned.1.call-done = bf16[2,512,4096]{2,1,0:T(8,128)(2,1)} async-done(((bf16[2,32,4096]{2,1,0:T(8,128)(2,1)}), bf16[2,512,4096]{2,1,0:T(8,128)(2,1)}) %all-gather.8.cloned.1.call-update) | async-done | bytes 8388624 | tf_op jit(solution)/shard_map/all_gather | solution.py:252
  276.1 3.5 fusion.75
  279.7 4.6 fusion.22
  284.7 1.2 fusion.81
  286.7 2.1 fusion.32
  289.1 1.2 fusion.76
  291.2 2.3 fusion.10
  293.5 1.6 multiply_convert_fusion.4
  295.1 5.6 %fusion.20 = f32[512,4096]{1,0:T(8,128)} fusion(bf16[448,512]{1,0:T(8,128)(2,1)S(1)} %get-tuple-element.15, bf16[1,448,4096]{2,1,0:T(8,128)(2,1)S(1)} %copy-done.4), kind=kOutput, calls=%fused_computation.42 | convolution fusion | flops 1879048192 | bytes 12517376 | tf_op jit(solution)/shard_map/dot_general | solution.py:18
  300.9 5.6 %fusion.8 = f32[512,4096]{1,0:T(8,128)} fusion(bf16[448,512]{1,0:T(8,128)(2,1)S(1)} %get-tuple-element.13, bf16[1,448,4096]{2,1,0:T(8,128)(2,1)S(1)} %copy-done.7), kind=kOutput, calls=%fused_computation.30 | convolution fusion | flops 1879048192 | bytes 12517376 | tf_op jit(solution)/shard_map/dot_general | solution.py:18
  307.4 1.2 convolution_convert_fusion
  309.0 1.0 copy.85
  310.0 7.2 %add_convert_fusion.2 = bf16[512,4096]{1,0:T(8,128)(2,1)S(1)} fusion(f32[512,4096]{1,0:T(8,128)} %fusion.16, f32[512,4096]{1,0:T(8,128)} %fusion.28, bf16[16,4096]{1,0:T(8,128)(2,1)S(1)} %bitcast.298, bf16[16,4096]{1,0:T(8,128)(2,1)S(1)} %bitcast.301, bf16[512,16]{0,1:T(8,128)(2,1)S(1)} %convolution_convert_fusion.7, ...), kind=kOutput, calls=%fused_computation.11 | convolution fusion | flops 143196160 | bytes 21266432 | tf_op jit(solution)/shard_map/dot_general | solution.py:18
  317.2 7.2 %add_convert_fusion.1 = bf16[512,4096]{1,0:T(8,128)(2,1)S(1)} fusion(f32[512,4096]{1,0:T(8,128)} %fusion.12, f32[512,4096]{1,0:T(8,128)} %fusion.24, bf16[16,4096]{1,0:T(8,128)(2,1)S(1)} %bitcast.299, bf16[16,4096]{1,0:T(8,128)(2,1)S(1)} %bitcast.302, bf16[512,16]{0,1:T(8,128)(2,1)S(1)} %convolution_convert_fusion.5, ...), kind=kOutput, calls=%fused_computation.10 | convolution fusion | flops 143196160 | bytes 21266432 | tf_op jit(solution)/shard_map/dot_general | solution.py:18
  324.5 1.2 slice-done.3
  325.7 3.2 add_convert_fusion
  328.9 11.1 %fusion.1 = bf16[16,96,4224]{2,1,0:T(8,128)(2,1)} fusion(bf16[16,96,48]{2,1,0:T(8,128)(2,1)} %copy.85, bf16[16,32,4096]{2,1,0:T(8,128)(2,1)} %bitcast.272, bf16[16,32,4096]{2,1,0:T(8,128)(2,1)S(1)} %bitcast.271, bf16[16,32,4096]{2,1,0:T(8,128)(2,1)S(1)} %bitcast.270), kind=kLoop, calls=%fused_computation.8 | loop fusion | flops 64880640 | bytes 25706496 | tf_op jit(solution)/shard_map/concatenate | solution.py:267
  340.9 1.2 fusion.143
  342.1 1.3 convolution_add_fusion.7
  343.4 1.9 fusion.70
  348.1 87.4 %reduce-scatter.4.cloned.1.call-done = bf16[1,96,4224]{2,1,0:T(8,128)(2,1)} async-done(((bf16[16,96,4224]{2,1,0:T(8,128)(2,1)}), bf16[1,96,4224]{2,1,0:T(8,128)(2,1)}) %reduce-scatter.4.cloned.1.call-update) | async-done | bytes 811024
  435.5 1.3 slice.110.src_ref
  436.8 1.2 slice.109
  438.0 9.6 %shard_map.180 = bf16[16,96,128]{2,1,0:T(8,128)(2,1)} custom-call(bf16[96,128]{1,0:T(8,128)(2,1)} %slice.110.src_ref), custom_call_target="tpu_custom_call" | custom-call | tf_op jit(solution)/shard_map/pallas_call | solution.py:179
  447.6 1.1 fusion.140
  449.6 7.2 %all-to-all-start.1 = ((bf16[96,8,512]{2,0,1:T(8,128)(2,1)}), bf16[96,8,512]{2,0,1:T(8,128)(2,1)S(1)}, u32[]{:S(2)}, u32[]{:S(2)}) async-start(bf16[96,8,512]{2,0,1:T(8,128)(2,1)} %bitcast.264), calls=%async_computation.1 | async-start | bytes 1572864 | tf_op jit(solution)/shard_map/all_to_all | solution.py:287
  456.9 3.1 fusion.38
  460.0 3.1 fusion.42
  463.1 2.9 fusion.43
  468.2 1.4 slice-done.11
  469.6 1.5 fusion.5
  471.1 1.4 fusion.7
  472.5 1.5 fusion.3
  474.4 1.0 gather_fusion.3
  475.7 1.3 reduce_sum.29
  (187 shorter events, 24.0 us)
Async XLA Ops:
  7.2 132.0 %copy-start = (bf16[1,4096,16]{1,2,0:T(8,128)(2,1)S(1)}, bf16[1,4096,16]{1,2,0:T(8,128)(2,1)}, u32[]{:S(2)}) copy-start(bf16[1,4096,16]{1,2,0:T(8,128)(2,1)} %param.25) | copy-start | bytes 393220
  7.2 12.6 %copy-start.20 = (bf16[128,512]{1,0:T(8,128)(2,1)S(1)}, bf16[128,512]{1,0:T(8,128)(2,1)}, u32[]{:S(2)}) copy-start(bf16[128,512]{1,0:T(8,128)(2,1)} %param.14) | copy-start | bytes 393220
  7.2 12.6 %copy-start.21 = (bf16[128,512]{1,0:T(8,128)(2,1)S(1)}, bf16[128,512]{1,0:T(8,128)(2,1)}, u32[]{:S(2)}) copy-start(bf16[128,512]{1,0:T(8,128)(2,1)} %param.13) | copy-start | bytes 393220
  7.2 123.5 %all-gather.4.cloned.1.call-start = ((), (), s32[]{:S(2)}) async-start(), calls=%async_computation.3 | async-start | bytes 8912896 | tf_op jit(solution)/shard_map/all_gather | solution.py:252
  56.2 74.5 %copy-start.14 = (bf16[1,16,4096]{2,1,0:T(8,128)(2,1)S(1)}, bf16[1,16,4096]{2,1,0:T(8,128)(2,1)}, u32[]{:S(2)}) copy-start(bf16[1,16,4096]{2,1,0:T(8,128)(2,1)} %param.22) | copy-start | bytes 393220
  60.0 143.2 %all-gather.6.cloned.1.call-start = ((), (), s32[]{:S(2)}) async-start(), calls=%async_computation.4 | async-start | bytes 8912896 | tf_op jit(solution)/shard_map/all_gather | solution.py:252
  60.8 215.3 %all-gather.8.cloned.1.call-start = ((), (), s32[]{:S(2)}) async-start(), calls=%async_computation.5 | async-start | bytes 8912896 | tf_op jit(solution)/shard_map/all_gather | solution.py:252
  61.5 374.0 %reduce-scatter.4.cloned.1.call-start = ((), (), s32[]{:S(2)}) async-start(), calls=%async_computation.6 | async-start | bytes 13787136
  130.7 3.5 copy-start.2
  130.7 8.5 %slice-start.12 = ((s8[8388608]{0:T(1024)(128)(4,1)}), s8[4194304]{0:T(1024)(128)(4,1)S(1)}, s32[]{:S(2)}) async-start(s8[8388608]{0:T(1024)(128)(4,1)} %bitcast.281), calls=%async_computation.19 | async-start | bytes 8388608
  134.2 4.6 copy-start.17
  134.2 5.0 %slice-start.13 = ((s8[8388608]{0:T(1024)(128)(4,1)}), s8[4194304]{0:T(1024)(128)(4,1)S(1)}, s32[]{:S(2)}) async-start(s8[8388608]{0:T(1024)(128)(4,1)} %bitcast.281), calls=%async_computation.20 | async-start | bytes 8388608
  139.2 2.0 copy-start.39
  141.3 2.1 copy-start.22
  141.3 2.1 copy-start.18
  141.3 2.5 copy-start.15
  143.7 2.1 copy-start.5
  145.8 2.1 copy-start.32
  145.8 2.1 copy-start.19
  148.7 157.9 %copy-start.12 = (bf16[448,512]{1,0:T(8,128)(2,1)}, bf16[448,512]{1,0:T(8,128)(2,1)S(1)}, u32[]{:S(2)}) copy-start(bf16[448,512]{1,0:T(8,128)(2,1)S(1)} %get-tuple-element.8) | copy-start | bytes 1376260
  203.3 3.5 copy-start.3
  203.3 8.9 %slice-start.4 = ((s8[8388608]{0:T(1024)(128)(4,1)}), s8[4194304]{0:T(1024)(128)(4,1)S(1)}, s32[]{:S(2)}) async-start(s8[8388608]{0:T(1024)(128)(4,1)} %bitcast.273), calls=%async_computation.11 | async-start | bytes 8388608
  206.8 5.1 %copy-start.24 = (bf16[512,16]{0,1:T(8,128)(2,1)}, bf16[512,16]{0,1:T(8,128)(2,1)S(1)}, u32[]{:S(2)}) copy-start(bf16[512,16]{0,1:T(8,128)(2,1)S(1)} %fusion.77) | copy-start | bytes 49156
  206.8 5.4 %slice-start.5 = ((s8[8388608]{0:T(1024)(128)(4,1)}), s8[4194304]{0:T(1024)(128)(4,1)S(1)}, s32[]{:S(2)}) async-start(s8[8388608]{0:T(1024)(128)(4,1)} %bitcast.273), calls=%async_computation.12 | async-start | bytes 8388608
  212.2 2.0 copy-start.40
  214.3 2.1 copy-start.26
  216.7 2.0 copy-start.6
  218.8 2.1 copy-start.34
  221.6 85.4 %copy-start.13 = (bf16[448,512]{1,0:T(8,128)(2,1)}, bf16[448,512]{1,0:T(8,128)(2,1)S(1)}, u32[]{:S(2)}) copy-start(bf16[448,512]{1,0:T(8,128)(2,1)S(1)} %get-tuple-element.11) | copy-start | bytes 1376260
  276.1 3.5 copy-start.4
  276.1 8.5 %slice-start.8 = ((s8[8388608]{0:T(1024)(128)(4,1)}), s8[4194304]{0:T(1024)(128)(4,1)S(1)}, s32[]{:S(2)}) async-start(s8[8388608]{0:T(1024)(128)(4,1)} %bitcast.277), calls=%async_computation.15 | async-start | bytes 8388608
  279.6 4.6 copy-start.28
  279.6 5.0 %slice-start.9 = ((s8[8388608]{0:T(1024)(128)(4,1)}), s8[4194304]{0:T(1024)(128)(4,1)S(1)}, s32[]{:S(2)}) async-start(s8[8388608]{0:T(1024)(128)(4,1)} %bitcast.277), calls=%async_computation.16 | async-start | bytes 8388608
  284.6 2.0 copy-start.41
  286.7 2.1 copy-start.30
  289.1 2.0 copy-start.7
  291.2 2.3 copy-start.36
  295.1 5.6 %copy-start.10 = (bf16[448,512]{1,0:T(8,128)(2,1)}, bf16[448,512]{1,0:T(8,128)(2,1)S(1)}, u32[]{:S(2)}) copy-start(bf16[448,512]{1,0:T(8,128)(2,1)S(1)} %get-tuple-element.15) | copy-start | bytes 1376260
  295.1 11.4 %copy-start.8 = (bf16[448,512]{1,0:T(8,128)(2,1)}, bf16[448,512]{1,0:T(8,128)(2,1)S(1)}, u32[]{:S(2)}) copy-start(bf16[448,512]{1,0:T(8,128)(2,1)S(1)} %get-tuple-element.13) | copy-start | bytes 1376260
  310.0 7.2 %copy-start.16 = (bf16[1,16,4096]{2,1,0:T(8,128)(2,1)S(1)}, bf16[1,16,4096]{2,1,0:T(8,128)(2,1)}, u32[]{:S(2)}) copy-start(bf16[1,16,4096]{2,1,0:T(8,128)(2,1)} %param.20) | copy-start | bytes 393220
  310.0 14.4 %slice-start = ((s8[8388608]{0:T(1024)(128)(4,1)}), s8[4194304]{0:T(1024)(128)(4,1)S(1)}, s32[]{:S(2)}) async-start(s8[8388608]{0:T(1024)(128)(4,1)} %bitcast.265), calls=%async_computation.7 | async-start | bytes 8388608
  310.0 14.4 %slice-start.2 = ((s8[8388608]{0:T(1024)(128)(4,1)}), s8[4194304]{0:T(1024)(128)(4,1)S(1)}, s32[]{:S(2)}) async-start(s8[8388608]{0:T(1024)(128)(4,1)} %bitcast.267), calls=%async_computation.9 | async-start | bytes 8388608
  317.2 7.3 %slice-start.1 = ((s8[8388608]{0:T(1024)(128)(4,1)}), s8[4194304]{0:T(1024)(128)(4,1)S(1)}, s32[]{:S(2)}) async-start(s8[8388608]{0:T(1024)(128)(4,1)} %bitcast.265), calls=%async_computation.8 | async-start | bytes 8388608
  317.2 8.5 %slice-start.3 = ((s8[8388608]{0:T(1024)(128)(4,1)}), s8[4194304]{0:T(1024)(128)(4,1)S(1)}, s32[]{:S(2)}) async-start(s8[8388608]{0:T(1024)(128)(4,1)} %bitcast.267), calls=%async_computation.10 | async-start | bytes 8388608
  340.0 0.6 copy-start.38
  340.0 0.9 copy-start.23
  340.0 2.1 copy-start.27
  340.0 3.4 copy-start.31
  340.0 5.5 %copy-start.25 = (bf16[512,16]{0,1:T(8,128)(2,1)S(1)}, bf16[512,16]{0,1:T(8,128)(2,1)}, u32[]{:S(2)}) copy-start(bf16[512,16]{0,1:T(8,128)(2,1)} %copy-done.24) | copy-start | bytes 49156
  340.0 5.8 %copy-start.11 = (bf16[448,512]{1,0:T(8,128)(2,1)S(1)}, bf16[448,512]{1,0:T(8,128)(2,1)}, u32[]{:S(2)}) copy-start(bf16[448,512]{1,0:T(8,128)(2,1)} %copy-done.10) | copy-start | bytes 1376260
  340.0 5.8 %copy-start.29 = (bf16[512,16]{0,1:T(8,128)(2,1)S(1)}, bf16[512,16]{0,1:T(8,128)(2,1)}, u32[]{:S(2)}) copy-start(bf16[512,16]{0,1:T(8,128)(2,1)} %copy-done.28) | copy-start | bytes 49156
  340.0 6.7 %copy-start.33 = (bf16[512,16]{0,1:T(8,128)(2,1)S(1)}, bf16[512,16]{0,1:T(8,128)(2,1)}, u32[]{:S(2)}) copy-start(bf16[512,16]{0,1:T(8,128)(2,1)} %copy-done.32) | copy-start | bytes 49156
  340.1 6.9 %copy-start.35 = (bf16[512,16]{0,1:T(8,128)(2,1)S(1)}, bf16[512,16]{0,1:T(8,128)(2,1)}, u32[]{:S(2)}) copy-start(bf16[512,16]{0,1:T(8,128)(2,1)} %copy-done.34) | copy-start | bytes 49156
  340.1 7.1 %copy-start.9 = (bf16[448,512]{1,0:T(8,128)(2,1)S(1)}, bf16[448,512]{1,0:T(8,128)(2,1)}, u32[]{:S(2)}) copy-start(bf16[448,512]{1,0:T(8,128)(2,1)} %copy-done.8) | copy-start | bytes 1376260
  340.1 7.1 %copy-start.37 = (bf16[512,16]{0,1:T(8,128)(2,1)S(1)}, bf16[512,16]{0,1:T(8,128)(2,1)}, u32[]{:S(2)}) copy-start(bf16[512,16]{0,1:T(8,128)(2,1)} %copy-done.36) | copy-start | bytes 49156
  449.6 24.3 %all-to-all-start.1 = ((bf16[96,8,512]{2,0,1:T(8,128)(2,1)}), bf16[96,8,512]{2,0,1:T(8,128)(2,1)S(1)}, u32[]{:S(2)}, u32[]{:S(2)}) async-start(bf16[96,8,512]{2,0,1:T(8,128)(2,1)} %bitcast.264), calls=%async_computation.1 | async-start | bytes 1572864 | tf_op jit(solution)/shard_map/all_to_all | solution.py:287
  456.9 9.1 %slice-start.6 = ((s8[8388608]{0:T(1024)(128)(4,1)}), s8[4194304]{0:T(1024)(128)(4,1)S(1)}, s32[]{:S(2)}) async-start(s8[8388608]{0:T(1024)(128)(4,1)} %bitcast.275), calls=%async_computation.13 | async-start | bytes 8388608
  460.0 6.0 %slice-start.7 = ((s8[8388608]{0:T(1024)(128)(4,1)}), s8[4194304]{0:T(1024)(128)(4,1)S(1)}, s32[]{:S(2)}) async-start(s8[8388608]{0:T(1024)(128)(4,1)} %bitcast.275), calls=%async_computation.14 | async-start | bytes 8388608
  465.9 2.2 slice-start.10
  466.7 2.9 slice-start.11
  472.5 4.6 copy-start.1
Sparse Core Ops, SparseCore 0:
  60.2 70.4 all-gather.3
  132.9 70.3 all-gather.5
  205.5 70.5 all-gather.7
  340.2 95.2 reduce-scatter.3

commit v5 on v3

--- a/solution.py
+++ b/solution.py
@@ -184,6 +184,44 @@
         scratch_shapes=[pltpu.SemaphoreType.DMA((n,)), pltpu.SemaphoreType.DMA((n,))],
         compiler_params=pltpu.CompilerParams(collective_id=0, has_side_effects=True),
     )(block)
+
+
+def a2a_expert_kernel(n, src_ref, out_ref, send_sem, recv_sem):
+    me = lax.axis_index("expert")
+    row = lax.axis_index("dp")
+    barrier = pltpu.get_barrier_semaphore()
+    for k in range(1, n):
+        peer = lax.rem(me + k, n)
+        pl.semaphore_signal(barrier, inc=1, device_id=(row, peer), device_id_type=MESH)
+    pl.semaphore_wait(barrier, n - 1)
+    copies = []
+    for k in range(1, n):
+        peer = lax.rem(me + k, n)
+        cp = pltpu.make_async_remote_copy(
+            src_ref.at[peer],
+            out_ref.at[me],
+            send_sem.at[k],
+            recv_sem.at[k],
+            device_id=(row, peer),
+            device_id_type=MESH,
+        )
+        cp.start()
+        copies.append(cp)
+    out_ref[me] = src_ref[me]
+    for cp in copies:
+        cp.wait()
+
+
+def a2a_expert(blocks):
+    n = blocks.shape[0]
+    return pl.pallas_call(
+        functools.partial(a2a_expert_kernel, n),
+        out_shape=jax.ShapeDtypeStruct(blocks.shape, blocks.dtype),
+        in_specs=[pl.BlockSpec(memory_space=pltpu.VMEM)],
+        out_specs=pl.BlockSpec(memory_space=pltpu.VMEM),
+        scratch_shapes=[pltpu.SemaphoreType.DMA((n,)), pltpu.SemaphoreType.DMA((n,))],
+        compiler_params=pltpu.CompilerParams(collective_id=1, has_side_effects=True),
+    )(blocks)
 
 
 def local(
@@ -238,8 +276,8 @@
         .reshape(experts, capacity, feat_local)
     )
     send_both = jnp.concatenate([send_x, send_dy], axis=2)
-    recv_both = lax.all_to_all(send_both, "expert", split_axis=0, concat_axis=2, tiled=True)[0]
-    recv_both = recv_both.reshape(capacity, experts, 2, feat_local).transpose(2, 0, 1, 3)
+    recv_both = a2a_expert(send_both)
+    recv_both = recv_both.reshape(experts, capacity, 2, feat_local).transpose(2, 1, 0, 3)
     recv_both = recv_both.reshape(2, capacity, complete_width)
 
     rows_chunks = []

time: 461 us -> 460 us (level)
  blocking collectives: 27.4 us -> 0 us
  Pallas kernels: 10.8 us -> 37.7 us
    all_to_all x1 -> x0, blocking collectives: 27.4 us -> none  [local(): lax.all_to_all(send_both, 'expert', split_axis=0, concat_axis=2, tiled=True)]
    pallas_call x0 -> x1, Pallas kernels: none -> 26.9 us  [a2a_expert(): pl.pallas_call(functools.partial(a2a_expert_kernel, n), out_shape=jax.Sha...]
where the time goes in v5:
time: 460 us; the launch traced here: 454 us
  waiting for transfers between devices  233 us (51%)
  matrix products  117 us (25%)
  Pallas kernels  37.7 us (8%)
  local copies, waits for them, and re-layouts  29.7 us (6%)
  other arithmetic  15.9 us (3%)
  between operations  14.9 us (3%)
  starting transfers between devices  6.26 us (1%)
    all_gather x2, waiting for transfers between devices, local(): gathered = lax.all_gather(part, 'dp', axis=1, tiled=True)  143 us
    dot_general x42, matrix products, contract_pair(): lax.dot_general(left, right, (((left_axis,), (right_axis,)), ((), ())), p...  117 us
    unnamed x4, waiting for transfers between devices  89.7 us
    pallas_call x1, Pallas kernels, a2a_expert(): pl.pallas_call(functools.partial(a2a_expert_kernel, n), out_shape=jax.Sha...  26.9 us
    pallas_call x1, Pallas kernels, gather_dp(): pl.pallas_call(functools.partial(gather_dp_kernel, n), out_shape=jax.Shap...  10.8 us
    concatenate x1, other arithmetic, local(): packed = jnp.concatenate([rows_all, parts_all], 2)  10.4 us
  transfers between devices with their start and end apart: 4, of which 3 were waited for; matrix products, arithmetic and copies ran while one was open for 13% of the time, Pallas kernels for 2%

profile of v5, /device:TPU:1, one launch (start us, length us, event | category | flops | bytes accessed | tf_op | source)
XLA Modules:
  0.0 454.1 jit_solution(5515228662605352183)
XLA Ops:
  7.2 0.8 convert_reduce_fusion
  8.4 0.7 select_reduce_fusion
  9.1 0.7 compare_select_fusion.3
  10.0 0.8 copy.43
  11.3 1.4 scatter_custom_fusion.1
  12.7 1.4 scatter_custom_fusion
  14.1 5.0 %gather_fusion.1 = f32[768]{0:T(1024)S(1)} fusion(f32[256]{0:T(256)S(1)} %reshape.107, s32[1024]{0:T(1024)S(1)} %get-tuple-element.21), kind=kCustom, calls=%fused_computation.1 | custom fusion | bytes 9216 | tf_op jit(solution)/shard_map/gather | solution.py:267
  19.2 2.7 gather_fusion.2
  21.9 2.7 gather_fusion
  24.9 1.4 pad_maximum_fusion.1.src_ref
  26.3 26.9 %shard_map.180 = bf16[8,96,1024]{2,1,0:T(8,128)(2,1)} custom-call(bf16[8,96,1024]{2,1,0:T(8,128)(2,1)} %pad_maximum_fusion.1.src_ref), custom_call_target="tpu_custom_call" | custom-call | tf_op jit(solution)/shard_map/pallas_call | solution.py:217
  53.2 2.9 reshape.108
  56.0 0.9 copy.57
  56.9 0.8 reshape.109
  57.7 1.3 fusion.103
  59.0 0.7 all-gather.5.cloned.1.call-update
  59.7 0.6 reduce-scatter.4.cloned.1.call-start
  60.3 88.6 %all-gather.3.cloned.1.call-done = bf16[2,768,4096]{2,1,0:T(8,128)(2,1)} async-done(((bf16[2,48,4096]{2,1,0:T(8,128)(2,1)}), bf16[2,768,4096]{2,1,0:T(8,128)(2,1)}) %all-gather.3.cloned.1.call-update) | async-done | bytes 12582928 | tf_op jit(solution)/shard_map/all_gather | solution.py:290
  148.9 4.7 %fusion.54 = bf16[768,16]{0,1:T(8,128)(2,1)S(1)} fusion(bf16[2,768,4096]{2,1,0:T(8,128)(2,1)} %all-gather.3.cloned.1.call-done, bf16[1,16,4096]{2,1,0:T(8,128)(2,1)S(1)} %copy-done.7), kind=kOutput, calls=%fused_computation.87 | convolution fusion | flops 100675584 | bytes 6447104 | tf_op jit(solution)/shard_map/dot_general | solution.py:18
  153.6 6.0 %fusion.27 = f32[768,448]{0,1:T(8,128)S(1)} fusion(bf16[1,448,4096]{2,1,0:T(8,128)(2,1)S(1)} %copy-done.2, bf16[2,768,4096]{2,1,0:T(8,128)(2,1)} %all-gather.3.cloned.1.call-done), kind=kOutput, calls=%fused_computation.42 | convolution fusion | flops 2818572288 | bytes 11337728 | tf_op jit(solution)/shard_map/dot_general | solution.py:18
  160.1 1.7 fusion.57
  161.8 0.7 copy-done.28
  162.5 3.1 fusion.2
  166.0 1.7 fusion.55
  168.1 3.2 fusion.19
  171.3 1.9 multiply_convert_fusion.5
  173.6 6.4 %fusion.25 = f32[768,4096]{1,0:T(8,128)} fusion(bf16[448,768]{1,0:T(8,128)(2,1)S(1)} %get-tuple-element.9, bf16[1,448,4096]{2,1,0:T(8,128)(2,1)S(1)} %copy-done.2), kind=kOutput, calls=%fused_computation.40 | convolution fusion | flops 2818572288 | bytes 16941056 | tf_op jit(solution)/shard_map/dot_general | solution.py:18
  180.0 6.3 %fusion.17 = f32[768,4096]{1,0:T(8,128)} fusion(bf16[448,768]{1,0:T(8,128)(2,1)S(1)} %get-tuple-element.7, bf16[1,448,4096]{2,1,0:T(8,128)(2,1)S(1)} %copy-done.4), kind=kOutput, calls=%fused_computation.32 | convolution fusion | flops 2818572288 | bytes 16941056 | tf_op jit(solution)/shard_map/dot_general | solution.py:18
  186.3 54.4 %all-gather.5.cloned.1.call-done = bf16[2,768,4096]{2,1,0:T(8,128)(2,1)} async-done(((bf16[2,48,4096]{2,1,0:T(8,128)(2,1)}), bf16[2,768,4096]{2,1,0:T(8,128)(2,1)}) %all-gather.5.cloned.1.call-update) | async-done | bytes 12582928 | tf_op jit(solution)/shard_map/all_gather | solution.py:290
  240.7 4.7 %fusion.52 = bf16[768,16]{0,1:T(8,128)(2,1)S(1)} fusion(bf16[2,768,4096]{2,1,0:T(8,128)(2,1)} %all-gather.5.cloned.1.call-done, bf16[1,16,4096]{2,1,0:T(8,128)(2,1)S(1)} %copy-done.7), kind=kOutput, calls=%fused_computation.85 | convolution fusion | flops 100675584 | bytes 6447104 | tf_op jit(solution)/shard_map/dot_general | solution.py:18
  245.4 6.0 %fusion.23 = f32[768,448]{0,1:T(8,128)S(1)} fusion(bf16[1,448,4096]{2,1,0:T(8,128)(2,1)S(1)} %copy-done.3, bf16[2,768,4096]{2,1,0:T(8,128)(2,1)} %all-gather.5.cloned.1.call-done), kind=kOutput, calls=%fused_computation.38 | convolution fusion | flops 2818572288 | bytes 11337728 | tf_op jit(solution)/shard_map/dot_general | solution.py:18
  251.8 1.7 fusion.56
  253.8 3.1 fusion.5
  256.9 0.4 fusion.43
  257.3 1.7 fusion.53
  259.3 3.3 fusion.15
  262.6 1.0 multiply_convert_fusion.3
  263.8 6.3 %fusion.21 = f32[768,4096]{1,0:T(8,128)} fusion(bf16[448,768]{1,0:T(8,128)(2,1)S(1)} %get-tuple-element.12, bf16[1,448,4096]{2,1,0:T(8,128)(2,1)S(1)} %copy-done.3), kind=kOutput, calls=%fused_computation.36 | convolution fusion | flops 2818572288 | bytes 16941056 | tf_op jit(solution)/shard_map/dot_general | solution.py:18
  270.4 6.3 %fusion.13 = f32[768,4096]{1,0:T(8,128)} fusion(bf16[448,768]{1,0:T(8,128)(2,1)S(1)} %get-tuple-element.10, bf16[1,448,4096]{2,1,0:T(8,128)(2,1)S(1)} %copy-done.5), kind=kOutput, calls=%fused_computation.28 | convolution fusion | flops 2818572288 | bytes 16941056 | tf_op jit(solution)/shard_map/dot_general | solution.py:18
  277.1 1.3 convolution_convert_fusion.1
  278.7 9.3 %add_convert_fusion.1 = bf16[768,4096]{1,0:T(8,128)(2,1)S(1)} fusion(f32[768,4096]{1,0:T(8,128)} %fusion.17, f32[768,4096]{1,0:T(8,128)} %fusion.25, bf16[16,4096]{1,0:T(8,128)(2,1)S(1)} %bitcast.216, bf16[16,4096]{1,0:T(8,128)(2,1)S(1)} %bitcast.218, bf16[768,16]{0,1:T(8,128)(2,1)} %copy-done.12, bf16[768,16]{0,1:T(8,128)(2,1)} %copy-done.11), kind=kOutput, calls=%fused_computation.8 | convolution fusion | flops 214532096 | bytes 31768576 | tf_op jit(solution)/shard_map/dot_general | solution.py:18
  288.0 12.0 %add_convert_fusion = bf16[768,4096]{1,0:T(8,128)(2,1)} fusion(f32[768,4096]{1,0:T(8,128)} %fusion.13, f32[768,4096]{1,0:T(8,128)} %fusion.21, bf16[16,4096]{1,0:T(8,128)(2,1)S(1)} %bitcast.217, bf16[16,4096]{1,0:T(8,128)(2,1)S(1)} %bitcast.219, bf16[768,16]{0,1:T(8,128)(2,1)S(1)} %convolution_convert_fusion.2, bf16[768,16]{0,1:T(8,128)(2,1)S(1)} %convolution_convert_fusion.3), kind=kOutput, calls=%fused_computation.7 | convolution fusion | flops 214532096 | bytes 31768576 | tf_op jit(solution)/shard_map/dot_general | solution.py:18
  300.0 10.4 %pad_maximum_fusion = bf16[16,96,4224]{2,1,0:T(8,128)(2,1)} fusion(bf16[16,96,128]{2,1,0:T(8,128)(2,1)S(1)} %fusion.66, bf16[16,48,4096]{2,1,0:T(8,128)(2,1)} %bitcast.193, bf16[16,48,4096]{2,1,0:T(8,128)(2,1)S(1)} %bitcast.192), kind=kLoop, calls=%fused_computation.6 | loop fusion | flops 38928384 | bytes 25952256 | tf_op jit(solution)/shard_map/concatenate | solution.py:305
  310.7 0.4 copy-done.18
  311.1 1.4 fusion.107
  312.5 2.1 fusion.59
  314.9 1.0 fusion.63
  316.1 1.0 fusion.61
  317.1 89.0 %reduce-scatter.4.cloned.1.call-done = bf16[1,96,4224]{2,1,0:T(8,128)(2,1)} async-done(((bf16[16,96,4224]{2,1,0:T(8,128)(2,1)}), bf16[1,96,4224]{2,1,0:T(8,128)(2,1)}) %reduce-scatter.4.cloned.1.call-update) | async-done | bytes 811024
  406.1 1.3 slice.79.src_ref
  407.4 1.2 slice.78
  408.6 1.0 copy.58
  409.6 5.6 %all-to-all-start = ((bf16[96,8,512]{2,0,1:T(8,128)(2,1)}), bf16[96,8,512]{2,0,1:T(8,128)(2,1)S(1)}, u32[]{:S(2)}, u32[]{:S(2)}) async-start(bf16[96,8,512]{2,0,1:T(8,128)(2,1)} %bitcast.189), calls=%async_computation | async-start | bytes 1572864 | tf_op jit(solution)/shard_map/all_to_all | solution.py:325
  415.2 10.8 %shard_map.181 = bf16[16,96,128]{2,1,0:T(8,128)(2,1)} custom-call(bf16[96,128]{1,0:T(8,128)(2,1)} %slice.79.src_ref), custom_call_target="tpu_custom_call" | custom-call | tf_op jit(solution)/shard_map/pallas_call | solution.py:179
  426.0 1.1 fusion.104
  427.1 4.0 fusion
  431.1 4.1 fusion.31
  435.2 3.7 fusion.32
  438.9 1.7 fusion.9
  440.6 1.7 fusion.7
  442.3 1.7 fusion.12
  444.1 0.5 copy.56
  444.5 1.0 gather_fusion.3
  445.8 1.3 reduce_sum.29
  (122 shorter events, 6.4 us)
Async XLA Ops:
  7.2 152.9 %copy-start = (bf16[1,4096,16]{1,2,0:T(8,128)(2,1)S(1)}, bf16[1,4096,16]{1,2,0:T(8,128)(2,1)}, u32[]{:S(2)}) copy-start(bf16[1,4096,16]{1,2,0:T(8,128)(2,1)} %param.25) | copy-start | bytes 393220
  7.2 12.0 %copy-start.13 = (bf16[128,512]{1,0:T(8,128)(2,1)S(1)}, bf16[128,512]{1,0:T(8,128)(2,1)}, u32[]{:S(2)}) copy-start(bf16[128,512]{1,0:T(8,128)(2,1)} %param.13) | copy-start | bytes 393220
  7.2 12.0 %copy-start.14 = (bf16[128,512]{1,0:T(8,128)(2,1)S(1)}, bf16[128,512]{1,0:T(8,128)(2,1)}, u32[]{:S(2)}) copy-start(bf16[128,512]{1,0:T(8,128)(2,1)} %param.14) | copy-start | bytes 393220
  7.2 141.7 %all-gather.3.cloned.1.call-start = ((), (), s32[]{:S(2)}) async-start(), calls=%async_computation.2 | async-start | bytes 13369344 | tf_op jit(solution)/shard_map/all_gather | solution.py:290
  56.9 92.0 %copy-start.7 = (bf16[1,16,4096]{2,1,0:T(8,128)(2,1)S(1)}, bf16[1,16,4096]{2,1,0:T(8,128)(2,1)}, u32[]{:S(2)}) copy-start(bf16[1,16,4096]{2,1,0:T(8,128)(2,1)} %param.22) | copy-start | bytes 393220
  59.0 181.7 %all-gather.5.cloned.1.call-start = ((), (), s32[]{:S(2)}) async-start(), calls=%async_computation.3 | async-start | bytes 13369344 | tf_op jit(solution)/shard_map/all_gather | solution.py:290
  59.7 346.4 %reduce-scatter.4.cloned.1.call-start = ((), (), s32[]{:S(2)}) async-start(), calls=%async_computation.4 | async-start | bytes 13787136
  148.9 4.7 %copy-start.2 = (bf16[1,448,4096]{2,1,0:T(8,128)(2,1)S(1)}, bf16[1,448,4096]{2,1,0:T(8,128)(2,1)}, u32[]{:S(2)}) copy-start(bf16[1,448,4096]{2,1,0:T(8,128)(2,1)} %param.18) | copy-start | bytes 11010052
  148.9 11.1 %slice-start = ((s8[12582912]{0:T(1024)(128)(4,1)}), s8[4194304]{0:T(1024)(128)(4,1)S(1)}, s32[]{:S(2)}) async-start(s8[12582912]{0:T(1024)(128)(4,1)} %bitcast.195), calls=%async_computation.5 | async-start | bytes 8388608
  153.6 6.0 %copy-start.15 = (bf16[768,16]{0,1:T(8,128)(2,1)}, bf16[768,16]{0,1:T(8,128)(2,1)S(1)}, u32[]{:S(2)}) copy-start(bf16[768,16]{0,1:T(8,128)(2,1)S(1)} %fusion.54) | copy-start | bytes 73732
  153.6 6.0 %copy-start.9 = (bf16[1,448,16]{1,2,0:T(8,128)(2,1)S(1)}, bf16[1,448,16]{1,2,0:T(8,128)(2,1)}, u32[]{:S(2)}) copy-start(bf16[1,448,16]{1,2,0:T(8,128)(2,1)} %param.23) | copy-start | bytes 43012
  153.6 6.4 %slice-start.1 = ((s8[12582912]{0:T(1024)(128)(4,1)}), s8[4194304]{0:T(1024)(128)(4,1)S(1)}, s32[]{:S(2)}) async-start(s8[12582912]{0:T(1024)(128)(4,1)} %bitcast.195), calls=%async_computation.6 | async-start | bytes 8388608
  153.6 6.4 %slice-start.2 = ((s8[12582912]{0:T(1024)(128)(4,1)}), s8[4194304]{0:T(1024)(128)(4,1)S(1)}, s32[]{:S(2)}) async-start(s8[12582912]{0:T(1024)(128)(4,1)} %bitcast.195), calls=%async_computation.7 | async-start | bytes 8388608
  160.1 2.4 copy-start.28
  162.5 3.1 copy-start.17
  162.5 3.1 copy-start.10
  162.5 3.5 copy-start.8
  166.0 2.1 copy-start.4
  168.1 3.3 copy-start.24
  168.1 3.3 copy-start.23
  173.4 105.0 %copy-start.11 = (bf16[768,16]{0,1:T(8,128)(2,1)}, bf16[768,16]{0,1:T(8,128)(2,1)S(1)}, u32[]{:S(2)}) copy-start(bf16[768,16]{0,1:T(8,128)(2,1)S(1)} %convolution_convert_fusion.5) | copy-start | bytes 73732
  173.6 104.8 %copy-start.12 = (bf16[768,16]{0,1:T(8,128)(2,1)}, bf16[768,16]{0,1:T(8,128)(2,1)S(1)}, u32[]{:S(2)}) copy-start(bf16[768,16]{0,1:T(8,128)(2,1)S(1)} %convolution_convert_fusion.4) | copy-start | bytes 73732
  240.7 4.7 %copy-start.3 = (bf16[1,448,4096]{2,1,0:T(8,128)(2,1)S(1)}, bf16[1,448,4096]{2,1,0:T(8,128)(2,1)}, u32[]{:S(2)}) copy-start(bf16[1,448,4096]{2,1,0:T(8,128)(2,1)} %param.18) | copy-start | bytes 11010052
  240.7 11.1 %slice-start.3 = ((s8[12582912]{0:T(1024)(128)(4,1)}), s8[4194304]{0:T(1024)(128)(4,1)S(1)}, s32[]{:S(2)}) async-start(s8[12582912]{0:T(1024)(128)(4,1)} %bitcast.197), calls=%async_computation.8 | async-start | bytes 8388608
  245.3 6.0 %copy-start.19 = (bf16[768,16]{0,1:T(8,128)(2,1)}, bf16[768,16]{0,1:T(8,128)(2,1)S(1)}, u32[]{:S(2)}) copy-start(bf16[768,16]{0,1:T(8,128)(2,1)S(1)} %fusion.52) | copy-start | bytes 73732
  245.3 6.4 %slice-start.4 = ((s8[12582912]{0:T(1024)(128)(4,1)}), s8[4194304]{0:T(1024)(128)(4,1)S(1)}, s32[]{:S(2)}) async-start(s8[12582912]{0:T(1024)(128)(4,1)} %bitcast.197), calls=%async_computation.9 | async-start | bytes 8388608
  245.4 6.4 %slice-start.5 = ((s8[12582912]{0:T(1024)(128)(4,1)}), s8[4194304]{0:T(1024)(128)(4,1)S(1)}, s32[]{:S(2)}) async-start(s8[12582912]{0:T(1024)(128)(4,1)} %bitcast.197), calls=%async_computation.10 | async-start | bytes 8388608
  251.8 2.0 copy-start.29
  253.8 3.1 copy-start.21
  257.3 2.0 copy-start.5
  259.3 3.3 copy-start.26
  263.6 13.0 %copy-start.6 = (bf16[448,768]{1,0:T(8,128)(2,1)}, bf16[448,768]{1,0:T(8,128)(2,1)S(1)}, u32[]{:S(2)}) copy-start(bf16[448,768]{1,0:T(8,128)(2,1)S(1)} %get-tuple-element.11) | copy-start | bytes 2064388
  310.4 0.7 copy-start.18
  310.4 2.1 copy-start.22
  310.4 4.2 copy-start.25
  310.4 4.5 copy-start.27
  310.4 5.4 %copy-start.16 = (bf16[768,16]{0,1:T(8,128)(2,1)S(1)}, bf16[768,16]{0,1:T(8,128)(2,1)}, u32[]{:S(2)}) copy-start(bf16[768,16]{0,1:T(8,128)(2,1)} %copy-done.15) | copy-start | bytes 73732
  310.4 5.7 %copy-start.20 = (bf16[768,16]{0,1:T(8,128)(2,1)S(1)}, bf16[768,16]{0,1:T(8,128)(2,1)}, u32[]{:S(2)}) copy-start(bf16[768,16]{0,1:T(8,128)(2,1)} %copy-done.19) | copy-start | bytes 73732
  409.6 34.5 %all-to-all-start = ((bf16[96,8,512]{2,0,1:T(8,128)(2,1)}), bf16[96,8,512]{2,0,1:T(8,128)(2,1)S(1)}, u32[]{:S(2)}, u32[]{:S(2)}) async-start(bf16[96,8,512]{2,0,1:T(8,128)(2,1)} %bitcast.189), calls=%async_computation | async-start | bytes 1572864 | tf_op jit(solution)/shard_map/all_to_all | solution.py:325
  427.1 11.8 %slice-start.6 = ((s8[12582912]{0:T(1024)(128)(4,1)}), s8[4194304]{0:T(1024)(128)(4,1)S(1)}, s32[]{:S(2)}) async-start(s8[12582912]{0:T(1024)(128)(4,1)} %bitcast.199), calls=%async_computation.11 | async-start | bytes 8388608
  427.1 11.8 %slice-start.7 = ((s8[12582912]{0:T(1024)(128)(4,1)}), s8[4194304]{0:T(1024)(128)(4,1)S(1)}, s32[]{:S(2)}) async-start(s8[12582912]{0:T(1024)(128)(4,1)} %bitcast.199), calls=%async_computation.12 | async-start | bytes 8388608
  431.1 7.8 %slice-start.8 = ((s8[12582912]{0:T(1024)(128)(4,1)}), s8[4194304]{0:T(1024)(128)(4,1)S(1)}, s32[]{:S(2)}) async-start(s8[12582912]{0:T(1024)(128)(4,1)} %bitcast.199), calls=%async_computation.13 | async-start | bytes 8388608
  444.1 3.1 copy-start.1
Sparse Core Ops, SparseCore 0:
  59.1 89.7 all-gather.2
  151.0 89.5 all-gather.4
  310.6 95.4 reduce-scatter.3

commit v6 on v5

--- a/solution.py
+++ b/solution.py
@@ -119,6 +119,30 @@
     sigmoid_gate = jax.nn.sigmoid(gate_preactivation)
     silu_gate = gate_preactivation * sigmoid_gate
     hidden_units = (silu_gate * up_preactivation).astype(jnp.bfloat16)
+    down_partial = contract_pair(hidden_units, down_adapter_lower, 0, 1).astype(jnp.bfloat16)
+    (
+        output_gradient_rows,
+        gate_preactivation,
+        up_preactivation,
+        sigmoid_gate,
+        silu_gate,
+        hidden_units,
+        down_partial,
+        gate_projected_lower,
+        up_projected_lower,
+    ) = lax.optimization_barrier(
+        (
+            output_gradient_rows,
+            gate_preactivation,
+            up_preactivation,
+            sigmoid_gate,
+            silu_gate,
+            hidden_units,
+            down_partial,
+            gate_projected_lower,
+            up_projected_lower,
+        )
+    )
     down_projected_lower = contract_pair(b_down, output_gradient_rows, 0, 1).astype(jnp.bfloat16)
     hidden_gradient = contract_pair(
         down_weight, output_gradient_rows, 1, 1
@@ -132,7 +156,6 @@
     up_gradient = (hidden_gradient * silu_gate).astype(jnp.bfloat16)
     gate_partial = contract_pair(gate_gradient, gate_adapter_upper, 0, 0).astype(jnp.bfloat16)
     up_partial = contract_pair(up_gradient, up_adapter_upper, 0, 0).astype(jnp.bfloat16)
-    down_partial = contract_pair(hidden_units, down_adapter_lower, 0, 1).astype(jnp.bfloat16)
     paired_partials = jnp.concatenate([gate_partial, up_partial], 1)
     paired_factors = jnp.concatenate([a_gate, a_up], 0)
     gradient_rows_out = (
@@ -280,48 +303,25 @@
     recv_both = recv_both.reshape(experts, capacity, 2, feat_local).transpose(2, 1, 0, 3)
     recv_both = recv_both.reshape(2, capacity, complete_width)
 
-    rows_chunks = []
-    part_chunks = []
-    x_chunks = []
-    dy_chunks = []
-    owned_total = None
-    for c in range(chunks):
-        part = recv_both[:, c * piece:(c + 1) * piece]
-        gathered = lax.all_gather(part, "dp", axis=1, tiled=True)
-        x_rows = gathered[0]
-        dy_rows = gathered[1]
-        rows_out, parts, owned_slice = rows_backward_parts(x_rows, dy_rows, params)
-        if c == 0:
-            owned_total = owned_slice
-        else:
-            owned_total = jax.tree.map(jnp.add, owned_total, owned_slice)
-        rows_chunks.append(rows_out.astype(jnp.bfloat16).reshape(shards, piece, complete_width))
-        part_chunks.append(parts.reshape(shards, piece, 3 * adapter_rank))
-        x_chunks.append(x_rows)
-        dy_chunks.append(dy_rows)
-    rows_all = jnp.concatenate(rows_chunks, 1)
-    parts_all = jnp.concatenate(part_chunks, 1)
-    parts_all = jnp.pad(parts_all, ((0, 0), (0, 0), (0, PART_COLS - 3 * adapter_rank)))
-    packed = jnp.concatenate([rows_all, parts_all], 2)
+    x_rows = lax.all_gather(recv_both[0], "dp", axis=0, tiled=True)
+    dy_rows = lax.all_gather(recv_both[1], "dp", axis=0, tiled=True)
+    rows_out, parts, owned_total = rows_backward_parts(x_rows, dy_rows, params)
+    rows_all = rows_out.astype(jnp.bfloat16)
+    parts_all = jnp.pad(parts, ((0, 0), (0, PART_COLS - 3 * adapter_rank)))
+    packed = jnp.concatenate([rows_all, parts_all], 1).reshape(
+        shards, capacity, complete_width + PART_COLS
+    )
     summed_packed = lax.psum_scatter(packed, "dp", scatter_dimension=0, tiled=True)[0]
     summed = summed_packed[:, :complete_width]
     parts_mine = summed_packed[:, complete_width:]
-    parts_sum = gather_dp(parts_mine, shards).reshape(shards, chunks, piece, PART_COLS)
-    grad_a_gate = None
-    for c in range(chunks):
-        parts_c = parts_sum[:, c].reshape(shards * piece, PART_COLS)
-        a_gate_c = contract_pair(parts_c[:, :adapter_rank], x_chunks[c], 0, 0)
-        a_up_c = contract_pair(parts_c[:, adapter_rank:2 * adapter_rank], x_chunks[c], 0, 0)
-        b_down_c = contract_pair(dy_chunks[c], parts_c[:, 2 * adapter_rank:3 * adapter_rank], 0, 0)
-        if grad_a_gate is None:
-            grad_a_gate, grad_a_up, grad_b_down = a_gate_c, a_up_c, b_down_c
-        else:
-            grad_a_gate = grad_a_gate + a_gate_c
-            grad_a_up = grad_a_up + a_up_c
-            grad_b_down = grad_b_down + b_down_c
-    grad_a_gate = ADAPTER_SCALE * grad_a_gate
-    grad_a_up = ADAPTER_SCALE * grad_a_up
-    grad_b_down = ADAPTER_SCALE * grad_b_down
+    parts_sum = gather_dp(parts_mine, shards).reshape(shards * capacity, PART_COLS)
+    grad_a_gate = ADAPTER_SCALE * contract_pair(parts_sum[:, :adapter_rank], x_rows, 0, 0)
+    grad_a_up = ADAPTER_SCALE * contract_pair(
+        parts_sum[:, adapter_rank:2 * adapter_rank], x_rows, 0, 0
+    )
+    grad_b_down = ADAPTER_SCALE * contract_pair(
+        dy_rows, parts_sum[:, 2 * adapter_rank:3 * adapter_rank], 0, 0
+    )
     returned_rows = lax.all_to_all(
         summed.reshape(capacity, experts, feat_local),
         "expert",

time: 460 us -> 464 us (level)
  waiting for transfers between devices: 233 us -> 238 us
    dot_general x42 -> x21, matrix products: 117 us -> 116 us  [contract_pair(): lax.dot_general(left, right, (((left_axis,), (right_axis,)), ((), ())), p...]
    concatenate x2 -> x1, other arithmetic: 10.6 us -> 10.7 us  [local(): jnp.concatenate([rows_all, parts_all], 1)]
  transfers between devices with their start and end apart: 4 -> 4, of which waited for: 3 -> 3; matrix products, arithmetic and copies ran while one was open for 13% -> 12% of each run, Pallas kernels for 2% -> 2%
where the time goes in v6:
time: 464 us; the launch traced here: 458 us
  waiting for transfers between devices  238 us (51%)
  matrix products  116 us (25%)
  Pallas kernels  37.7 us (8%)
  local copies, waits for them, and re-layouts  29.4 us (6%)
  other arithmetic  16 us (3%)
  between operations  14.4 us (3%)
  starting transfers between devices  5.81 us (1%)
    dot_general x21, matrix products, contract_pair(): lax.dot_general(left, right, (((left_axis,), (right_axis,)), ((), ())), p...  116 us
    unnamed x4, waiting for transfers between devices  90.6 us
    all_gather x1, waiting for transfers between devices, local(): x_rows = lax.all_gather(recv_both[0], 'dp', axis=0, tiled=True)  88.4 us
    all_gather x1, waiting for transfers between devices, local(): dy_rows = lax.all_gather(recv_both[1], 'dp', axis=0, tiled=True)  59 us
    pallas_call x1, Pallas kernels, a2a_expert(): pl.pallas_call(functools.partial(a2a_expert_kernel, n), out_shape=jax.Sha...  26.9 us
    pallas_call x1, Pallas kernels, gather_dp(): pl.pallas_call(functools.partial(gather_dp_kernel, n), out_shape=jax.Shap...  10.9 us
    concatenate x1, other arithmetic, local(): jnp.concatenate([rows_all, parts_all], 1)  10.7 us
  transfers between devices with their start and end apart: 4, of which 3 were waited for; matrix products, arithmetic and copies ran while one was open for 12% of the time, Pallas kernels for 2%

profile of v6, /device:TPU:1, one launch (start us, length us, event | category | flops | bytes accessed | tf_op | source)
XLA Modules:
  0.0 457.6 jit_solution(13851111496396557789)
XLA Ops:
  7.2 0.7 convert_reduce_fusion
  8.0 0.1 copy.36
  8.1 0.2 reduce_window_sum.11
  8.3 0.7 select_reduce_fusion
  9.0 0.7 compare_select_fusion.3
  9.7 0.1 copy.39
  9.8 0.1 reshape.97
  10.0 0.8 copy.40
  10.8 0.1 reshape.100
  10.9 0.1 reshape.154
  11.1 0.1 reshape.146
  11.2 1.4 scatter_custom_fusion.1
  12.6 1.4 scatter_custom_fusion
  14.1 5.0 %gather_fusion.1 = f32[768]{0:T(1024)S(1)} fusion(f32[256]{0:T(256)S(1)} %reshape.100, s32[1024]{0:T(1024)S(1)} %get-tuple-element.37), kind=kCustom, calls=%fused_computation.1 | custom fusion | bytes 9216 | tf_op jit(solution)/shard_map/gather | solution.py:290
  19.2 2.7 gather_fusion.2
  21.9 2.7 gather_fusion
  24.6 0.2 fusion.21
  24.8 1.4 pad_maximum_fusion.src_ref
  26.2 26.9 %shard_map.180 = bf16[8,96,1024]{2,1,0:T(8,128)(2,1)} custom-call(bf16[8,96,1024]{2,1,0:T(8,128)(2,1)} %pad_maximum_fusion.src_ref), custom_call_target="tpu_custom_call" | custom-call | tf_op jit(solution)/shard_map/pallas_call | solution.py:240
  53.1 2.9 reshape.101
  56.0 0.9 copy.54
  57.0 1.2 copy.49
  58.2 1.2 copy.48
  59.5 0.2 reduce-scatter.4.cloned.1.call-start
  59.7 88.4 %all-gather.5.cloned.1.call-done = bf16[1536,4096]{1,0:T(8,128)(2,1)} async-done(((bf16[96,4096]{1,0:T(8,128)(2,1)}), bf16[1536,4096]{1,0:T(8,128)(2,1)}) %all-gather.5.cloned.1.call-update) | async-done | bytes 12582928 | tf_op jit(solution)/shard_map/all_gather | solution.py:306
  148.1 8.1 %convolution_convert_fusion.5 = bf16[1536,16]{0,1:T(8,128)(2,1)S(1)} fusion(bf16[1536,4096]{1,0:T(8,128)(2,1)} %all-gather.5.cloned.1.call-done, bf16[1,16,4096]{2,1,0:T(8,128)(2,1)S(1)} %copy-done.13), kind=kOutput, calls=%fused_computation.44 | convolution fusion | flops 201351168 | bytes 12763136 | tf_op jit(solution)/shard_map/dot_general | solution.py:18
  156.2 8.0 %fusion.13 = f32[1536,448]{0,1:T(8,128)S(1)} fusion(bf16[1536,4096]{1,0:T(8,128)(2,1)S(1)} %copy-done.2, bf16[1,448,4096]{2,1,0:T(8,128)(2,1)} %param.17), kind=kOutput, calls=%fused_computation.24 | convolution fusion | flops 5637144576 | bytes 19005440 | tf_op jit(solution)/shard_map/dot_general | solution.py:18
  164.2 0.6 fusion.18
  164.8 0.3 copy-done.14
  165.1 3.3 convolution_convert_fusion.4
  168.5 6.1 %fusion.9 = f32[1536,448]{0,1:T(8,128)S(1)} fusion(bf16[1536,4096]{1,0:T(8,128)(2,1)S(1)} %copy-done.2, bf16[1,448,4096]{2,1,0:T(8,128)(2,1)S(1)} %copy-done.20), kind=kOutput, calls=%fused_computation.20 | convolution fusion | flops 5637144576 | bytes 19005440 | tf_op jit(solution)/shard_map/dot_general | solution.py:18
  174.6 3.9 multiply_convert_fusion.2
  178.5 1.6 copy-done.10
  180.1 0.9 convolution_convert_fusion.2
  181.0 59.0 %all-gather.3.cloned.1.call-done = bf16[1536,4096]{1,0:T(8,128)(2,1)} async-done(((bf16[96,4096]{1,0:T(8,128)(2,1)}), bf16[1536,4096]{1,0:T(8,128)(2,1)}) %all-gather.3.cloned.1.call-update) | async-done | bytes 12582928 | tf_op jit(solution)/shard_map/all_gather | solution.py:307
  240.0 8.1 %convolution_convert_fusion.3 = bf16[1536,16]{0,1:T(8,128)(2,1)S(1)} fusion(bf16[1536,4096]{1,0:T(8,128)(2,1)} %all-gather.3.cloned.1.call-done, bf16[1,4096,16]{1,2,0:T(8,128)(2,1)S(1)} %copy-done), kind=kOutput, calls=%fused_computation.42 | convolution fusion | flops 201351168 | bytes 12763136 | tf_op jit(solution)/shard_map/dot_general | solution.py:18
  248.1 8.5 %fusion.5 = f32[1536,448]{0,1:T(8,128)S(1)} fusion(bf16[1536,4096]{1,0:T(8,128)(2,1)S(1)} %copy-done.3, bf16[1,448,4096]{2,1,0:T(8,128)(2,1)} %param.19), kind=kOutput, calls=%fused_computation.16 | convolution fusion | flops 5637144576 | bytes 19005440 | tf_op jit(solution)/shard_map/dot_general | solution.py:18
  256.7 1.3 multiply_convert_fusion.1
  258.0 0.3 convolution_convert_fusion
  258.3 0.4 copy-done.21
  258.7 11.7 %fusion.7 = f32[1536,4096]{1,0:T(8,128)} fusion(bf16[448,1536]{1,0:T(8,128)(2,1)S(1)} %get-tuple-element.26, bf16[1,448,4096]{2,1,0:T(8,128)(2,1)S(1)} %copy-done.21), kind=kOutput, calls=%fused_computation.18 | convolution fusion | flops 5637144576 | bytes 30212096 | tf_op jit(solution)/shard_map/dot_general | solution.py:18
  270.5 0.3 convolution_convert_fusion.1
  270.7 11.7 %fusion.11 = f32[1536,4096]{1,0:T(8,128)} fusion(bf16[448,1536]{1,0:T(8,128)(2,1)S(1)} %get-tuple-element.25, bf16[1,448,4096]{2,1,0:T(8,128)(2,1)S(1)} %copy-done.22), kind=kOutput, calls=%fused_computation.22 | convolution fusion | flops 5637144576 | bytes 30212096 | tf_op jit(solution)/shard_map/dot_general | solution.py:18
  282.5 0.2 copy.46
  282.7 21.9 %add_convert_fusion = bf16[1536,4096]{1,0:T(8,128)(2,1)} fusion(f32[1536,4096]{1,0:T(8,128)} %fusion.11, f32[1536,4096]{1,0:T(8,128)} %fusion.7, bf16[16,4096]{1,0:T(8,128)(2,1)S(1)} %bitcast.127, bf16[16,4096]{1,0:T(8,128)(2,1)S(1)} %bitcast.126, bf16[1536,16]{0,1:T(8,128)(2,1)S(1)} %convolution_convert_fusion, ...), kind=kOutput, calls=%fused_computation.8 | convolution fusion | flops 428539904 | bytes 63275008 | tf_op jit(solution)/shard_map/dot_general | solution.py:18
  304.6 10.7 %fusion.1 = bf16[1536,4224]{1,0:T(8,128)(2,1)} fusion(bf16[1536,48]{1,0:T(8,128)(2,1)S(1)} %copy.46, bf16[1536,4096]{1,0:T(8,128)(2,1)} %add_convert_fusion), kind=kLoop, calls=%fused_computation.9 | loop fusion | flops 38928384 | bytes 25706496 | tf_op jit(solution)/shard_map/concatenate | solution.py:311
  315.3 0.1 copy.45
  315.4 0.1 reshape.136
  315.5 2.6 fusion.22
  318.1 1.1 fusion.23
  319.2 1.1 fusion.24
  320.3 90.5 %reduce-scatter.4.cloned.1.call-done = bf16[1,96,4224]{2,1,0:T(8,128)(2,1)} async-done(((bf16[16,96,4224]{2,1,0:T(8,128)(2,1)}), bf16[1,96,4224]{2,1,0:T(8,128)(2,1)}) %reduce-scatter.4.cloned.1.call-update) | async-done | bytes 811024
  410.9 1.3 slice.41.src_ref
  412.2 1.2 slice.40
  413.4 1.0 copy.55
  414.4 5.5 %all-to-all-start = ((bf16[96,8,512]{2,0,1:T(8,128)(2,1)}), bf16[96,8,512]{2,0,1:T(8,128)(2,1)S(1)}, u32[]{:S(2)}, u32[]{:S(2)}) async-start(bf16[96,8,512]{2,0,1:T(8,128)(2,1)} %bitcast.106), calls=%async_computation | async-start | bytes 1572864 | tf_op jit(solution)/shard_map/all_to_all | solution.py:325
  419.9 10.9 %shard_map.181 = bf16[16,96,128]{2,1,0:T(8,128)(2,1)} custom-call(bf16[96,128]{1,0:T(8,128)(2,1)} %slice.41.src_ref), custom_call_target="tpu_custom_call" | custom-call | tf_op jit(solution)/shard_map/pallas_call | solution.py:202
  430.8 7.3 %fusion.4 = f32[1,4096,16]{1,2,0:T(8,128)} fusion(bf16[1536,4096]{1,0:T(8,128)(2,1)} %all-gather.3.cloned.1.call-done, bf16[1536,128]{1,0:T(8,128)(2,1)} %bitcast.113), kind=kOutput, calls=%fused_computation.15 | convolution fusion | flops 201392128 | bytes 13238272 | tf_op jit(solution)/shard_map/dot_general | solution.py:18
  438.1 7.3 %fusion.2 = f32[1,16,4096]{2,1,0:T(8,128)} fusion(bf16[1536,4096]{1,0:T(8,128)(2,1)} %all-gather.5.cloned.1.call-done, bf16[1536,128]{1,0:T(8,128)(2,1)S(1)} %bitcast.114), kind=kOutput, calls=%fused_computation.11 | convolution fusion | flops 201392128 | bytes 13238272 | tf_op jit(solution)/shard_map/dot_general | solution.py:18
  445.4 2.5 fusion.3
  447.8 0.5 copy.53
  448.3 1.0 gather_fusion.3
  449.3 0.3 reshape.139
  449.6 1.3 reduce_sum.29
  (70 shorter events, 0.7 us)
Async XLA Ops:
  7.2 232.8 %copy-start = (bf16[1,4096,16]{1,2,0:T(8,128)(2,1)S(1)}, bf16[1,4096,16]{1,2,0:T(8,128)(2,1)}, u32[]{:S(2)}) copy-start(bf16[1,4096,16]{1,2,0:T(8,128)(2,1)} %param.25) | copy-start | bytes 393220
  7.2 12.0 %copy-start.15 = (bf16[128,512]{1,0:T(8,128)(2,1)S(1)}, bf16[128,512]{1,0:T(8,128)(2,1)}, u32[]{:S(2)}) copy-start(bf16[128,512]{1,0:T(8,128)(2,1)} %param.13) | copy-start | bytes 393220
  7.2 140.9 %all-gather.5.cloned.1.call-start = ((), (), s32[]{:S(2)}) async-start(), calls=%async_computation.3 | async-start | bytes 13369344 | tf_op jit(solution)/shard_map/all_gather | solution.py:306
  8.1 11.1 %copy-start.16 = (bf16[128,512]{1,0:T(8,128)(2,1)S(1)}, bf16[128,512]{1,0:T(8,128)(2,1)}, u32[]{:S(2)}) copy-start(bf16[128,512]{1,0:T(8,128)(2,1)} %param.14) | copy-start | bytes 393220
  57.0 91.1 %copy-start.13 = (bf16[1,16,4096]{2,1,0:T(8,128)(2,1)S(1)}, bf16[1,16,4096]{2,1,0:T(8,128)(2,1)}, u32[]{:S(2)}) copy-start(bf16[1,16,4096]{2,1,0:T(8,128)(2,1)} %param.20) | copy-start | bytes 393220
  58.1 181.8 %all-gather.3.cloned.1.call-start = ((), (), s32[]{:S(2)}) async-start(), calls=%async_computation.2 | async-start | bytes 13369344 | tf_op jit(solution)/shard_map/all_gather | solution.py:307
  59.5 351.4 %reduce-scatter.4.cloned.1.call-start = ((), (), s32[]{:S(2)}) async-start(), calls=%async_computation.4 | async-start | bytes 13787136
  148.1 8.2 %copy-start.2 = (bf16[1536,4096]{1,0:T(8,128)(2,1)S(1)}, bf16[1536,4096]{1,0:T(8,128)(2,1)}, u32[]{:S(2)}) copy-start(bf16[1536,4096]{1,0:T(8,128)(2,1)} %all-gather.5.cloned.1.call-done) | copy-start | bytes 37748740
  156.2 8.0 %copy-start.17 = (bf16[1,448,16]{1,2,0:T(8,128)(2,1)S(1)}, bf16[1,448,16]{1,2,0:T(8,128)(2,1)}, u32[]{:S(2)}) copy-start(bf16[1,448,16]{1,2,0:T(8,128)(2,1)} %param.21) | copy-start | bytes 43012
  164.2 0.9 copy-start.14
  165.1 3.3 copy-start.20
  168.4 6.1 %copy-start.18 = (bf16[1,448,16]{1,2,0:T(8,128)(2,1)S(1)}, bf16[1,448,16]{1,2,0:T(8,128)(2,1)}, u32[]{:S(2)}) copy-start(bf16[1,448,16]{1,2,0:T(8,128)(2,1)} %param.23) | copy-start | bytes 43012
  174.6 5.5 %copy-start.19 = (bf16[1,16,448]{2,1,0:T(8,128)(2,1)S(1)}, bf16[1,16,448]{2,1,0:T(8,128)(2,1)}, u32[]{:S(2)}) copy-start(bf16[1,16,448]{2,1,0:T(8,128)(2,1)} %param.24) | copy-start | bytes 43012
  178.5 1.6 copy-start.10
  240.0 8.2 %copy-start.3 = (bf16[1536,4096]{1,0:T(8,128)(2,1)S(1)}, bf16[1536,4096]{1,0:T(8,128)(2,1)}, u32[]{:S(2)}) copy-start(bf16[1536,4096]{1,0:T(8,128)(2,1)} %all-gather.3.cloned.1.call-done) | copy-start | bytes 37748740
  248.1 8.5 %copy-start.8 = (f32[448,1536]{1,0:T(8,128)S(1)}, f32[448,1536]{1,0:T(8,128)}, u32[]{:S(2)}) copy-start(f32[448,1536]{1,0:T(8,128)} %get-tuple-element.20) | copy-start | bytes 8257540
  248.1 8.5 %copy-start.9 = (f32[448,1536]{1,0:T(8,128)S(1)}, f32[448,1536]{1,0:T(8,128)}, u32[]{:S(2)}) copy-start(f32[448,1536]{1,0:T(8,128)} %get-tuple-element.18) | copy-start | bytes 8257540
  248.1 8.5 %copy-start.11 = (f32[448,1536]{1,0:T(8,128)S(1)}, f32[448,1536]{1,0:T(8,128)}, u32[]{:S(2)}) copy-start(f32[448,1536]{1,0:T(8,128)} %copy-done.10) | copy-start | bytes 8257540
  256.7 2.0 copy-start.21
  258.0 12.5 %copy-start.6 = (bf16[448,1536]{1,0:T(8,128)(2,1)}, bf16[448,1536]{1,0:T(8,128)(2,1)S(1)}, u32[]{:S(2)}) copy-start(bf16[448,1536]{1,0:T(8,128)(2,1)S(1)} %get-tuple-element.26) | copy-start | bytes 4128772
  258.0 12.8 %copy-start.4 = (bf16[448,1536]{1,0:T(8,128)(2,1)}, bf16[448,1536]{1,0:T(8,128)(2,1)S(1)}, u32[]{:S(2)}) copy-start(bf16[448,1536]{1,0:T(8,128)(2,1)S(1)} %get-tuple-element.25) | copy-start | bytes 4128772
  258.7 12.0 %copy-start.22 = (bf16[1,448,4096]{2,1,0:T(8,128)(2,1)S(1)}, bf16[1,448,4096]{2,1,0:T(8,128)(2,1)}, u32[]{:S(2)}) copy-start(bf16[1,448,4096]{2,1,0:T(8,128)(2,1)} %param.17) | copy-start | bytes 11010052
  315.2 2.9 copy-start.7
  315.3 4.0 copy-start.5
  414.4 33.5 %all-to-all-start = ((bf16[96,8,512]{2,0,1:T(8,128)(2,1)}), bf16[96,8,512]{2,0,1:T(8,128)(2,1)S(1)}, u32[]{:S(2)}, u32[]{:S(2)}) async-start(bf16[96,8,512]{2,0,1:T(8,128)(2,1)} %bitcast.106), calls=%async_computation | async-start | bytes 1572864 | tf_op jit(solution)/shard_map/all_to_all | solution.py:325
  430.7 7.3 %copy-start.12 = (bf16[16,96,128]{2,1,0:T(8,128)(2,1)S(1)}, bf16[16,96,128]{2,1,0:T(8,128)(2,1)}, u32[]{:S(2)}) copy-start(bf16[16,96,128]{2,1,0:T(8,128)(2,1)} %shard_map.181) | copy-start | bytes 1179652
  430.8 14.6 %slice-start = ((s8[12582912]{0:T(1024)(128)(4,1)}), s8[4194304]{0:T(1024)(128)(4,1)S(1)}, s32[]{:S(2)}) async-start(s8[12582912]{0:T(1024)(128)(4,1)} %bitcast.109), calls=%async_computation.5 | async-start | bytes 8388608
  430.8 14.6 %slice-start.1 = ((s8[12582912]{0:T(1024)(128)(4,1)}), s8[4194304]{0:T(1024)(128)(4,1)S(1)}, s32[]{:S(2)}) async-start(s8[12582912]{0:T(1024)(128)(4,1)} %bitcast.109), calls=%async_computation.6 | async-start | bytes 8388608
  438.1 7.3 %slice-start.2 = ((s8[12582912]{0:T(1024)(128)(4,1)}), s8[4194304]{0:T(1024)(128)(4,1)S(1)}, s32[]{:S(2)}) async-start(s8[12582912]{0:T(1024)(128)(4,1)} %bitcast.109), calls=%async_computation.7 | async-start | bytes 8388608
  448.3 2.6 copy-start.1
Sparse Core Ops, SparseCore 0:
  58.3 89.7 all-gather.4
  150.3 89.6 all-gather.2
  315.4 95.4 reduce-scatter.3

commit v7 on v6

--- a/solution.py
+++ b/solution.py
@@ -156,14 +156,27 @@
     up_gradient = (hidden_gradient * silu_gate).astype(jnp.bfloat16)
     gate_partial = contract_pair(gate_gradient, gate_adapter_upper, 0, 0).astype(jnp.bfloat16)
     up_partial = contract_pair(up_gradient, up_adapter_upper, 0, 0).astype(jnp.bfloat16)
-    paired_partials = jnp.concatenate([gate_partial, up_partial], 1)
-    paired_factors = jnp.concatenate([a_gate, a_up], 0)
-    gradient_rows_out = (
-        contract_pair(gate_gradient, gate_weight, 0, 0)
-        + contract_pair(up_gradient, up_weight, 0, 0)
-        + ADAPTER_SCALE * contract_pair(paired_partials, paired_factors, 1, 0)
-    )
     parts = jnp.concatenate([gate_partial, up_partial, down_partial], 1)
+    rank3 = parts.shape[1]
+    hidden_here, width = gate_weight.shape
+    lhs = jnp.concatenate([gate_gradient, up_gradient, parts.T], 0)
+    lora_rows = jnp.concatenate(
+        [
+            (ADAPTER_SCALE * a_gate.astype(jnp.float32)).astype(jnp.bfloat16),
+            (ADAPTER_SCALE * a_up.astype(jnp.float32)).astype(jnp.bfloat16),
+            jnp.zeros((rank3 - a_gate.shape[0] - a_up.shape[0], width), jnp.bfloat16),
+        ],
+        0,
+    )
+    left_block = jnp.concatenate([gate_weight, up_weight, lora_rows], 0)
+    picker = (
+        jnp.arange(2 * hidden_here + rank3, dtype=jnp.int32)[:, None] - 2 * hidden_here
+        == jnp.arange(PART_COLS, dtype=jnp.int32)[None, :]
+    ).astype(jnp.bfloat16)
+    extended = jnp.concatenate([left_block, picker], 1)
+    gradient_rows_out = lax.dot_general(
+        lhs, extended, (((0,), (0,)), ((), ())), preferred_element_type=jnp.float32
+    ).astype(jnp.bfloat16)
     owned_slice = (
         ADAPTER_SCALE * contract_pair(gate_gradient, gate_projected_lower, 1, 1),
         ADAPTER_SCALE * contract_pair(up_gradient, up_projected_lower, 1, 1),
@@ -306,11 +319,7 @@
     x_rows = lax.all_gather(recv_both[0], "dp", axis=0, tiled=True)
     dy_rows = lax.all_gather(recv_both[1], "dp", axis=0, tiled=True)
     rows_out, parts, owned_total = rows_backward_parts(x_rows, dy_rows, params)
-    rows_all = rows_out.astype(jnp.bfloat16)
-    parts_all = jnp.pad(parts, ((0, 0), (0, PART_COLS - 3 * adapter_rank)))
-    packed = jnp.concatenate([rows_all, parts_all], 1).reshape(
-        shards, capacity, complete_width + PART_COLS
-    )
+    packed = rows_out.reshape(shards, capacity, complete_width + PART_COLS)
     summed_packed = lax.psum_scatter(packed, "dp", scatter_dimension=0, tiled=True)[0]
     summed = summed_packed[:, :complete_width]
     parts_mine = summed_packed[:, complete_width:]

time: 464 us -> 427 us (0.920)
  matrix products: 116 us -> 91 us
  other arithmetic: 16 us -> 6.85 us
  waiting for transfers between devices: 238 us -> 229 us
  local copies, waits for them, and re-layouts: 29.4 us -> 35.7 us
    dot_general x21 -> x18, matrix products: 116 us -> 70.8 us  [contract_pair(): lax.dot_general(left, right, (((left_axis,), (right_axis,)), ((), ())), p...]
    dot_general x0 -> x1, matrix products: none -> 20.2 us  [rows_backward_parts(): lax.dot_general(lhs, extended, (((0,), (0,)), ((), ())), preferred_elemen...]
    concatenate x2 -> x0, other arithmetic: 10.7 us -> none  [the longest x1 10.7 us: local(): jnp.concatenate([rows_all, parts_all], 1)]
    all_gather x1, waiting for transfers between devices: 88.4 us -> 79.2 us  [local(): x_rows = lax.all_gather(recv_both[0], 'dp', axis=0, tiled=True)]
    unnamed x56 -> x55, local copies, waits for them, and re-layouts: 6 us -> 11.7 us
  transfers between devices with their start and end apart: 4 -> 4, of which waited for: 3 -> 3; matrix products, arithmetic and copies ran while one was open for 12% -> 15% of each run, Pallas kernels for 2% -> 3%
where the time goes in v7:
time: 427 us; the launch traced here: 421 us
  waiting for transfers between devices  229 us (54%)
  matrix products  91 us (21%)
  Pallas kernels  37.7 us (9%)
  local copies, waits for them, and re-layouts  35.7 us (8%)
  between operations  14.4 us (3%)
  other arithmetic  6.85 us (2%)
  starting transfers between devices  6.27 us (1%)
    unnamed x4, waiting for transfers between devices  90.3 us
    all_gather x1, waiting for transfers between devices, local(): x_rows = lax.all_gather(recv_both[0], 'dp', axis=0, tiled=True)  79.2 us
    dot_general x18, matrix products, contract_pair(): lax.dot_general(left, right, (((left_axis,), (right_axis,)), ((), ())), p...  70.8 us
    all_gather x1, waiting for transfers between devices, local(): dy_rows = lax.all_gather(recv_both[1], 'dp', axis=0, tiled=True)  59.4 us
    pallas_call x1, Pallas kernels, a2a_expert(): pl.pallas_call(functools.partial(a2a_expert_kernel, n), out_shape=jax.Sha...  26.9 us
    dot_general x1, matrix products, rows_backward_parts(): lax.dot_general(lhs, extended, (((0,), (0,)), ((), ())), preferred_elemen...  20.2 us
    unnamed x55, local copies, waits for them, and re-layouts  11.7 us
    pallas_call x1, Pallas kernels, gather_dp(): pl.pallas_call(functools.partial(gather_dp_kernel, n), out_shape=jax.Shap...  10.8 us
  transfers between devices with their start and end apart: 4, of which 3 were waited for; matrix products, arithmetic and copies ran while one was open for 15% of the time, Pallas kernels for 3%

profile of v7, /device:TPU:1, one launch (start us, length us, event | category | flops | bytes accessed | tf_op | source)
XLA Modules:
  0.0 420.9 jit_solution(11742495163426936392)
XLA Ops:
  7.2 0.7 convert_reduce_fusion
  8.0 0.1 copy.33
  8.1 0.2 reduce_window_sum.11
  8.3 0.7 select_reduce_fusion
  9.0 0.7 compare_select_fusion.3
  9.7 0.1 copy.36
  9.8 0.1 reshape.102
  10.0 0.8 copy.37
  10.8 0.1 reshape.105
  10.9 0.1 reshape.159
  11.1 0.1 reshape.151
  11.2 1.4 scatter_custom_fusion.1
  12.6 1.4 scatter_custom_fusion
  14.1 5.0 %gather_fusion.1 = f32[768]{0:T(1024)S(1)} fusion(f32[256]{0:T(256)S(1)} %reshape.105, s32[1024]{0:T(1024)S(1)} %get-tuple-element.37), kind=kCustom, calls=%fused_computation.1 | custom fusion | bytes 9216 | tf_op jit(solution)/shard_map/gather | solution.py:303
  19.2 2.7 gather_fusion.2
  21.9 2.7 gather_fusion
  24.6 0.2 fusion.23
  24.8 1.4 pad_maximum_fusion.src_ref
  26.2 26.9 %shard_map.180 = bf16[8,96,1024]{2,1,0:T(8,128)(2,1)} custom-call(bf16[8,96,1024]{2,1,0:T(8,128)(2,1)} %pad_maximum_fusion.src_ref), custom_call_target="tpu_custom_call" | custom-call | tf_op jit(solution)/shard_map/pallas_call | solution.py:253
  53.1 2.9 reshape.106
  56.0 0.9 copy.49
  56.9 1.2 copy.44
  58.2 1.2 copy.43
  59.5 0.6 reduce-scatter.4.cloned.1.call-start
  60.0 0.2 fusion.27
  60.2 4.4 %bitcast_dynamic-update-slice_fusion.1 = bf16[944,4096]{1,0:T(8,128)(2,1)} fusion(bf16[1,448,4096]{2,1,0:T(8,128)(2,1)} %param.17), kind=kLoop, calls=%fused_computation.21 | loop fusion | bytes 7340032
  64.7 2.2 bitcast_dynamic-update-slice_fusion
  66.9 0.7 fusion.31
  67.6 0.7 fusion.32
  68.2 0.7 broadcast_dynamic-update-slice_fusion
  68.9 79.2 %all-gather.5.cloned.1.call-done = bf16[1536,4096]{1,0:T(8,128)(2,1)} async-done(((bf16[96,4096]{1,0:T(8,128)(2,1)}), bf16[1536,4096]{1,0:T(8,128)(2,1)}) %all-gather.5.cloned.1.call-update) | async-done | bytes 12582928 | tf_op jit(solution)/shard_map/all_gather | solution.py:319
  148.1 8.1 %convolution_convert_fusion.6 = bf16[1536,16]{0,1:T(8,128)(2,1)S(1)} fusion(bf16[1536,4096]{1,0:T(8,128)(2,1)} %all-gather.5.cloned.1.call-done, bf16[1,16,4096]{2,1,0:T(8,128)(2,1)S(1)} %copy-done.15), kind=kOutput, calls=%fused_computation.47 | convolution fusion | flops 201351168 | bytes 12763136 | tf_op jit(solution)/shard_map/dot_general | solution.py:18
  156.2 8.0 %fusion.10 = f32[1536,448]{0,1:T(8,128)S(1)} fusion(bf16[1536,4096]{1,0:T(8,128)(2,1)S(1)} %copy-done.2, bf16[1,448,4096]{2,1,0:T(8,128)(2,1)} %param.17), kind=kOutput, calls=%fused_computation.22 | convolution fusion | flops 5637144576 | bytes 19005440 | tf_op jit(solution)/shard_map/dot_general | solution.py:18
  164.2 0.6 fusion.15
  164.8 3.3 convolution_convert_fusion.5
  168.1 6.1 %fusion.8 = f32[1536,448]{0,1:T(8,128)S(1)} fusion(bf16[1536,4096]{1,0:T(8,128)(2,1)S(1)} %copy-done.2, bf16[1,448,4096]{2,1,0:T(8,128)(2,1)S(1)} %copy-done.14), kind=kOutput, calls=%fused_computation.19 | convolution fusion | flops 5637144576 | bytes 19005440 | tf_op jit(solution)/shard_map/dot_general | solution.py:18
  174.2 3.9 multiply_convert_fusion.2
  178.1 1.6 copy-done.10
  179.6 0.9 convolution_convert_fusion.3
  180.5 59.4 %all-gather.3.cloned.1.call-done = bf16[1536,4096]{1,0:T(8,128)(2,1)} async-done(((bf16[96,4096]{1,0:T(8,128)(2,1)}), bf16[1536,4096]{1,0:T(8,128)(2,1)}) %all-gather.3.cloned.1.call-update) | async-done | bytes 12582928 | tf_op jit(solution)/shard_map/all_gather | solution.py:320
  239.9 8.1 %convolution_convert_fusion.4 = bf16[1536,16]{0,1:T(8,128)(2,1)S(1)} fusion(bf16[1536,4096]{1,0:T(8,128)(2,1)} %all-gather.3.cloned.1.call-done, bf16[1,4096,16]{1,2,0:T(8,128)(2,1)S(1)} %copy-done), kind=kOutput, calls=%fused_computation.45 | convolution fusion | flops 201351168 | bytes 12763136 | tf_op jit(solution)/shard_map/dot_general | solution.py:18
  248.1 8.3 %fusion.6 = f32[1536,448]{0,1:T(8,128)S(1)} fusion(bf16[1536,4096]{1,0:T(8,128)(2,1)S(1)} %copy-done.3, bf16[1,448,4096]{2,1,0:T(8,128)(2,1)} %param.19), kind=kOutput, calls=%fused_computation.16 | convolution fusion | flops 5637144576 | bytes 19005440 | tf_op jit(solution)/shard_map/dot_general | solution.py:18
  256.4 1.3 multiply_convert_fusion.1
  257.7 0.3 convolution_convert_fusion.2
  258.0 0.3 convolution_convert_fusion.1
  258.4 20.2 %convolution_convert_fusion = bf16[1536,4224]{1,0:T(8,128)(2,1)} fusion(bf16[944,128]{1,0:T(8,128)(2,1)S(1)} %fusion.27, bf16[944,4096]{1,0:T(8,128)(2,1)} %broadcast_dynamic-update-slice_fusion, bf16[48,1536]{1,0:T(8,128)(2,1)S(1)} %maximum_bitcast_fusion, bf16[448,1536]{1,0:T(8,128)(2,1)S(1)} %get-tuple-element.26, bf16[448,1536]{1,0:T(8,128)(2,1)S(1)} %get-tuple-element.25), kind=kOutput, calls=%fused_computation.6 | convolution fusion | flops 12280602624 | bytes 23851008 | tf_op jit(solution)/shard_map/dot_general | solution.py:177
  278.6 0.1 copy.41
  278.7 0.1 reshape.141
  278.9 2.6 fusion.24
  281.5 1.1 fusion.25
  282.6 1.1 fusion.26
  283.7 90.3 %reduce-scatter.4.cloned.1.call-done = bf16[1,96,4224]{2,1,0:T(8,128)(2,1)} async-done(((bf16[16,96,4224]{2,1,0:T(8,128)(2,1)}), bf16[1,96,4224]{2,1,0:T(8,128)(2,1)}) %reduce-scatter.4.cloned.1.call-update) | async-done | bytes 811024
  374.0 1.3 slice.41.src_ref
  375.3 1.2 slice.40
  376.5 1.0 copy.50
  377.5 5.6 %all-to-all-start = ((bf16[96,8,512]{2,0,1:T(8,128)(2,1)}), bf16[96,8,512]{2,0,1:T(8,128)(2,1)S(1)}, u32[]{:S(2)}, u32[]{:S(2)}) async-start(bf16[96,8,512]{2,0,1:T(8,128)(2,1)} %bitcast.106), calls=%async_computation | async-start | bytes 1572864 | tf_op jit(solution)/shard_map/all_to_all | solution.py:334
  383.1 10.8 %shard_map.181 = bf16[16,96,128]{2,1,0:T(8,128)(2,1)} custom-call(bf16[96,128]{1,0:T(8,128)(2,1)} %slice.41.src_ref), custom_call_target="tpu_custom_call" | custom-call | tf_op jit(solution)/shard_map/pallas_call | solution.py:215
  394.0 7.3 %fusion.5 = f32[1,4096,16]{1,2,0:T(8,128)} fusion(bf16[1536,4096]{1,0:T(8,128)(2,1)} %all-gather.3.cloned.1.call-done, bf16[1536,128]{1,0:T(8,128)(2,1)} %bitcast.113), kind=kOutput, calls=%fused_computation.15 | convolution fusion | flops 201392128 | bytes 13238272 | tf_op jit(solution)/shard_map/dot_general | solution.py:18
  401.3 7.3 %fusion.3 = f32[1,16,4096]{2,1,0:T(8,128)} fusion(bf16[1536,4096]{1,0:T(8,128)(2,1)} %all-gather.5.cloned.1.call-done, bf16[1536,128]{1,0:T(8,128)(2,1)S(1)} %bitcast.114), kind=kOutput, calls=%fused_computation.11 | convolution fusion | flops 201392128 | bytes 13238272 | tf_op jit(solution)/shard_map/dot_general | solution.py:18
  408.5 2.5 fusion.4
  411.0 0.5 copy.48
  411.5 1.0 gather_fusion.3
  412.4 0.3 reshape.144
  412.8 1.3 reduce_sum.29
  (71 shorter events, 0.7 us)
Async XLA Ops:
  7.2 232.7 %copy-start = (bf16[1,4096,16]{1,2,0:T(8,128)(2,1)S(1)}, bf16[1,4096,16]{1,2,0:T(8,128)(2,1)}, u32[]{:S(2)}) copy-start(bf16[1,4096,16]{1,2,0:T(8,128)(2,1)} %param.25) | copy-start | bytes 393220
  7.2 12.0 %copy-start.17 = (bf16[128,512]{1,0:T(8,128)(2,1)S(1)}, bf16[128,512]{1,0:T(8,128)(2,1)}, u32[]{:S(2)}) copy-start(bf16[128,512]{1,0:T(8,128)(2,1)} %param.13) | copy-start | bytes 393220
  7.2 140.9 %all-gather.5.cloned.1.call-start = ((), (), s32[]{:S(2)}) async-start(), calls=%async_computation.3 | async-start | bytes 13369344 | tf_op jit(solution)/shard_map/all_gather | solution.py:319
  8.1 11.1 %copy-start.18 = (bf16[128,512]{1,0:T(8,128)(2,1)S(1)}, bf16[128,512]{1,0:T(8,128)(2,1)}, u32[]{:S(2)}) copy-start(bf16[128,512]{1,0:T(8,128)(2,1)} %param.14) | copy-start | bytes 393220
  58.1 181.8 %all-gather.3.cloned.1.call-start = ((), (), s32[]{:S(2)}) async-start(), calls=%async_computation.2 | async-start | bytes 13369344 | tf_op jit(solution)/shard_map/all_gather | solution.py:320
  59.5 314.5 %reduce-scatter.4.cloned.1.call-start = ((), (), s32[]{:S(2)}) async-start(), calls=%async_computation.4 | async-start | bytes 13787136
  60.2 4.4 %copy-start.13 = (bf16[1,448,4096]{2,1,0:T(8,128)(2,1)S(1)}, bf16[1,448,4096]{2,1,0:T(8,128)(2,1)}, u32[]{:S(2)}) copy-start(bf16[1,448,4096]{2,1,0:T(8,128)(2,1)} %param.18) | copy-start | bytes 11010052
  64.7 2.2 copy-start.15
  64.7 2.9 copy-start.16
  148.0 8.2 %copy-start.2 = (bf16[1536,4096]{1,0:T(8,128)(2,1)S(1)}, bf16[1536,4096]{1,0:T(8,128)(2,1)}, u32[]{:S(2)}) copy-start(bf16[1536,4096]{1,0:T(8,128)(2,1)} %all-gather.5.cloned.1.call-done) | copy-start | bytes 37748740
  156.2 8.0 %copy-start.19 = (bf16[1,448,16]{1,2,0:T(8,128)(2,1)S(1)}, bf16[1,448,16]{1,2,0:T(8,128)(2,1)}, u32[]{:S(2)}) copy-start(bf16[1,448,16]{1,2,0:T(8,128)(2,1)} %param.21) | copy-start | bytes 43012
  164.7 3.4 copy-start.14
  168.1 6.1 %copy-start.20 = (bf16[1,448,16]{1,2,0:T(8,128)(2,1)S(1)}, bf16[1,448,16]{1,2,0:T(8,128)(2,1)}, u32[]{:S(2)}) copy-start(bf16[1,448,16]{1,2,0:T(8,128)(2,1)} %param.23) | copy-start | bytes 43012
  174.2 5.4 %copy-start.21 = (bf16[1,16,448]{2,1,0:T(8,128)(2,1)S(1)}, bf16[1,16,448]{2,1,0:T(8,128)(2,1)}, u32[]{:S(2)}) copy-start(bf16[1,16,448]{2,1,0:T(8,128)(2,1)} %param.24) | copy-start | bytes 43012
  178.1 1.6 copy-start.10
  239.9 8.2 %copy-start.3 = (bf16[1536,4096]{1,0:T(8,128)(2,1)S(1)}, bf16[1536,4096]{1,0:T(8,128)(2,1)}, u32[]{:S(2)}) copy-start(bf16[1536,4096]{1,0:T(8,128)(2,1)} %all-gather.3.cloned.1.call-done) | copy-start | bytes 37748740
  248.1 8.3 %copy-start.8 = (f32[448,1536]{1,0:T(8,128)S(1)}, f32[448,1536]{1,0:T(8,128)}, u32[]{:S(2)}) copy-start(f32[448,1536]{1,0:T(8,128)} %get-tuple-element.20) | copy-start | bytes 8257540
  248.1 8.3 %copy-start.9 = (f32[448,1536]{1,0:T(8,128)S(1)}, f32[448,1536]{1,0:T(8,128)}, u32[]{:S(2)}) copy-start(f32[448,1536]{1,0:T(8,128)} %get-tuple-element.18) | copy-start | bytes 8257540
  248.1 8.3 %copy-start.11 = (f32[448,1536]{1,0:T(8,128)S(1)}, f32[448,1536]{1,0:T(8,128)}, u32[]{:S(2)}) copy-start(f32[448,1536]{1,0:T(8,128)} %copy-done.10) | copy-start | bytes 8257540
  257.7 20.9 %copy-start.4 = (bf16[448,1536]{1,0:T(8,128)(2,1)}, bf16[448,1536]{1,0:T(8,128)(2,1)S(1)}, u32[]{:S(2)}) copy-start(bf16[448,1536]{1,0:T(8,128)(2,1)S(1)} %get-tuple-element.25) | copy-start | bytes 4128772
  257.7 20.8 %copy-start.6 = (bf16[448,1536]{1,0:T(8,128)(2,1)}, bf16[448,1536]{1,0:T(8,128)(2,1)S(1)}, u32[]{:S(2)}) copy-start(bf16[448,1536]{1,0:T(8,128)(2,1)S(1)} %get-tuple-element.26) | copy-start | bytes 4128772
  278.6 2.9 copy-start.7
  278.6 4.0 copy-start.5
  377.5 33.5 %all-to-all-start = ((bf16[96,8,512]{2,0,1:T(8,128)(2,1)}), bf16[96,8,512]{2,0,1:T(8,128)(2,1)S(1)}, u32[]{:S(2)}, u32[]{:S(2)}) async-start(bf16[96,8,512]{2,0,1:T(8,128)(2,1)} %bitcast.106), calls=%async_computation | async-start | bytes 1572864 | tf_op jit(solution)/shard_map/all_to_all | solution.py:334
  393.9 7.3 %copy-start.12 = (bf16[16,96,128]{2,1,0:T(8,128)(2,1)S(1)}, bf16[16,96,128]{2,1,0:T(8,128)(2,1)}, u32[]{:S(2)}) copy-start(bf16[16,96,128]{2,1,0:T(8,128)(2,1)} %shard_map.181) | copy-start | bytes 1179652
  393.9 14.6 %slice-start = ((s8[12582912]{0:T(1024)(128)(4,1)}), s8[4194304]{0:T(1024)(128)(4,1)S(1)}, s32[]{:S(2)}) async-start(s8[12582912]{0:T(1024)(128)(4,1)} %bitcast.109), calls=%async_computation.5 | async-start | bytes 8388608
  393.9 14.6 %slice-start.1 = ((s8[12582912]{0:T(1024)(128)(4,1)}), s8[4194304]{0:T(1024)(128)(4,1)S(1)}, s32[]{:S(2)}) async-start(s8[12582912]{0:T(1024)(128)(4,1)} %bitcast.109), calls=%async_computation.6 | async-start | bytes 8388608
  401.3 7.3 %slice-start.2 = ((s8[12582912]{0:T(1024)(128)(4,1)}), s8[4194304]{0:T(1024)(128)(4,1)S(1)}, s32[]{:S(2)}) async-start(s8[12582912]{0:T(1024)(128)(4,1)} %bitcast.109), calls=%async_computation.7 | async-start | bytes 8388608
  411.5 2.6 copy-start.1
Sparse Core Ops, SparseCore 0:
  58.2 89.7 all-gather.4
  150.2 89.6 all-gather.2
  278.7 95.1 reduce-scatter.3

commit v8 on v7

--- a/solution.py
+++ b/solution.py
@@ -222,7 +222,7 @@
     )(block)
 
 
-def a2a_expert_kernel(n, src_ref, out_ref, send_sem, recv_sem):
+def a2a_expert_kernel(n, width, x_ref, dy_ref, x_out, dy_out, send_sem, recv_sem):
     me = lax.axis_index("expert")
     row = lax.axis_index("dp")
     barrier = pltpu.get_barrier_semaphore()
@@ -230,35 +230,38 @@
         peer = lax.rem(me + k, n)
         pl.semaphore_signal(barrier, inc=1, device_id=(row, peer), device_id_type=MESH)
     pl.semaphore_wait(barrier, n - 1)
+    mine = pl.ds(pl.multiple_of(me * width, width), width)
     copies = []
     for k in range(1, n):
         peer = lax.rem(me + k, n)
-        cp = pltpu.make_async_remote_copy(
-            src_ref.at[peer],
-            out_ref.at[me],
-            send_sem.at[k],
-            recv_sem.at[k],
-            device_id=(row, peer),
-            device_id_type=MESH,
-        )
-        cp.start()
-        copies.append(cp)
-    out_ref[me] = src_ref[me]
+        for which, (src_ref, out_ref) in enumerate(((x_ref, x_out), (dy_ref, dy_out))):
+            cp = pltpu.make_async_remote_copy(
+                src_ref.at[peer],
+                out_ref.at[:, mine],
+                send_sem.at[which, k],
+                recv_sem.at[which, k],
+                device_id=(row, peer),
+                device_id_type=MESH,
+            )
+            cp.start()
+            copies.append(cp)
+    x_out[:, mine] = x_ref[me]
+    dy_out[:, mine] = dy_ref[me]
     for cp in copies:
         cp.wait()
 
 
-def a2a_expert(blocks):
-    n = blocks.shape[0]
+def a2a_expert(send_x, send_dy):
+    n, rows, width = send_x.shape
+    out = jax.ShapeDtypeStruct((rows, n * width), send_x.dtype)
     return pl.pallas_call(
-        functools.partial(a2a_expert_kernel, n),
-        out_shape=jax.ShapeDtypeStruct(blocks.shape, blocks.dtype),
-        in_specs=[pl.BlockSpec(memory_space=pltpu.VMEM)],
-        out_specs=pl.BlockSpec(memory_space=pltpu.VMEM),
-        scratch_shapes=[pltpu.SemaphoreType.DMA((n,)), pltpu.SemaphoreType.DMA((n,))],
+        functools.partial(a2a_expert_kernel, n, width),
+        out_shape=(out, out),
+        in_specs=[pl.BlockSpec(memory_space=pltpu.VMEM)] * 2,
+        out_specs=(pl.BlockSpec(memory_space=pltpu.VMEM),) * 2,
+        scratch_shapes=[pltpu.SemaphoreType.DMA((2, n)), pltpu.SemaphoreType.DMA((2, n))],
         compiler_params=pltpu.CompilerParams(collective_id=1, has_side_effects=True),
-    )(blocks)
-
+    )(send_x, send_dy)
 
 def local(
     tokens,
@@ -311,23 +314,18 @@
         .astype(jnp.bfloat16)
         .reshape(experts, capacity, feat_local)
     )
-    send_both = jnp.concatenate([send_x, send_dy], axis=2)
-    recv_both = a2a_expert(send_both)
-    recv_both = recv_both.reshape(experts, capacity, 2, feat_local).transpose(2, 1, 0, 3)
-    recv_both = recv_both.reshape(2, capacity, complete_width)
-
-    x_rows = lax.all_gather(recv_both[0], "dp", axis=0, tiled=True)
-    dy_rows = lax.all_gather(recv_both[1], "dp", axis=0, tiled=True)
+    x_block, dy_block = a2a_expert(send_x, send_dy)
+    x_rows = lax.all_gather(x_block, "dp", axis=0, tiled=True)
+    dy_rows = lax.all_gather(dy_block, "dp", axis=0, tiled=True)
     rows_out, parts, owned_total = rows_backward_parts(x_rows, dy_rows, params)
     packed = rows_out.reshape(shards, capacity, complete_width + PART_COLS)
     summed_packed = lax.psum_scatter(packed, "dp", scatter_dimension=0, tiled=True)[0]
     summed = summed_packed[:, :complete_width]
     parts_mine = summed_packed[:, complete_width:]
     parts_sum = gather_dp(parts_mine, shards).reshape(shards * capacity, PART_COLS)
-    grad_a_gate = ADAPTER_SCALE * contract_pair(parts_sum[:, :adapter_rank], x_rows, 0, 0)
-    grad_a_up = ADAPTER_SCALE * contract_pair(
-        parts_sum[:, adapter_rank:2 * adapter_rank], x_rows, 0, 0
-    )
+    grad_a_pair = ADAPTER_SCALE * contract_pair(parts_sum[:, :2 * adapter_rank], x_rows, 0, 0)
+    grad_a_gate = grad_a_pair[:adapter_rank]
+    grad_a_up = grad_a_pair[adapter_rank:]
     grad_b_down = ADAPTER_SCALE * contract_pair(
         dy_rows, parts_sum[:, 2 * adapter_rank:3 * adapter_rank], 0, 0
     )

time: 427 us -> 419 us (0.981)
  local copies, waits for them, and re-layouts: 35.7 us -> 30.9 us
    dot_general x18 -> x17, matrix products: 70.8 us -> 67.9 us  [contract_pair(): lax.dot_general(left, right, (((left_axis,), (right_axis,)), ((), ())), p...]
    unnamed x55 -> x47, local copies, waits for them, and re-layouts: 11.7 us -> 9.2 us
  transfers between devices with their start and end apart: 4 -> 4, of which waited for: 3 -> 3; matrix products, arithmetic and copies ran while one was open for 15% -> 14% of each run, Pallas kernels for 3% -> 3%
where the time goes in v8:
time: 419 us; the launch traced here: 414 us
  waiting for transfers between devices  230 us (55%)
  matrix products  88.1 us (21%)
  Pallas kernels  37.9 us (9%)
  local copies, waits for them, and re-layouts  30.9 us (7%)
  between operations  14.4 us (3%)
  other arithmetic  6.35 us (2%)
  starting transfers between devices  6.21 us (1%)
    unnamed x4, waiting for transfers between devices  91.1 us
    all_gather x1, waiting for transfers between devices, local(): x_rows = lax.all_gather(x_block, 'dp', axis=0, tiled=True)  79.8 us
    dot_general x17, matrix products, contract_pair(): lax.dot_general(left, right, (((left_axis,), (right_axis,)), ((), ())), p...  67.9 us
    all_gather x1, waiting for transfers between devices, local(): dy_rows = lax.all_gather(dy_block, 'dp', axis=0, tiled=True)  59.4 us
    pallas_call x1, Pallas kernels, a2a_expert(): pl.pallas_call(functools.partial(a2a_expert_kernel, n, width), out_shape=...  27 us
    dot_general x1, matrix products, rows_backward_parts(): lax.dot_general(lhs, extended, (((0,), (0,)), ((), ())), preferred_elemen...  20.2 us
    pallas_call x1, Pallas kernels, gather_dp(): pl.pallas_call(functools.partial(gather_dp_kernel, n), out_shape=jax.Shap...  10.9 us
    unnamed x47, local copies, waits for them, and re-layouts  9.2 us
  transfers between devices with their start and end apart: 4, of which 3 were waited for; matrix products, arithmetic and copies ran while one was open for 14% of the time, Pallas kernels for 3%

profile of v8, /device:TPU:1, one launch (start us, length us, event | category | flops | bytes accessed | tf_op | source)
XLA Modules:
  0.0 414.0 jit_solution(4932780711027523092)
XLA Ops:
  7.2 0.7 convert_reduce_fusion
  8.0 0.1 copy.31
  8.1 0.2 reduce_window_sum.11
  8.3 0.7 select_reduce_fusion
  9.0 0.7 compare_select_fusion.3
  9.7 0.1 copy.34
  9.8 0.1 reshape.94
  10.0 0.8 copy.35
  10.8 0.1 reshape.97
  10.9 0.1 reshape.150
  11.1 0.1 reshape.142
  11.2 1.4 scatter_custom_fusion.1
  12.6 1.4 scatter_custom_fusion
  14.1 5.0 %gather_fusion.1 = f32[768]{0:T(1024)S(1)} fusion(f32[256]{0:T(256)S(1)} %reshape.97, s32[1024]{0:T(1024)S(1)} %get-tuple-element.41), kind=kCustom, calls=%fused_computation.1 | custom fusion | bytes 9216 | tf_op jit(solution)/shard_map/gather | solution.py:306
  19.1 0.1 mul.106
  19.2 2.7 gather_fusion.2
  21.9 3.3 gather_fusion
  25.2 1.1 fusion.21.dy_ref
  26.4 27.0 %shard_map.180 = (bf16[96,4096]{1,0:T(8,128)(2,1)}, bf16[96,4096]{1,0:T(8,128)(2,1)}) custom-call(bf16[8,96,512]{2,1,0:T(8,128)(2,1)} %bitcast.103, bf16[8,96,512]{2,1,0:T(8,128)(2,1)} %fusion.21.dy_ref), custom_call_target="tpu_custom_call" | custom-call | tf_op jit(solution)/shard_map/pallas_call | solution.py:257
  53.4 0.0 all-gather.3.cloned.1.call-start
  53.5 0.7 all-gather.3.cloned.1.call-update
  54.2 0.6 reduce-scatter.4.cloned.1.call-start
  54.8 0.2 fusion.25
  55.0 4.4 %bitcast_dynamic-update-slice_fusion.1 = bf16[944,4096]{1,0:T(8,128)(2,1)} fusion(bf16[1,448,4096]{2,1,0:T(8,128)(2,1)} %param.17), kind=kLoop, calls=%fused_computation.18 | loop fusion | bytes 7340032
  59.4 2.2 bitcast_dynamic-update-slice_fusion
  61.6 0.7 fusion.28
  62.2 0.7 fusion.29
  62.9 0.7 broadcast_dynamic-update-slice_fusion
  63.6 79.8 %all-gather.5.cloned.1.call-done = bf16[1536,4096]{1,0:T(8,128)(2,1)} async-done(((bf16[96,4096]{1,0:T(8,128)(2,1)}), bf16[1536,4096]{1,0:T(8,128)(2,1)}) %all-gather.5.cloned.1.call-update) | async-done | bytes 12582928 | tf_op jit(solution)/shard_map/all_gather | solution.py:318
  143.3 8.1 %convolution_convert_fusion.6 = bf16[1536,16]{0,1:T(8,128)(2,1)S(1)} fusion(bf16[1536,4096]{1,0:T(8,128)(2,1)} %all-gather.5.cloned.1.call-done, bf16[1,16,4096]{2,1,0:T(8,128)(2,1)S(1)} %copy-done.15), kind=kOutput, calls=%fused_computation.44 | convolution fusion | flops 201351168 | bytes 12763136 | tf_op jit(solution)/shard_map/dot_general | solution.py:18
  151.4 0.1 copy-done.2
  151.5 8.0 %fusion.8 = f32[1536,448]{0,1:T(8,128)S(1)} fusion(bf16[1536,4096]{1,0:T(8,128)(2,1)S(1)} %copy-done.2, bf16[1,448,4096]{2,1,0:T(8,128)(2,1)} %param.17), kind=kOutput, calls=%fused_computation.19 | convolution fusion | flops 5637144576 | bytes 19005440 | tf_op jit(solution)/shard_map/dot_general | solution.py:18
  159.5 0.6 fusion.13
  160.1 3.3 convolution_convert_fusion.5
  163.4 6.1 %fusion.6 = f32[1536,448]{0,1:T(8,128)S(1)} fusion(bf16[1536,4096]{1,0:T(8,128)(2,1)S(1)} %copy-done.2, bf16[1,448,4096]{2,1,0:T(8,128)(2,1)S(1)} %copy-done.14), kind=kOutput, calls=%fused_computation.16 | convolution fusion | flops 5637144576 | bytes 19005440 | tf_op jit(solution)/shard_map/dot_general | solution.py:18
  169.5 3.9 multiply_convert_fusion.2
  173.4 1.5 copy-done.10
  175.0 0.9 convolution_convert_fusion.3
  175.8 59.4 %all-gather.3.cloned.1.call-done = bf16[1536,4096]{1,0:T(8,128)(2,1)} async-done(((bf16[96,4096]{1,0:T(8,128)(2,1)}), bf16[1536,4096]{1,0:T(8,128)(2,1)}) %all-gather.3.cloned.1.call-update) | async-done | bytes 12582928 | tf_op jit(solution)/shard_map/all_gather | solution.py:319
  235.2 8.1 %convolution_convert_fusion.4 = bf16[1536,16]{0,1:T(8,128)(2,1)S(1)} fusion(bf16[1536,4096]{1,0:T(8,128)(2,1)} %all-gather.3.cloned.1.call-done, bf16[1,4096,16]{1,2,0:T(8,128)(2,1)S(1)} %copy-done), kind=kOutput, calls=%fused_computation.42 | convolution fusion | flops 201351168 | bytes 12763136 | tf_op jit(solution)/shard_map/dot_general | solution.py:18
  243.3 0.1 copy-done.3
  243.4 8.3 %fusion.4 = f32[1536,448]{0,1:T(8,128)S(1)} fusion(bf16[1536,4096]{1,0:T(8,128)(2,1)S(1)} %copy-done.3, bf16[1,448,4096]{2,1,0:T(8,128)(2,1)} %param.19), kind=kOutput, calls=%fused_computation.13 | convolution fusion | flops 5637144576 | bytes 19005440 | tf_op jit(solution)/shard_map/dot_general | solution.py:18
  251.7 1.3 multiply_convert_fusion.1
  253.0 0.3 convolution_convert_fusion.2
  253.3 0.3 convolution_convert_fusion.1
  253.7 20.2 %convolution_convert_fusion = bf16[1536,4224]{1,0:T(8,128)(2,1)} fusion(bf16[944,128]{1,0:T(8,128)(2,1)S(1)} %fusion.25, bf16[944,4096]{1,0:T(8,128)(2,1)} %broadcast_dynamic-update-slice_fusion, bf16[48,1536]{1,0:T(8,128)(2,1)S(1)} %maximum_bitcast_fusion, bf16[448,1536]{1,0:T(8,128)(2,1)S(1)} %get-tuple-element.30, bf16[448,1536]{1,0:T(8,128)(2,1)S(1)} %get-tuple-element.29), kind=kOutput, calls=%fused_computation.6 | convolution fusion | flops 12280602624 | bytes 23851008 | tf_op jit(solution)/shard_map/dot_general | solution.py:177
  273.9 0.1 copy.38
  274.0 0.1 reshape.132
  274.2 2.6 fusion.22
  276.8 1.1 fusion.23
  277.9 1.1 fusion.24
  279.0 90.3 %reduce-scatter.4.cloned.1.call-done = bf16[1,96,4224]{2,1,0:T(8,128)(2,1)} async-done(((bf16[16,96,4224]{2,1,0:T(8,128)(2,1)}), bf16[1,96,4224]{2,1,0:T(8,128)(2,1)}) %reduce-scatter.4.cloned.1.call-update) | async-done | bytes 811024
  369.3 1.3 slice.33.src_ref
  370.7 1.2 slice.32
  371.8 1.0 copy.43
  372.8 5.6 %all-to-all-start = ((bf16[96,8,512]{2,0,1:T(8,128)(2,1)}), bf16[96,8,512]{2,0,1:T(8,128)(2,1)S(1)}, u32[]{:S(2)}, u32[]{:S(2)}) async-start(bf16[96,8,512]{2,0,1:T(8,128)(2,1)} %bitcast.96), calls=%async_computation | async-start | bytes 1572864 | tf_op jit(solution)/shard_map/all_to_all | solution.py:332
  378.4 10.9 %shard_map.181 = bf16[16,96,128]{2,1,0:T(8,128)(2,1)} custom-call(bf16[96,128]{1,0:T(8,128)(2,1)} %slice.33.src_ref), custom_call_target="tpu_custom_call" | custom-call | tf_op jit(solution)/shard_map/pallas_call | solution.py:215
  389.2 7.2 %fusion.3 = f32[1,4096,16]{1,2,0:T(8,128)} fusion(bf16[1536,4096]{1,0:T(8,128)(2,1)} %all-gather.3.cloned.1.call-done, bf16[1536,128]{1,0:T(8,128)(2,1)} %bitcast.101), kind=kOutput, calls=%fused_computation.12 | convolution fusion | flops 201392128 | bytes 13238272 | tf_op jit(solution)/shard_map/dot_general | solution.py:18
  396.4 6.9 %convolution_multiply_fusion = f32[32,4096]{1,0:T(8,128)S(1)} fusion(bf16[1536,4096]{1,0:T(8,128)(2,1)} %all-gather.5.cloned.1.call-done, bf16[1536,128]{1,0:T(8,128)(2,1)S(1)} %bitcast.102), kind=kOutput, calls=%fused_computation.10 | convolution fusion | flops 402784256 | bytes 13500416 | tf_op jit(solution)/shard_map/dot_general | solution.py:18
  403.3 0.8 slice_bitcast_fusion
  404.2 0.5 copy.42
  404.6 1.0 gather_fusion.3
  405.6 0.3 reshape.135
  405.9 1.3 reduce_sum.29
  (58 shorter events, 0.3 us)
Async XLA Ops:
  7.2 228.0 %copy-start = (bf16[1,4096,16]{1,2,0:T(8,128)(2,1)S(1)}, bf16[1,4096,16]{1,2,0:T(8,128)(2,1)}, u32[]{:S(2)}) copy-start(bf16[1,4096,16]{1,2,0:T(8,128)(2,1)} %param.25) | copy-start | bytes 393220
  7.2 12.0 %copy-start.17 = (bf16[128,512]{1,0:T(8,128)(2,1)S(1)}, bf16[128,512]{1,0:T(8,128)(2,1)}, u32[]{:S(2)}) copy-start(bf16[128,512]{1,0:T(8,128)(2,1)} %param.13) | copy-start | bytes 393220
  7.2 136.1 %all-gather.5.cloned.1.call-start = ((), (), s32[]{:S(2)}) async-start(), calls=%async_computation.3 | async-start | bytes 13369344 | tf_op jit(solution)/shard_map/all_gather | solution.py:318
  8.1 11.1 %copy-start.18 = (bf16[128,512]{1,0:T(8,128)(2,1)S(1)}, bf16[128,512]{1,0:T(8,128)(2,1)}, u32[]{:S(2)}) copy-start(bf16[128,512]{1,0:T(8,128)(2,1)} %param.14) | copy-start | bytes 393220
  53.4 181.8 %all-gather.3.cloned.1.call-start = ((), (), s32[]{:S(2)}) async-start(), calls=%async_computation.2 | async-start | bytes 13369344 | tf_op jit(solution)/shard_map/all_gather | solution.py:319
  54.2 315.1 %reduce-scatter.4.cloned.1.call-start = ((), (), s32[]{:S(2)}) async-start(), calls=%async_computation.4 | async-start | bytes 13787136
  54.9 4.4 %copy-start.13 = (bf16[1,448,4096]{2,1,0:T(8,128)(2,1)S(1)}, bf16[1,448,4096]{2,1,0:T(8,128)(2,1)}, u32[]{:S(2)}) copy-start(bf16[1,448,4096]{2,1,0:T(8,128)(2,1)} %param.18) | copy-start | bytes 11010052
  59.4 2.2 copy-start.15
  59.4 2.9 copy-start.16
  143.3 8.2 %copy-start.2 = (bf16[1536,4096]{1,0:T(8,128)(2,1)S(1)}, bf16[1536,4096]{1,0:T(8,128)(2,1)}, u32[]{:S(2)}) copy-start(bf16[1536,4096]{1,0:T(8,128)(2,1)} %all-gather.5.cloned.1.call-done) | copy-start | bytes 37748740
  151.5 8.0 %copy-start.19 = (bf16[1,448,16]{1,2,0:T(8,128)(2,1)S(1)}, bf16[1,448,16]{1,2,0:T(8,128)(2,1)}, u32[]{:S(2)}) copy-start(bf16[1,448,16]{1,2,0:T(8,128)(2,1)} %param.21) | copy-start | bytes 43012
  160.0 3.4 copy-start.14
  163.4 6.1 %copy-start.20 = (bf16[1,448,16]{1,2,0:T(8,128)(2,1)S(1)}, bf16[1,448,16]{1,2,0:T(8,128)(2,1)}, u32[]{:S(2)}) copy-start(bf16[1,448,16]{1,2,0:T(8,128)(2,1)} %param.23) | copy-start | bytes 43012
  169.5 5.4 %copy-start.21 = (bf16[1,16,448]{2,1,0:T(8,128)(2,1)S(1)}, bf16[1,16,448]{2,1,0:T(8,128)(2,1)}, u32[]{:S(2)}) copy-start(bf16[1,16,448]{2,1,0:T(8,128)(2,1)} %param.24) | copy-start | bytes 43012
  173.4 1.5 copy-start.10
  235.2 8.2 %copy-start.3 = (bf16[1536,4096]{1,0:T(8,128)(2,1)S(1)}, bf16[1536,4096]{1,0:T(8,128)(2,1)}, u32[]{:S(2)}) copy-start(bf16[1536,4096]{1,0:T(8,128)(2,1)} %all-gather.3.cloned.1.call-done) | copy-start | bytes 37748740
  243.4 8.3 %copy-start.8 = (f32[448,1536]{1,0:T(8,128)S(1)}, f32[448,1536]{1,0:T(8,128)}, u32[]{:S(2)}) copy-start(f32[448,1536]{1,0:T(8,128)} %get-tuple-element.24) | copy-start | bytes 8257540
  243.4 8.3 %copy-start.9 = (f32[448,1536]{1,0:T(8,128)S(1)}, f32[448,1536]{1,0:T(8,128)}, u32[]{:S(2)}) copy-start(f32[448,1536]{1,0:T(8,128)} %get-tuple-element.22) | copy-start | bytes 8257540
  243.4 8.3 %copy-start.11 = (f32[448,1536]{1,0:T(8,128)S(1)}, f32[448,1536]{1,0:T(8,128)}, u32[]{:S(2)}) copy-start(f32[448,1536]{1,0:T(8,128)} %copy-done.10) | copy-start | bytes 8257540
  253.0 20.8 %copy-start.4 = (bf16[448,1536]{1,0:T(8,128)(2,1)}, bf16[448,1536]{1,0:T(8,128)(2,1)S(1)}, u32[]{:S(2)}) copy-start(bf16[448,1536]{1,0:T(8,128)(2,1)S(1)} %get-tuple-element.29) | copy-start | bytes 4128772
  253.0 20.8 %copy-start.6 = (bf16[448,1536]{1,0:T(8,128)(2,1)}, bf16[448,1536]{1,0:T(8,128)(2,1)S(1)}, u32[]{:S(2)}) copy-start(bf16[448,1536]{1,0:T(8,128)(2,1)S(1)} %get-tuple-element.30) | copy-start | bytes 4128772
  273.8 2.9 copy-start.7
  273.9 4.0 copy-start.5
  372.8 31.4 %all-to-all-start = ((bf16[96,8,512]{2,0,1:T(8,128)(2,1)}), bf16[96,8,512]{2,0,1:T(8,128)(2,1)S(1)}, u32[]{:S(2)}, u32[]{:S(2)}) async-start(bf16[96,8,512]{2,0,1:T(8,128)(2,1)} %bitcast.96), calls=%async_computation | async-start | bytes 1572864 | tf_op jit(solution)/shard_map/all_to_all | solution.py:332
  389.2 7.2 %copy-start.12 = (bf16[16,96,128]{2,1,0:T(8,128)(2,1)S(1)}, bf16[16,96,128]{2,1,0:T(8,128)(2,1)}, u32[]{:S(2)}) copy-start(bf16[16,96,128]{2,1,0:T(8,128)(2,1)} %shard_map.181) | copy-start | bytes 1179652
  404.6 2.6 copy-start.1
Sparse Core Ops, SparseCore 0:
  53.5 89.7 all-gather.4
  145.5 89.6 all-gather.2
  274.0 95.2 reduce-scatter.3

commit v9 on v7

--- a/solution.py
+++ b/solution.py
@@ -222,7 +222,7 @@
     )(block)
 
 
-def a2a_expert_kernel(n, src_ref, out_ref, send_sem, recv_sem):
+def a2a_expert_kernel(n, width, src_ref, out_ref, send_sem, recv_sem):
     me = lax.axis_index("expert")
     row = lax.axis_index("dp")
     barrier = pltpu.get_barrier_semaphore()
@@ -230,12 +230,13 @@
         peer = lax.rem(me + k, n)
         pl.semaphore_signal(barrier, inc=1, device_id=(row, peer), device_id_type=MESH)
     pl.semaphore_wait(barrier, n - 1)
+    mine = pl.ds(pl.multiple_of(me * width, width), width)
     copies = []
     for k in range(1, n):
         peer = lax.rem(me + k, n)
         cp = pltpu.make_async_remote_copy(
             src_ref.at[peer],
-            out_ref.at[me],
+            out_ref.at[:, mine],
             send_sem.at[k],
             recv_sem.at[k],
             device_id=(row, peer),
@@ -243,22 +244,21 @@
         )
         cp.start()
         copies.append(cp)
-    out_ref[me] = src_ref[me]
+    out_ref[:, mine] = src_ref[me]
     for cp in copies:
         cp.wait()
 
 
-def a2a_expert(blocks):
-    n = blocks.shape[0]
+def a2a_expert(send, exchange_id):
+    n, rows, width = send.shape
     return pl.pallas_call(
-        functools.partial(a2a_expert_kernel, n),
-        out_shape=jax.ShapeDtypeStruct(blocks.shape, blocks.dtype),
+        functools.partial(a2a_expert_kernel, n, width),
+        out_shape=jax.ShapeDtypeStruct((rows, n * width), send.dtype),
         in_specs=[pl.BlockSpec(memory_space=pltpu.VMEM)],
         out_specs=pl.BlockSpec(memory_space=pltpu.VMEM),
         scratch_shapes=[pltpu.SemaphoreType.DMA((n,)), pltpu.SemaphoreType.DMA((n,))],
-        compiler_params=pltpu.CompilerParams(collective_id=1, has_side_effects=True),
-    )(blocks)
-
+        compiler_params=pltpu.CompilerParams(collective_id=exchange_id, has_side_effects=True),
+    )(send)
 
 def local(
     tokens,
@@ -311,23 +311,19 @@
         .astype(jnp.bfloat16)
         .reshape(experts, capacity, feat_local)
     )
-    send_both = jnp.concatenate([send_x, send_dy], axis=2)
-    recv_both = a2a_expert(send_both)
-    recv_both = recv_both.reshape(experts, capacity, 2, feat_local).transpose(2, 1, 0, 3)
-    recv_both = recv_both.reshape(2, capacity, complete_width)
-
-    x_rows = lax.all_gather(recv_both[0], "dp", axis=0, tiled=True)
-    dy_rows = lax.all_gather(recv_both[1], "dp", axis=0, tiled=True)
+    x_block = a2a_expert(send_x, 1)
+    x_rows = lax.all_gather(x_block, "dp", axis=0, tiled=True)
+    dy_block = a2a_expert(send_dy, 2)
+    dy_rows = lax.all_gather(dy_block, "dp", axis=0, tiled=True)
     rows_out, parts, owned_total = rows_backward_parts(x_rows, dy_rows, params)
     packed = rows_out.reshape(shards, capacity, complete_width + PART_COLS)
     summed_packed = lax.psum_scatter(packed, "dp", scatter_dimension=0, tiled=True)[0]
     summed = summed_packed[:, :complete_width]
     parts_mine = summed_packed[:, complete_width:]
     parts_sum = gather_dp(parts_mine, shards).reshape(shards * capacity, PART_COLS)
-    grad_a_gate = ADAPTER_SCALE * contract_pair(parts_sum[:, :adapter_rank], x_rows, 0, 0)
-    grad_a_up = ADAPTER_SCALE * contract_pair(
-        parts_sum[:, adapter_rank:2 * adapter_rank], x_rows, 0, 0
-    )
+    grad_a_pair = ADAPTER_SCALE * contract_pair(parts_sum[:, :2 * adapter_rank], x_rows, 0, 0)
+    grad_a_gate = grad_a_pair[:adapter_rank]
+    grad_a_up = grad_a_pair[adapter_rank:]
     grad_b_down = ADAPTER_SCALE * contract_pair(
         dy_rows, parts_sum[:, 2 * adapter_rank:3 * adapter_rank], 0, 0
     )

time: 427 us -> 401 us (0.939)
  waiting for transfers between devices: 229 us -> 206 us
  Pallas kernels: 37.7 us -> 43.5 us
  local copies, waits for them, and re-layouts: 35.7 us -> 31.1 us
    all_gather x2, waiting for transfers between devices: 139 us -> 116 us  [the longest x1 59.4 us: local(): dy_rows = lax.all_gather(dy_block, 'dp', axis=0, tiled=True)]
    pallas_call x1 -> x2, Pallas kernels: 26.9 us -> 32.6 us  [a2a_expert(): pl.pallas_call(functools.partial(a2a_expert_kernel, n, width), out_shape=...]
    unnamed x55 -> x47, local copies, waits for them, and re-layouts: 11.7 us -> 8.51 us
    dot_general x18 -> x17, matrix products: 70.8 us -> 67.9 us  [contract_pair(): lax.dot_general(left, right, (((left_axis,), (right_axis,)), ((), ())), p...]
  transfers between devices with their start and end apart: 4 -> 4, of which waited for: 3 -> 3; matrix products, arithmetic and copies ran while one was open for 15% -> 17% of each run, Pallas kernels for 3% -> 6%
where the time goes in v9:
time: 401 us; the launch traced here: 396 us
  waiting for transfers between devices  206 us (51%)
  matrix products  88.1 us (22%)
  Pallas kernels  43.5 us (11%)
  local copies, waits for them, and re-layouts  31.1 us (8%)
  between operations  14.4 us (4%)
  other arithmetic  6.34 us (2%)
  starting transfers between devices  6.27 us (2%)
    unnamed x4, waiting for transfers between devices  90.5 us
    dot_general x17, matrix products, contract_pair(): lax.dot_general(left, right, (((left_axis,), (right_axis,)), ((), ())), p...  67.9 us
    all_gather x1, waiting for transfers between devices, local(): dy_rows = lax.all_gather(dy_block, 'dp', axis=0, tiled=True)  59.4 us
    all_gather x1, waiting for transfers between devices, local(): x_rows = lax.all_gather(x_block, 'dp', axis=0, tiled=True)  56.5 us
    pallas_call x2, Pallas kernels, a2a_expert(): pl.pallas_call(functools.partial(a2a_expert_kernel, n, width), out_shape=...  32.6 us
    dot_general x1, matrix products, rows_backward_parts(): lax.dot_general(lhs, extended, (((0,), (0,)), ((), ())), preferred_elemen...  20.2 us
    pallas_call x1, Pallas kernels, gather_dp(): pl.pallas_call(functools.partial(gather_dp_kernel, n), out_shape=jax.Shap...  10.8 us
    unnamed x47, local copies, waits for them, and re-layouts  8.51 us
  transfers between devices with their start and end apart: 4, of which 3 were waited for; matrix products, arithmetic and copies ran while one was open for 17% of the time, Pallas kernels for 6%

profile of v9, /device:TPU:1, one launch (start us, length us, event | category | flops | bytes accessed | tf_op | source)
XLA Modules:
  0.0 396.0 jit_solution(17949341318705556167)
XLA Ops:
  7.2 0.7 convert_reduce_fusion
  7.9 0.1 copy.31
  8.1 0.2 reduce_window_sum.11
  8.3 0.7 select_reduce_fusion
  9.0 0.7 compare_select_fusion.3
  9.7 0.1 copy.34
  9.8 0.1 reshape.94
  10.0 0.1 reshape.150
  10.1 0.1 reshape.142
  10.3 1.4 scatter_custom_fusion.1
  11.7 1.4 scatter_custom_fusion
  13.1 0.9 concatenate.19
  14.0 3.3 gather_fusion.2
  17.4 17.9 %shard_map.181 = bf16[96,4096]{1,0:T(8,128)(2,1)} custom-call(bf16[8,96,512]{2,1,0:T(8,128)(2,1)} %bitcast.104), custom_call_target="tpu_custom_call" | custom-call | tf_op jit(solution)/shard_map/pallas_call | solution.py:254
  35.4 0.1 copy.35
  35.5 0.1 reshape.96
  35.7 5.0 %gather_fusion = f32[768]{0:T(1024)S(1)} fusion(f32[256]{0:T(256)S(1)} %reshape.96, s32[1024]{0:T(1024)S(1)} %get-tuple-element.38), kind=kCustom, calls=%fused_computation | custom fusion | bytes 9216 | tf_op jit(solution)/shard_map/gather | solution.py:303
  40.7 0.1 mul.106
  40.7 2.7 gather_fusion.1
  43.4 1.1 fusion.21.src_ref
  44.6 14.7 %shard_map.180 = bf16[96,4096]{1,0:T(8,128)(2,1)} custom-call(bf16[8,96,512]{2,1,0:T(8,128)(2,1)} %fusion.21.src_ref), custom_call_target="tpu_custom_call" | custom-call | tf_op jit(solution)/shard_map/pallas_call | solution.py:254
  59.3 0.6 reduce-scatter.4.cloned.1.call-start
  59.9 0.2 fusion.25
  60.1 4.4 %bitcast_dynamic-update-slice_fusion.1 = bf16[944,4096]{1,0:T(8,128)(2,1)} fusion(bf16[1,448,4096]{2,1,0:T(8,128)(2,1)} %param.17), kind=kLoop, calls=%fused_computation.18 | loop fusion | bytes 7340032
  64.5 2.2 bitcast_dynamic-update-slice_fusion
  66.7 0.7 fusion.28
  67.4 0.7 fusion.29
  68.1 0.7 broadcast_dynamic-update-slice_fusion
  68.7 56.5 %all-gather.5.cloned.1.call-done = bf16[1536,4096]{1,0:T(8,128)(2,1)} async-done(((bf16[96,4096]{1,0:T(8,128)(2,1)}), bf16[1536,4096]{1,0:T(8,128)(2,1)}) %all-gather.5.cloned.1.call-update) | async-done | bytes 12582928 | tf_op jit(solution)/shard_map/all_gather | solution.py:315
  125.3 8.1 %convolution_convert_fusion.6 = bf16[1536,16]{0,1:T(8,128)(2,1)S(1)} fusion(bf16[1536,4096]{1,0:T(8,128)(2,1)} %all-gather.5.cloned.1.call-done, bf16[1,16,4096]{2,1,0:T(8,128)(2,1)S(1)} %copy-done.15), kind=kOutput, calls=%fused_computation.44 | convolution fusion | flops 201351168 | bytes 12763136 | tf_op jit(solution)/shard_map/dot_general | solution.py:18
  133.3 0.1 copy-done.2
  133.4 8.0 %fusion.8 = f32[1536,448]{0,1:T(8,128)S(1)} fusion(bf16[1536,4096]{1,0:T(8,128)(2,1)S(1)} %copy-done.2, bf16[1,448,4096]{2,1,0:T(8,128)(2,1)} %param.17), kind=kOutput, calls=%fused_computation.19 | convolution fusion | flops 5637144576 | bytes 19005440 | tf_op jit(solution)/shard_map/dot_general | solution.py:18
  141.4 0.6 fusion.13
  142.0 3.3 convolution_convert_fusion.5
  145.3 6.1 %fusion.6 = f32[1536,448]{0,1:T(8,128)S(1)} fusion(bf16[1536,4096]{1,0:T(8,128)(2,1)S(1)} %copy-done.2, bf16[1,448,4096]{2,1,0:T(8,128)(2,1)S(1)} %copy-done.14), kind=kOutput, calls=%fused_computation.16 | convolution fusion | flops 5637144576 | bytes 19005440 | tf_op jit(solution)/shard_map/dot_general | solution.py:18
  151.4 3.9 multiply_convert_fusion.2
  155.3 1.5 copy-done.10
  156.9 0.9 convolution_convert_fusion.3
  157.7 59.4 %all-gather.3.cloned.1.call-done = bf16[1536,4096]{1,0:T(8,128)(2,1)} async-done(((bf16[96,4096]{1,0:T(8,128)(2,1)}), bf16[1536,4096]{1,0:T(8,128)(2,1)}) %all-gather.3.cloned.1.call-update) | async-done | bytes 12582928 | tf_op jit(solution)/shard_map/all_gather | solution.py:317
  217.1 8.1 %convolution_convert_fusion.4 = bf16[1536,16]{0,1:T(8,128)(2,1)S(1)} fusion(bf16[1536,4096]{1,0:T(8,128)(2,1)} %all-gather.3.cloned.1.call-done, bf16[1,4096,16]{1,2,0:T(8,128)(2,1)S(1)} %copy-done), kind=kOutput, calls=%fused_computation.42 | convolution fusion | flops 201351168 | bytes 12763136 | tf_op jit(solution)/shard_map/dot_general | solution.py:18
  225.2 0.1 copy-done.3
  225.3 8.3 %fusion.4 = f32[1536,448]{0,1:T(8,128)S(1)} fusion(bf16[1536,4096]{1,0:T(8,128)(2,1)S(1)} %copy-done.3, bf16[1,448,4096]{2,1,0:T(8,128)(2,1)} %param.19), kind=kOutput, calls=%fused_computation.13 | convolution fusion | flops 5637144576 | bytes 19005440 | tf_op jit(solution)/shard_map/dot_general | solution.py:18
  233.6 1.3 multiply_convert_fusion.1
  235.0 0.3 convolution_convert_fusion.2
  235.2 0.3 convolution_convert_fusion.1
  235.6 20.2 %convolution_convert_fusion = bf16[1536,4224]{1,0:T(8,128)(2,1)} fusion(bf16[944,128]{1,0:T(8,128)(2,1)S(1)} %fusion.25, bf16[944,4096]{1,0:T(8,128)(2,1)} %broadcast_dynamic-update-slice_fusion, bf16[48,1536]{1,0:T(8,128)(2,1)S(1)} %maximum_bitcast_fusion, bf16[448,1536]{1,0:T(8,128)(2,1)S(1)} %get-tuple-element.26, bf16[448,1536]{1,0:T(8,128)(2,1)S(1)} %get-tuple-element.25), kind=kOutput, calls=%fused_computation.6 | convolution fusion | flops 12280602624 | bytes 23851008 | tf_op jit(solution)/shard_map/dot_general | solution.py:177
  255.8 0.1 copy.38
  255.9 0.1 reshape.132
  256.1 2.6 fusion.22
  258.7 1.1 fusion.23
  259.8 1.1 fusion.24
  260.9 90.4 %reduce-scatter.4.cloned.1.call-done = bf16[1,96,4224]{2,1,0:T(8,128)(2,1)} async-done(((bf16[16,96,4224]{2,1,0:T(8,128)(2,1)}), bf16[1,96,4224]{2,1,0:T(8,128)(2,1)}) %reduce-scatter.4.cloned.1.call-update) | async-done | bytes 811024
  351.3 1.3 slice.33.src_ref
  352.6 1.2 slice.32
  353.8 1.0 copy.43
  354.8 5.6 %all-to-all-start = ((bf16[96,8,512]{2,0,1:T(8,128)(2,1)}), bf16[96,8,512]{2,0,1:T(8,128)(2,1)S(1)}, u32[]{:S(2)}, u32[]{:S(2)}) async-start(bf16[96,8,512]{2,0,1:T(8,128)(2,1)} %bitcast.96), calls=%async_computation | async-start | bytes 1572864 | tf_op jit(solution)/shard_map/all_to_all | solution.py:330
  360.4 10.8 %shard_map.182 = bf16[16,96,128]{2,1,0:T(8,128)(2,1)} custom-call(bf16[96,128]{1,0:T(8,128)(2,1)} %slice.33.src_ref), custom_call_target="tpu_custom_call" | custom-call | tf_op jit(solution)/shard_map/pallas_call | solution.py:215
  371.2 7.2 %fusion.3 = f32[1,4096,16]{1,2,0:T(8,128)} fusion(bf16[1536,4096]{1,0:T(8,128)(2,1)} %all-gather.3.cloned.1.call-done, bf16[1536,128]{1,0:T(8,128)(2,1)} %bitcast.101), kind=kOutput, calls=%fused_computation.12 | convolution fusion | flops 201392128 | bytes 13238272 | tf_op jit(solution)/shard_map/dot_general | solution.py:18
  378.4 6.9 %convolution_multiply_fusion = f32[32,4096]{1,0:T(8,128)S(1)} fusion(bf16[1536,4096]{1,0:T(8,128)(2,1)} %all-gather.5.cloned.1.call-done, bf16[1536,128]{1,0:T(8,128)(2,1)S(1)} %bitcast.102), kind=kOutput, calls=%fused_computation.10 | convolution fusion | flops 402784256 | bytes 13500416 | tf_op jit(solution)/shard_map/dot_general | solution.py:18
  385.3 0.8 slice_bitcast_fusion
  386.2 0.5 copy.42
  386.6 1.0 gather_fusion.3
  387.6 0.3 reshape.135
  387.9 1.3 reduce_sum.29
  (59 shorter events, 0.4 us)
Async XLA Ops:
  7.2 210.0 %copy-start = (bf16[1,4096,16]{1,2,0:T(8,128)(2,1)S(1)}, bf16[1,4096,16]{1,2,0:T(8,128)(2,1)}, u32[]{:S(2)}) copy-start(bf16[1,4096,16]{1,2,0:T(8,128)(2,1)} %param.25) | copy-start | bytes 393220
  7.2 118.1 %all-gather.5.cloned.1.call-start = ((), (), s32[]{:S(2)}) async-start(), calls=%async_computation.3 | async-start | bytes 13369344 | tf_op jit(solution)/shard_map/all_gather | solution.py:315
  14.0 21.4 %copy-start.21 = (f32[128,2]{0,1:T(2,128)S(1)}, f32[128,2]{0,1:T(2,128)}, u32[]{:S(2)}) copy-start(f32[128,2]{0,1:T(2,128)} %param.16) | copy-start | bytes 3076
  35.3 5.4 %copy-start.17 = (bf16[128,512]{1,0:T(8,128)(2,1)S(1)}, bf16[128,512]{1,0:T(8,128)(2,1)}, u32[]{:S(2)}) copy-start(bf16[128,512]{1,0:T(8,128)(2,1)} %param.14) | copy-start | bytes 393220
  35.3 181.8 %all-gather.3.cloned.1.call-start = ((), (), s32[]{:S(2)}) async-start(), calls=%async_computation.2 | async-start | bytes 13369344 | tf_op jit(solution)/shard_map/all_gather | solution.py:317
  59.3 291.9 %reduce-scatter.4.cloned.1.call-start = ((), (), s32[]{:S(2)}) async-start(), calls=%async_computation.4 | async-start | bytes 13787136
  60.1 4.4 %copy-start.13 = (bf16[1,448,4096]{2,1,0:T(8,128)(2,1)S(1)}, bf16[1,448,4096]{2,1,0:T(8,128)(2,1)}, u32[]{:S(2)}) copy-start(bf16[1,448,4096]{2,1,0:T(8,128)(2,1)} %param.18) | copy-start | bytes 11010052
  64.5 2.2 copy-start.15
  64.5 2.9 copy-start.16
  125.3 8.2 %copy-start.2 = (bf16[1536,4096]{1,0:T(8,128)(2,1)S(1)}, bf16[1536,4096]{1,0:T(8,128)(2,1)}, u32[]{:S(2)}) copy-start(bf16[1536,4096]{1,0:T(8,128)(2,1)} %all-gather.5.cloned.1.call-done) | copy-start | bytes 37748740
  133.4 8.0 %copy-start.18 = (bf16[1,448,16]{1,2,0:T(8,128)(2,1)S(1)}, bf16[1,448,16]{1,2,0:T(8,128)(2,1)}, u32[]{:S(2)}) copy-start(bf16[1,448,16]{1,2,0:T(8,128)(2,1)} %param.21) | copy-start | bytes 43012
  142.0 3.4 copy-start.14
  145.3 6.1 %copy-start.19 = (bf16[1,448,16]{1,2,0:T(8,128)(2,1)S(1)}, bf16[1,448,16]{1,2,0:T(8,128)(2,1)}, u32[]{:S(2)}) copy-start(bf16[1,448,16]{1,2,0:T(8,128)(2,1)} %param.23) | copy-start | bytes 43012
  151.4 5.4 %copy-start.20 = (bf16[1,16,448]{2,1,0:T(8,128)(2,1)S(1)}, bf16[1,16,448]{2,1,0:T(8,128)(2,1)}, u32[]{:S(2)}) copy-start(bf16[1,16,448]{2,1,0:T(8,128)(2,1)} %param.24) | copy-start | bytes 43012
  155.3 1.5 copy-start.10
  217.1 8.2 %copy-start.3 = (bf16[1536,4096]{1,0:T(8,128)(2,1)S(1)}, bf16[1536,4096]{1,0:T(8,128)(2,1)}, u32[]{:S(2)}) copy-start(bf16[1536,4096]{1,0:T(8,128)(2,1)} %all-gather.3.cloned.1.call-done) | copy-start | bytes 37748740
  225.3 8.3 %copy-start.8 = (f32[448,1536]{1,0:T(8,128)S(1)}, f32[448,1536]{1,0:T(8,128)}, u32[]{:S(2)}) copy-start(f32[448,1536]{1,0:T(8,128)} %get-tuple-element.20) | copy-start | bytes 8257540
  225.3 8.3 %copy-start.9 = (f32[448,1536]{1,0:T(8,128)S(1)}, f32[448,1536]{1,0:T(8,128)}, u32[]{:S(2)}) copy-start(f32[448,1536]{1,0:T(8,128)} %get-tuple-element.18) | copy-start | bytes 8257540
  225.3 8.3 %copy-start.11 = (f32[448,1536]{1,0:T(8,128)S(1)}, f32[448,1536]{1,0:T(8,128)}, u32[]{:S(2)}) copy-start(f32[448,1536]{1,0:T(8,128)} %copy-done.10) | copy-start | bytes 8257540
  234.9 20.8 %copy-start.4 = (bf16[448,1536]{1,0:T(8,128)(2,1)}, bf16[448,1536]{1,0:T(8,128)(2,1)S(1)}, u32[]{:S(2)}) copy-start(bf16[448,1536]{1,0:T(8,128)(2,1)S(1)} %get-tuple-element.25) | copy-start | bytes 4128772
  235.0 20.8 %copy-start.6 = (bf16[448,1536]{1,0:T(8,128)(2,1)}, bf16[448,1536]{1,0:T(8,128)(2,1)S(1)}, u32[]{:S(2)}) copy-start(bf16[448,1536]{1,0:T(8,128)(2,1)S(1)} %get-tuple-element.26) | copy-start | bytes 4128772
  255.8 2.9 copy-start.7
  255.8 4.0 %copy-start.5 = (bf16[448,1536]{1,0:T(8,128)(2,1)S(1)}, bf16[448,1536]{1,0:T(8,128)(2,1)}, u32[]{:S(2)}) copy-start(bf16[448,1536]{1,0:T(8,128)(2,1)} %copy-done.4) | copy-start | bytes 4128772
  354.8 31.4 %all-to-all-start = ((bf16[96,8,512]{2,0,1:T(8,128)(2,1)}), bf16[96,8,512]{2,0,1:T(8,128)(2,1)S(1)}, u32[]{:S(2)}, u32[]{:S(2)}) async-start(bf16[96,8,512]{2,0,1:T(8,128)(2,1)} %bitcast.96), calls=%async_computation | async-start | bytes 1572864 | tf_op jit(solution)/shard_map/all_to_all | solution.py:330
  371.2 7.2 %copy-start.12 = (bf16[16,96,128]{2,1,0:T(8,128)(2,1)S(1)}, bf16[16,96,128]{2,1,0:T(8,128)(2,1)}, u32[]{:S(2)}) copy-start(bf16[16,96,128]{2,1,0:T(8,128)(2,1)} %shard_map.182) | copy-start | bytes 1179652
  386.6 2.6 copy-start.1
Sparse Core Ops, SparseCore 0:
  35.5 89.7 all-gather.4
  127.4 89.6 all-gather.2
  255.9 95.3 reduce-scatter.3

commit v10 on v9

--- a/solution.py
+++ b/solution.py
@@ -157,23 +157,16 @@
     gate_partial = contract_pair(gate_gradient, gate_adapter_upper, 0, 0).astype(jnp.bfloat16)
     up_partial = contract_pair(up_gradient, up_adapter_upper, 0, 0).astype(jnp.bfloat16)
     parts = jnp.concatenate([gate_partial, up_partial, down_partial], 1)
-    rank3 = parts.shape[1]
-    hidden_here, width = gate_weight.shape
-    lhs = jnp.concatenate([gate_gradient, up_gradient, parts.T], 0)
+    pair = jnp.concatenate([gate_partial, up_partial], 1)
+    lhs = jnp.concatenate([gate_gradient, up_gradient, pair.T], 0)
     lora_rows = jnp.concatenate(
         [
             (ADAPTER_SCALE * a_gate.astype(jnp.float32)).astype(jnp.bfloat16),
             (ADAPTER_SCALE * a_up.astype(jnp.float32)).astype(jnp.bfloat16),
-            jnp.zeros((rank3 - a_gate.shape[0] - a_up.shape[0], width), jnp.bfloat16),
         ],
         0,
     )
-    left_block = jnp.concatenate([gate_weight, up_weight, lora_rows], 0)
-    picker = (
-        jnp.arange(2 * hidden_here + rank3, dtype=jnp.int32)[:, None] - 2 * hidden_here
-        == jnp.arange(PART_COLS, dtype=jnp.int32)[None, :]
-    ).astype(jnp.bfloat16)
-    extended = jnp.concatenate([left_block, picker], 1)
+    extended = jnp.concatenate([gate_weight, up_weight, lora_rows], 0)
     gradient_rows_out = lax.dot_general(
         lhs, extended, (((0,), (0,)), ((), ())), preferred_element_type=jnp.float32
     ).astype(jnp.bfloat16)
@@ -259,6 +252,49 @@
         scratch_shapes=[pltpu.SemaphoreType.DMA((n,)), pltpu.SemaphoreType.DMA((n,))],
         compiler_params=pltpu.CompilerParams(collective_id=exchange_id, has_side_effects=True),
     )(send)
+
+def reduce_dp_kernel(n, src_ref, out_ref, landing, send_sem, recv_sem):
+    me = lax.axis_index("dp")
+    ex = lax.axis_index("expert")
+    barrier = pltpu.get_barrier_semaphore()
+    for k in range(1, n):
+        peer = lax.rem(me + k, n)
+        pl.semaphore_signal(barrier, inc=1, device_id=(peer, ex), device_id_type=MESH)
+    pl.semaphore_wait(barrier, n - 1)
+    copies = []
+    for k in range(1, n):
+        peer = lax.rem(me + k, n)
+        cp = pltpu.make_async_remote_copy(
+            src_ref.at[peer],
+            landing.at[me],
+            send_sem.at[k],
+            recv_sem.at[k],
+            device_id=(peer, ex),
+            device_id_type=MESH,
+        )
+        cp.start()
+        copies.append(cp)
+    landing[me] = src_ref[me]
+    for cp in copies:
+        cp.wait()
+    out_ref[...] = jnp.sum(landing[...].astype(jnp.float32), axis=0)
+
+
+def reduce_dp(blocks):
+    n, rows, cols = blocks.shape
+    return pl.pallas_call(
+        functools.partial(reduce_dp_kernel, n),
+        out_shape=jax.ShapeDtypeStruct((rows, cols), jnp.float32),
+        in_specs=[pl.BlockSpec(memory_space=pltpu.VMEM)],
+        out_specs=pl.BlockSpec(memory_space=pltpu.VMEM),
+        scratch_shapes=[
+            pltpu.VMEM((n, rows, cols), blocks.dtype),
+            pltpu.SemaphoreType.DMA((n,)),
+            pltpu.SemaphoreType.DMA((n,)),
+        ],
+        compiler_params=pltpu.CompilerParams(collective_id=3, has_side_effects=True),
+    )(blocks)
+
 
 def local(
     tokens,
@@ -316,10 +352,10 @@
     dy_block = a2a_expert(send_dy, 2)
     dy_rows = lax.all_gather(dy_block, "dp", axis=0, tiled=True)
     rows_out, parts, owned_total = rows_backward_parts(x_rows, dy_rows, params)
-    packed = rows_out.reshape(shards, capacity, complete_width + PART_COLS)
-    summed_packed = lax.psum_scatter(packed, "dp", scatter_dimension=0, tiled=True)[0]
-    summed = summed_packed[:, :complete_width]
-    parts_mine = summed_packed[:, complete_width:]
+    packed = rows_out.reshape(shards, capacity, complete_width)
+    summed = lax.psum_scatter(packed, "dp", scatter_dimension=0, tiled=True)[0]
+    parts_blocks = jnp.pad(parts, ((0, 0), (0, PART_COLS - 3 * adapter_rank)))
+    parts_mine = reduce_dp(parts_blocks.reshape(shards, capacity, PART_COLS))
     parts_sum = gather_dp(parts_mine, shards).reshape(shards * capacity, PART_COLS)
     grad_a_pair = ADAPTER_SCALE * contract_pair(parts_sum[:, :2 * adapter_rank], x_rows, 0, 0)
     grad_a_gate = grad_a_pair[:adapter_rank]

time: 401 us -> 394 us (0.983)
  Pallas kernels: 43.5 us -> 66.1 us
  waiting for transfers between devices: 206 us -> 190 us
  local copies, waits for them, and re-layouts: 31.1 us -> 24.5 us
  matrix products: 88.1 us -> 83.5 us
    unnamed x4, waiting for transfers between devices: 90.5 us -> 54.1 us
    pallas_call x0 -> x1, Pallas kernels: none -> 11.6 us  [reduce_dp(): pl.pallas_call(functools.partial(reduce_dp_kernel, n), out_shape=jax.Shap...]
    all_to_all x1, waiting for transfers between devices: 0.01 us -> 11.5 us  [local(): lax.all_to_all(summed.reshape(capacity, experts, feat_local), 'expert', s...]
    pallas_call x1, Pallas kernels: 10.8 us -> 21.8 us  [gather_dp(): pl.pallas_call(functools.partial(gather_dp_kernel, n), out_shape=jax.Shap...]
    all_gather x1, waiting for transfers between devices: 56.5 us -> 65.3 us  [local(): x_rows = lax.all_gather(x_block, 'dp', axis=0, tiled=True)]
    unnamed x47 -> x55, local copies, waits for them, and re-layouts: 8.51 us -> 4.05 us
  transfers between devices with their start and end apart: 4 -> 4, of which waited for: 3 -> 4; matrix products, arithmetic and copies ran while one was open for 17% -> 15% of each run, Pallas kernels for 6% -> 12%
where the time goes in v10:
time: 394 us; the launch traced here: 389 us
  waiting for transfers between devices  190 us (48%)
  matrix products  83.5 us (21%)
  Pallas kernels  66.1 us (17%)
  local copies, waits for them, and re-layouts  24.5 us (6%)
  between operations  14.5 us (4%)
  starting transfers between devices  5.97 us (2%)
  other arithmetic  4.84 us (1%)
    all_gather x1, waiting for transfers between devices, local(): x_rows = lax.all_gather(x_block, 'dp', axis=0, tiled=True)  65.3 us
    dot_general x17, matrix products, contract_pair(): lax.dot_general(left, right, (((left_axis,), (right_axis,)), ((), ())), p...  64.5 us
    all_gather x1, waiting for transfers between devices, local(): dy_rows = lax.all_gather(dy_block, 'dp', axis=0, tiled=True)  58.7 us
    unnamed x4, waiting for transfers between devices  54.1 us
    pallas_call x2, Pallas kernels, a2a_expert(): pl.pallas_call(functools.partial(a2a_expert_kernel, n, width), out_shape=...  32.7 us
    pallas_call x1, Pallas kernels, gather_dp(): pl.pallas_call(functools.partial(gather_dp_kernel, n), out_shape=jax.Shap...  21.8 us
    dot_general x1, matrix products, rows_backward_parts(): lax.dot_general(lhs, extended, (((0,), (0,)), ((), ())), preferred_elemen...  19 us
    pallas_call x1, Pallas kernels, reduce_dp(): pl.pallas_call(functools.partial(reduce_dp_kernel, n), out_shape=jax.Shap...  11.6 us
  transfers between devices with their start and end apart: 4, of which 4 were waited for; matrix products, arithmetic and copies ran while one was open for 15% of the time, Pallas kernels for 12%

profile of v10, /device:TPU:1, one launch (start us, length us, event | category | flops | bytes accessed | tf_op | source)
XLA Modules:
  0.0 388.9 jit_solution(7133401142819682071)
XLA Ops:
  7.2 0.0 all-gather.5.cloned.1.call-start
  7.2 0.7 convert_reduce_fusion
  7.9 0.1 copy.34
  8.1 0.2 reduce_window_sum.11
  8.3 0.7 select_reduce_fusion
  9.0 0.7 compare_select_fusion.3
  9.7 0.1 copy.37
  9.8 0.1 reshape.89
  10.0 0.1 reshape.145
  10.1 0.1 reshape.137
  10.3 1.4 scatter_custom_fusion.1
  11.7 1.4 scatter_custom_fusion
  13.1 0.9 concatenate.19
  14.0 3.3 gather_fusion.2
  17.4 18.0 %shard_map.181 = bf16[96,4096]{1,0:T(8,128)(2,1)} custom-call(bf16[8,96,512]{2,1,0:T(8,128)(2,1)} %bitcast.103), custom_call_target="tpu_custom_call" | custom-call | tf_op jit(solution)/shard_map/pallas_call | solution.py:247
  35.4 0.0 all-gather.3.cloned.1.call-start
  35.5 0.1 copy.38
  35.6 0.1 reshape.91
  35.7 5.0 %gather_fusion = f32[768]{0:T(1024)S(1)} fusion(f32[256]{0:T(256)S(1)} %reshape.91, s32[1024]{0:T(1024)S(1)} %get-tuple-element.38), kind=kCustom, calls=%fused_computation | custom fusion | bytes 9216 | tf_op jit(solution)/shard_map/gather | solution.py:339
  40.7 0.1 mul.106
  40.8 2.7 gather_fusion.1
  43.5 1.1 fusion.21.src_ref
  44.7 14.7 %shard_map.180 = bf16[96,4096]{1,0:T(8,128)(2,1)} custom-call(bf16[8,96,512]{2,1,0:T(8,128)(2,1)} %fusion.21.src_ref), custom_call_target="tpu_custom_call" | custom-call | tf_op jit(solution)/shard_map/pallas_call | solution.py:247
  59.4 0.6 reduce-scatter.4.cloned.1.call-start
  60.0 65.3 %all-gather.5.cloned.1.call-done = bf16[1536,4096]{1,0:T(8,128)(2,1)} async-done(((bf16[96,4096]{1,0:T(8,128)(2,1)}), bf16[1536,4096]{1,0:T(8,128)(2,1)}) %all-gather.5.cloned.1.call-update) | async-done | bytes 12582928 | tf_op jit(solution)/shard_map/all_gather | solution.py:351
  125.3 8.1 %convolution_convert_fusion.6 = bf16[1536,16]{0,1:T(8,128)(2,1)S(1)} fusion(bf16[1536,4096]{1,0:T(8,128)(2,1)} %all-gather.5.cloned.1.call-done, bf16[1,16,4096]{2,1,0:T(8,128)(2,1)S(1)} %copy-done.13), kind=kOutput, calls=%fused_computation.42 | convolution fusion | flops 201351168 | bytes 12763136 | tf_op jit(solution)/shard_map/dot_general | solution.py:18
  133.4 0.1 copy-done.2
  133.5 8.0 %fusion.43 = f32[1536,448]{0,1:T(8,128)S(1)} fusion(bf16[1536,4096]{1,0:T(8,128)(2,1)S(1)} %copy-done.2, bf16[1,448,4096]{2,1,0:T(8,128)(2,1)} %param.17), kind=kOutput, calls=%fused_computation.88 | convolution fusion | flops 5637144576 | bytes 19005440 | tf_op jit(solution)/shard_map/dot_general | solution.py:18
  141.5 0.6 fusion.13
  142.1 3.3 convolution_convert_fusion.5
  145.4 6.1 %fusion.41 = f32[1536,448]{0,1:T(8,128)S(1)} fusion(bf16[1536,4096]{1,0:T(8,128)(2,1)S(1)} %copy-done.2, bf16[1,448,4096]{2,1,0:T(8,128)(2,1)S(1)} %copy-done.22), kind=kOutput, calls=%fused_computation.86 | convolution fusion | flops 5637144576 | bytes 19005440 | tf_op jit(solution)/shard_map/dot_general | solution.py:18
  151.5 4.0 %multiply_convert_fusion.2 = (bf16[448,1536]{1,0:T(8,128)(2,1)}, f32[448,1536]{1,0:T(8,128)}, f32[448,1536]{1,0:T(8,128)}, f32[448,1536]{1,0:T(8,128)S(1)}) fusion(f32[448,1536]{1,0:T(8,128)S(1)} %fusion.13, f32[1536,448]{0,1:T(8,128)S(1)} %fusion.41, bf16[1536,16]{0,1:T(8,128)(2,1)S(1)} %convolution_convert_fusion.5, bf16[1,448,16]{1,2,0:T(8,128)(2,1)S(1)} %copy-done.18), kind=kOutput, calls=%fused_computation.35 | convolution fusion | flops 27525120 | bytes 15202304 | tf_op jit(solution)/shard_map/dot_general | solution.py:18
  155.5 1.5 copy-done.10
  157.0 1.5 convolution_convert_fusion.3
  158.5 58.7 %all-gather.3.cloned.1.call-done = bf16[1536,4096]{1,0:T(8,128)(2,1)} async-done(((bf16[96,4096]{1,0:T(8,128)(2,1)}), bf16[1536,4096]{1,0:T(8,128)(2,1)}) %all-gather.3.cloned.1.call-update) | async-done | bytes 12582928 | tf_op jit(solution)/shard_map/all_gather | solution.py:353
  217.2 8.1 %convolution_convert_fusion.4 = bf16[1536,16]{0,1:T(8,128)(2,1)S(1)} fusion(bf16[1536,4096]{1,0:T(8,128)(2,1)} %all-gather.3.cloned.1.call-done, bf16[1,4096,16]{1,2,0:T(8,128)(2,1)S(1)} %copy-done), kind=kOutput, calls=%fused_computation.40 | convolution fusion | flops 201351168 | bytes 12763136 | tf_op jit(solution)/shard_map/dot_general | solution.py:18
  225.3 0.1 copy-done.3
  225.4 8.3 %fusion.8 = f32[1536,448]{0,1:T(8,128)S(1)} fusion(bf16[1536,4096]{1,0:T(8,128)(2,1)S(1)} %copy-done.3, bf16[1,448,4096]{2,1,0:T(8,128)(2,1)} %param.19), kind=kOutput, calls=%fused_computation.17 | convolution fusion | flops 5637144576 | bytes 19005440 | tf_op jit(solution)/shard_map/dot_general | solution.py:18
  233.7 1.3 multiply_convert_fusion.1
  235.1 0.3 convolution_convert_fusion.2
  235.3 0.3 convolution_convert_fusion.1
  235.7 19.0 %convolution_convert_fusion = bf16[1536,4096]{1,0:T(8,128)(2,1)} fusion(bf16[16,4096]{1,0:T(8,128)(2,1)S(1)} %get-tuple-element.39, bf16[16,4096]{1,0:T(8,128)(2,1)S(1)} %get-tuple-element.40, bf16[448,4096]{1,0:T(8,128)(2,1)} %bitcast.111, bf16[448,4096]{1,0:T(8,128)(2,1)} %bitcast.112, bf16[32,1536]{1,0:T(8,128)(2,1)S(1)} %maximum_bitcast_fusion, ...), kind=kOutput, calls=%fused_computation.6 | convolution fusion | flops 11722194944 | bytes 23035904 | tf_op jit(solution)/shard_map/dot_general | solution.py:170
  254.7 0.1 copy.41
  254.8 0.1 reshape.127
  255.0 0.5 copy-done.19
  255.5 0.2 copy.43
  255.7 0.8 pad.6.clone
  256.6 11.6 %shard_map.182.src_ref = f32[96,128]{1,0:T(8,128)} custom-call(bf16[16,96,128]{2,1,0:T(8,128)(2,1)} %bitcast.105), custom_call_target="tpu_custom_call" | custom-call | tf_op jit(solution)/shard_map/pallas_call | solution.py:285
  268.2 21.8 %shard_map.183 = f32[16,96,128]{2,1,0:T(8,128)} custom-call(f32[96,128]{1,0:T(8,128)} %shard_map.182.src_ref), custom_call_target="tpu_custom_call" | custom-call | tf_op jit(solution)/shard_map/pallas_call | solution.py:208
  290.0 2.7 fusion.22
  292.7 1.1 fusion.23
  293.8 1.1 fusion.24
  294.9 7.3 %convolution_multiply_fusion = f32[32,4096]{1,0:T(8,128)S(1)} fusion(bf16[1536,4096]{1,0:T(8,128)(2,1)} %all-gather.5.cloned.1.call-done, f32[1536,128]{1,0:T(8,128)S(1)} %bitcast.100), kind=kOutput, calls=%fused_computation.14 | convolution fusion | flops 402784256 | bytes 13500416 | tf_op jit(solution)/shard_map/dot_general | solution.py:18
  302.3 2.6 fusion.7
  304.8 54.1 %reduce-scatter.4.cloned.1.call-done = bf16[1,96,4096]{2,1,0:T(8,128)(2,1)} async-done(((bf16[16,96,4096]{2,1,0:T(8,128)(2,1)}), bf16[1,96,4096]{2,1,0:T(8,128)(2,1)}) %reduce-scatter.4.cloned.1.call-update) | async-done | bytes 786448
  358.9 1.4 copy.44
  360.3 1.1 copy.39
  361.4 5.3 %all-to-all-start = ((bf16[96,8,512]{2,0,1:T(8,128)(2,1)}), bf16[96,8,512]{2,0,1:T(8,128)(2,1)S(1)}, u32[]{:S(2)}, u32[]{:S(2)}) async-start(bf16[96,8,512]{2,0,1:T(8,128)(2,1)} %copy.39), calls=%async_computation | async-start | bytes 1572864 | tf_op jit(solution)/shard_map/all_to_all | solution.py:366
  366.8 0.8 slice_bitcast_fusion
  367.6 11.5 %all-to-all-done = bf16[96,8,512]{2,0,1:T(8,128)(2,1)S(1)} async-done(((bf16[96,8,512]{2,0,1:T(8,128)(2,1)}), bf16[96,8,512]{2,0,1:T(8,128)(2,1)S(1)}, u32[]{:S(2)}, u32[]{:S(2)}) %all-to-all-start) | async-done | bytes 786464 | tf_op jit(solution)/shard_map/all_to_all | solution.py:366
  379.1 0.5 copy.46
  379.5 1.0 gather_fusion.3
  380.5 0.3 reshape.130
  380.8 1.3 reduce_sum.29
  (65 shorter events, 0.4 us)
Async XLA Ops:
  7.2 210.0 %copy-start = (bf16[1,4096,16]{1,2,0:T(8,128)(2,1)S(1)}, bf16[1,4096,16]{1,2,0:T(8,128)(2,1)}, u32[]{:S(2)}) copy-start(bf16[1,4096,16]{1,2,0:T(8,128)(2,1)} %param.25) | copy-start | bytes 393220
  7.2 118.2 %all-gather.5.cloned.1.call-start = ((), (), s32[]{:S(2)}) async-start(), calls=%async_computation.3 | async-start | bytes 13369344 | tf_op jit(solution)/shard_map/all_gather | solution.py:351
  14.0 21.4 %copy-start.21 = (f32[128,2]{0,1:T(2,128)S(1)}, f32[128,2]{0,1:T(2,128)}, u32[]{:S(2)}) copy-start(f32[128,2]{0,1:T(2,128)} %param.16) | copy-start | bytes 3076
  35.4 5.4 %copy-start.16 = (bf16[128,512]{1,0:T(8,128)(2,1)S(1)}, bf16[128,512]{1,0:T(8,128)(2,1)}, u32[]{:S(2)}) copy-start(bf16[128,512]{1,0:T(8,128)(2,1)} %param.14) | copy-start | bytes 393220
  35.4 181.8 %all-gather.3.cloned.1.call-start = ((), (), s32[]{:S(2)}) async-start(), calls=%async_computation.2 | async-start | bytes 13369344 | tf_op jit(solution)/shard_map/all_gather | solution.py:353
  43.5 16.4 %copy-start.13 = (bf16[1,16,4096]{2,1,0:T(8,128)(2,1)S(1)}, bf16[1,16,4096]{2,1,0:T(8,128)(2,1)}, u32[]{:S(2)}) copy-start(bf16[1,16,4096]{2,1,0:T(8,128)(2,1)} %param.20) | copy-start | bytes 393220
  43.5 16.4 %copy-start.14 = (bf16[1,16,4096]{2,1,0:T(8,128)(2,1)S(1)}, bf16[1,16,4096]{2,1,0:T(8,128)(2,1)}, u32[]{:S(2)}) copy-start(bf16[1,16,4096]{2,1,0:T(8,128)(2,1)} %param.22) | copy-start | bytes 393220
  59.4 299.5 %reduce-scatter.4.cloned.1.call-start = ((), (), s32[]{:S(2)}) async-start(), calls=%async_computation.4 | async-start | bytes 13369344
  125.3 8.2 %copy-start.2 = (bf16[1536,4096]{1,0:T(8,128)(2,1)S(1)}, bf16[1536,4096]{1,0:T(8,128)(2,1)}, u32[]{:S(2)}) copy-start(bf16[1536,4096]{1,0:T(8,128)(2,1)} %all-gather.5.cloned.1.call-done) | copy-start | bytes 37748740
  133.5 8.0 %copy-start.17 = (bf16[1,448,16]{1,2,0:T(8,128)(2,1)S(1)}, bf16[1,448,16]{1,2,0:T(8,128)(2,1)}, u32[]{:S(2)}) copy-start(bf16[1,448,16]{1,2,0:T(8,128)(2,1)} %param.21) | copy-start | bytes 43012
  142.0 3.4 copy-start.22
  145.4 6.1 %copy-start.18 = (bf16[1,448,16]{1,2,0:T(8,128)(2,1)S(1)}, bf16[1,448,16]{1,2,0:T(8,128)(2,1)}, u32[]{:S(2)}) copy-start(bf16[1,448,16]{1,2,0:T(8,128)(2,1)} %param.23) | copy-start | bytes 43012
  151.5 5.5 %copy-start.20 = (bf16[1,16,448]{2,1,0:T(8,128)(2,1)S(1)}, bf16[1,16,448]{2,1,0:T(8,128)(2,1)}, u32[]{:S(2)}) copy-start(bf16[1,16,448]{2,1,0:T(8,128)(2,1)} %param.24) | copy-start | bytes 43012
  155.5 1.5 copy-start.10
  217.2 8.2 %copy-start.3 = (bf16[1536,4096]{1,0:T(8,128)(2,1)S(1)}, bf16[1536,4096]{1,0:T(8,128)(2,1)}, u32[]{:S(2)}) copy-start(bf16[1536,4096]{1,0:T(8,128)(2,1)} %all-gather.3.cloned.1.call-done) | copy-start | bytes 37748740
  225.4 8.3 %copy-start.15 = (bf16[1536,16]{0,1:T(8,128)(2,1)}, bf16[1536,16]{0,1:T(8,128)(2,1)S(1)}, u32[]{:S(2)}) copy-start(bf16[1536,16]{0,1:T(8,128)(2,1)S(1)} %convolution_convert_fusion.4) | copy-start | bytes 147460
  225.4 8.3 %copy-start.8 = (f32[448,1536]{1,0:T(8,128)S(1)}, f32[448,1536]{1,0:T(8,128)}, u32[]{:S(2)}) copy-start(f32[448,1536]{1,0:T(8,128)} %get-tuple-element.20) | copy-start | bytes 8257540
  225.4 8.4 %copy-start.9 = (f32[448,1536]{1,0:T(8,128)S(1)}, f32[448,1536]{1,0:T(8,128)}, u32[]{:S(2)}) copy-start(f32[448,1536]{1,0:T(8,128)} %get-tuple-element.18) | copy-start | bytes 8257540
  225.4 8.4 %copy-start.11 = (f32[448,1536]{1,0:T(8,128)S(1)}, f32[448,1536]{1,0:T(8,128)}, u32[]{:S(2)}) copy-start(f32[448,1536]{1,0:T(8,128)} %copy-done.10) | copy-start | bytes 8257540
  235.0 19.6 %copy-start.4 = (bf16[448,1536]{1,0:T(8,128)(2,1)}, bf16[448,1536]{1,0:T(8,128)(2,1)S(1)}, u32[]{:S(2)}) copy-start(bf16[448,1536]{1,0:T(8,128)(2,1)S(1)} %get-tuple-element.25) | copy-start | bytes 4128772
  235.0 19.6 %copy-start.6 = (bf16[448,1536]{1,0:T(8,128)(2,1)}, bf16[448,1536]{1,0:T(8,128)(2,1)S(1)}, u32[]{:S(2)}) copy-start(bf16[448,1536]{1,0:T(8,128)(2,1)S(1)} %get-tuple-element.26) | copy-start | bytes 4128772
  254.6 0.8 copy-start.19
  254.7 38.0 %copy-start.7 = (bf16[448,1536]{1,0:T(8,128)(2,1)S(1)}, bf16[448,1536]{1,0:T(8,128)(2,1)}, u32[]{:S(2)}) copy-start(bf16[448,1536]{1,0:T(8,128)(2,1)} %copy-done.6) | copy-start | bytes 4128772
  255.5 38.3 %copy-start.5 = (bf16[448,1536]{1,0:T(8,128)(2,1)S(1)}, bf16[448,1536]{1,0:T(8,128)(2,1)}, u32[]{:S(2)}) copy-start(bf16[448,1536]{1,0:T(8,128)(2,1)} %copy-done.4) | copy-start | bytes 4128772
  290.0 4.9 %copy-start.12 = (f32[16,96,128]{2,1,0:T(8,128)S(1)}, f32[16,96,128]{2,1,0:T(8,128)}, u32[]{:S(2)}) copy-start(f32[16,96,128]{2,1,0:T(8,128)} %shard_map.183) | copy-start | bytes 2359300
  292.7 9.5 %slice-start = ((s8[12582912]{0:T(1024)(128)(4,1)}), s8[4194304]{0:T(1024)(128)(4,1)S(1)}, s32[]{:S(2)}) async-start(s8[12582912]{0:T(1024)(128)(4,1)} %bitcast.96), calls=%async_computation.5 | async-start | bytes 8388608
  294.9 7.3 %slice-start.1 = ((s8[12582912]{0:T(1024)(128)(4,1)}), s8[4194304]{0:T(1024)(128)(4,1)S(1)}, s32[]{:S(2)}) async-start(s8[12582912]{0:T(1024)(128)(4,1)} %bitcast.96), calls=%async_computation.6 | async-start | bytes 8388608
  294.9 7.3 %slice-start.2 = ((s8[12582912]{0:T(1024)(128)(4,1)}), s8[4194304]{0:T(1024)(128)(4,1)S(1)}, s32[]{:S(2)}) async-start(s8[12582912]{0:T(1024)(128)(4,1)} %bitcast.96), calls=%async_computation.7 | async-start | bytes 8388608
  361.4 17.6 %all-to-all-start = ((bf16[96,8,512]{2,0,1:T(8,128)(2,1)}), bf16[96,8,512]{2,0,1:T(8,128)(2,1)S(1)}, u32[]{:S(2)}, u32[]{:S(2)}) async-start(bf16[96,8,512]{2,0,1:T(8,128)(2,1)} %copy.39), calls=%async_computation | async-start | bytes 1572864 | tf_op jit(solution)/shard_map/all_to_all | solution.py:366
  379.5 2.6 copy-start.1
Sparse Core Ops, SparseCore 0:
  35.5 89.7 all-gather.4
  127.5 89.6 all-gather.2
  254.8 104.0 reduce-scatter.3

commit v11 on v10

--- a/solution.py
+++ b/solution.py
@@ -354,9 +354,10 @@
     rows_out, parts, owned_total = rows_backward_parts(x_rows, dy_rows, params)
     packed = rows_out.reshape(shards, capacity, complete_width)
     summed = lax.psum_scatter(packed, "dp", scatter_dimension=0, tiled=True)[0]
-    parts_blocks = jnp.pad(parts, ((0, 0), (0, PART_COLS - 3 * adapter_rank)))
-    parts_mine = reduce_dp(parts_blocks.reshape(shards, capacity, PART_COLS))
-    parts_sum = gather_dp(parts_mine, shards).reshape(shards * capacity, PART_COLS)
+    dense_rows = capacity * 3 * adapter_rank // PART_COLS
+    parts_blocks = parts.reshape(shards, dense_rows, PART_COLS)
+    parts_mine = reduce_dp(parts_blocks)
+    parts_sum = gather_dp(parts_mine, shards).reshape(shards * capacity, 3 * adapter_rank)
     grad_a_pair = ADAPTER_SCALE * contract_pair(parts_sum[:, :2 * adapter_rank], x_rows, 0, 0)
     grad_a_gate = grad_a_pair[:adapter_rank]
     grad_a_up = grad_a_pair[adapter_rank:]

time: 394 us -> 387 us (0.982)
  Pallas kernels: 66.1 us -> 53.7 us
  waiting for transfers between devices: 190 us -> 194 us
    pallas_call x1, Pallas kernels: 21.8 us -> 11.6 us  [gather_dp(): pl.pallas_call(functools.partial(gather_dp_kernel, n), out_shape=jax.Shap...]
  transfers between devices with their start and end apart: 4 -> 4, of which waited for: 4 -> 4; matrix products, arithmetic and copies ran while one was open for 15% -> 15% of each run, Pallas kernels for 12% -> 9%
where the time goes in v11:
time: 387 us; the launch traced here: 382 us
  waiting for transfers between devices  194 us (50%)
  matrix products  82.9 us (21%)
  Pallas kernels  53.7 us (14%)
  local copies, waits for them, and re-layouts  25.8 us (7%)
  between operations  14.5 us (4%)
  starting transfers between devices  5.99 us (2%)
  other arithmetic  4.84 us (1%)
    all_gather x1, waiting for transfers between devices, local(): x_rows = lax.all_gather(x_block, 'dp', axis=0, tiled=True)  65.3 us
    dot_general x17, matrix products, contract_pair(): lax.dot_general(left, right, (((left_axis,), (right_axis,)), ((), ())), p...  63.8 us
    all_gather x1, waiting for transfers between devices, local(): dy_rows = lax.all_gather(dy_block, 'dp', axis=0, tiled=True)  59.3 us
    unnamed x4, waiting for transfers between devices  58 us
    pallas_call x2, Pallas kernels, a2a_expert(): pl.pallas_call(functools.partial(a2a_expert_kernel, n, width), out_shape=...  32.7 us
    dot_general x1, matrix products, rows_backward_parts(): lax.dot_general(lhs, extended, (((0,), (0,)), ((), ())), preferred_elemen...  19 us
    pallas_call x1, Pallas kernels, gather_dp(): pl.pallas_call(functools.partial(gather_dp_kernel, n), out_shape=jax.Shap...  11.6 us
    all_to_all x1, waiting for transfers between devices, local(): lax.all_to_all(summed.reshape(capacity, experts, feat_local), 'expert', s...  11.5 us
  transfers between devices with their start and end apart: 4, of which 4 were waited for; matrix products, arithmetic and copies ran while one was open for 15% of the time, Pallas kernels for 9%

profile of v11, /device:TPU:1, one launch (start us, length us, event | category | flops | bytes accessed | tf_op | source)
XLA Modules:
  0.0 381.8 jit_solution(13971557212225113167)
XLA Ops:
  7.2 0.7 convert_reduce_fusion
  7.9 0.1 copy.34
  8.1 0.2 reduce_window_sum.11
  8.3 0.7 select_reduce_fusion
  9.0 0.7 compare_select_fusion.3
  9.7 0.1 copy.37
  9.8 0.1 reshape.89
  10.0 0.1 reshape.145
  10.1 0.1 reshape.137
  10.3 1.4 scatter_custom_fusion.1
  11.7 1.4 scatter_custom_fusion
  13.1 0.9 concatenate.19
  14.0 3.3 gather_fusion.2
  17.4 18.0 %shard_map.181 = bf16[96,4096]{1,0:T(8,128)(2,1)} custom-call(bf16[8,96,512]{2,1,0:T(8,128)(2,1)} %bitcast.99), custom_call_target="tpu_custom_call" | custom-call | tf_op jit(solution)/shard_map/pallas_call | solution.py:247
  35.4 0.0 all-gather.3.cloned.1.call-start
  35.5 0.1 copy.38
  35.6 0.1 reshape.91
  35.7 5.0 %gather_fusion = f32[768]{0:T(1024)S(1)} fusion(f32[256]{0:T(256)S(1)} %reshape.91, s32[1024]{0:T(1024)S(1)} %get-tuple-element.38), kind=kCustom, calls=%fused_computation | custom fusion | bytes 9216 | tf_op jit(solution)/shard_map/gather | solution.py:339
  40.7 0.1 mul.106
  40.8 2.7 gather_fusion.1
  43.5 1.1 fusion.21.src_ref
  44.7 14.7 %shard_map.180 = bf16[96,4096]{1,0:T(8,128)(2,1)} custom-call(bf16[8,96,512]{2,1,0:T(8,128)(2,1)} %fusion.21.src_ref), custom_call_target="tpu_custom_call" | custom-call | tf_op jit(solution)/shard_map/pallas_call | solution.py:247
  59.4 0.6 reduce-scatter.4.cloned.1.call-start
  60.0 65.3 %all-gather.5.cloned.1.call-done = bf16[1536,4096]{1,0:T(8,128)(2,1)} async-done(((bf16[96,4096]{1,0:T(8,128)(2,1)}), bf16[1536,4096]{1,0:T(8,128)(2,1)}) %all-gather.5.cloned.1.call-update) | async-done | bytes 12582928 | tf_op jit(solution)/shard_map/all_gather | solution.py:351
  125.3 8.1 %convolution_convert_fusion.6 = bf16[1536,16]{0,1:T(8,128)(2,1)S(1)} fusion(bf16[1536,4096]{1,0:T(8,128)(2,1)} %all-gather.5.cloned.1.call-done, bf16[1,16,4096]{2,1,0:T(8,128)(2,1)S(1)} %copy-done.12), kind=kOutput, calls=%fused_computation.42 | convolution fusion | flops 201351168 | bytes 12763136 | tf_op jit(solution)/shard_map/dot_general | solution.py:18
  133.4 0.1 copy-done.2
  133.5 8.0 %fusion.43 = f32[1536,448]{0,1:T(8,128)S(1)} fusion(bf16[1536,4096]{1,0:T(8,128)(2,1)S(1)} %copy-done.2, bf16[1,448,4096]{2,1,0:T(8,128)(2,1)} %param.17), kind=kOutput, calls=%fused_computation.88 | convolution fusion | flops 5637144576 | bytes 19005440 | tf_op jit(solution)/shard_map/dot_general | solution.py:18
  141.5 0.6 fusion.13
  142.0 3.3 convolution_convert_fusion.5
  145.4 6.1 %fusion.41 = f32[1536,448]{0,1:T(8,128)S(1)} fusion(bf16[1536,4096]{1,0:T(8,128)(2,1)S(1)} %copy-done.2, bf16[1,448,4096]{2,1,0:T(8,128)(2,1)S(1)} %copy-done.20), kind=kOutput, calls=%fused_computation.86 | convolution fusion | flops 5637144576 | bytes 19005440 | tf_op jit(solution)/shard_map/dot_general | solution.py:18
  151.5 4.0 %multiply_convert_fusion.2 = (bf16[448,1536]{1,0:T(8,128)(2,1)}, f32[448,1536]{1,0:T(8,128)}, f32[448,1536]{1,0:T(8,128)}, f32[448,1536]{1,0:T(8,128)S(1)}) fusion(f32[448,1536]{1,0:T(8,128)S(1)} %fusion.13, f32[1536,448]{0,1:T(8,128)S(1)} %fusion.41, bf16[1536,16]{0,1:T(8,128)(2,1)S(1)} %convolution_convert_fusion.5, bf16[1,448,16]{1,2,0:T(8,128)(2,1)S(1)} %copy-done.17), kind=kOutput, calls=%fused_computation.35 | convolution fusion | flops 27525120 | bytes 15202304 | tf_op jit(solution)/shard_map/dot_general | solution.py:18
  155.5 1.5 copy-done.10
  157.0 0.9 convolution_convert_fusion.3
  157.9 59.3 %all-gather.3.cloned.1.call-done = bf16[1536,4096]{1,0:T(8,128)(2,1)} async-done(((bf16[96,4096]{1,0:T(8,128)(2,1)}), bf16[1536,4096]{1,0:T(8,128)(2,1)}) %all-gather.3.cloned.1.call-update) | async-done | bytes 12582928 | tf_op jit(solution)/shard_map/all_gather | solution.py:353
  217.2 8.1 %convolution_convert_fusion.4 = bf16[1536,16]{0,1:T(8,128)(2,1)S(1)} fusion(bf16[1536,4096]{1,0:T(8,128)(2,1)} %all-gather.3.cloned.1.call-done, bf16[1,4096,16]{1,2,0:T(8,128)(2,1)S(1)} %copy-done), kind=kOutput, calls=%fused_computation.40 | convolution fusion | flops 201351168 | bytes 12763136 | tf_op jit(solution)/shard_map/dot_general | solution.py:18
  225.3 0.1 copy-done.3
  225.4 8.3 %fusion.8 = f32[1536,448]{0,1:T(8,128)S(1)} fusion(bf16[1536,4096]{1,0:T(8,128)(2,1)S(1)} %copy-done.3, bf16[1,448,4096]{2,1,0:T(8,128)(2,1)} %param.19), kind=kOutput, calls=%fused_computation.17 | convolution fusion | flops 5637144576 | bytes 19005440 | tf_op jit(solution)/shard_map/dot_general | solution.py:18
  233.7 1.3 multiply_convert_fusion.1
  235.0 0.3 convolution_convert_fusion.2
  235.3 0.3 convolution_convert_fusion.1
  235.7 19.0 %convolution_convert_fusion = bf16[1536,4096]{1,0:T(8,128)(2,1)} fusion(bf16[16,4096]{1,0:T(8,128)(2,1)S(1)} %get-tuple-element.39, bf16[16,4096]{1,0:T(8,128)(2,1)S(1)} %get-tuple-element.40, bf16[448,4096]{1,0:T(8,128)(2,1)} %bitcast.106, bf16[448,4096]{1,0:T(8,128)(2,1)} %bitcast.107, bf16[32,1536]{1,0:T(8,128)(2,1)S(1)} %maximum_bitcast_fusion, ...), kind=kOutput, calls=%fused_computation.6 | convolution fusion | flops 11722194944 | bytes 23035904 | tf_op jit(solution)/shard_map/dot_general | solution.py:170
  254.7 0.1 copy.41
  254.9 0.1 reshape.127
  255.0 0.2 copy.42
  255.3 1.2 reshape.96.src_ref
  256.5 9.4 %shard_map.182.src_ref = f32[36,128]{1,0:T(8,128)} custom-call(bf16[16,36,128]{2,1,0:T(8,128)(2,1)} %reshape.96.src_ref), custom_call_target="tpu_custom_call" | custom-call | tf_op jit(solution)/shard_map/pallas_call | solution.py:285
  265.9 11.6 %shard_map.183 = f32[16,36,128]{2,1,0:T(8,128)} custom-call(f32[36,128]{1,0:T(8,128)} %shard_map.182.src_ref), custom_call_target="tpu_custom_call" | custom-call | tf_op jit(solution)/shard_map/pallas_call | solution.py:208
  277.6 1.3 reshape.97
  278.9 2.5 fusion.22
  281.4 1.1 fusion.23
  282.5 1.1 fusion.24
  283.6 7.5 %convolution_multiply_fusion = f32[32,4096]{1,0:T(8,128)S(1)} fusion(bf16[1536,4096]{1,0:T(8,128)(2,1)} %all-gather.5.cloned.1.call-done, bf16[1536,48]{1,0:T(8,128)(2,1)S(1)} %reshape.97), kind=kOutput, calls=%fused_computation.14 | convolution fusion | flops 402784256 | bytes 13254656 | tf_op jit(solution)/shard_map/dot_general | solution.py:18
  291.1 0.2 slice-done.2
  291.3 2.6 fusion.7
  293.8 58.0 %reduce-scatter.4.cloned.1.call-done = bf16[1,96,4096]{2,1,0:T(8,128)(2,1)} async-done(((bf16[16,96,4096]{2,1,0:T(8,128)(2,1)}), bf16[1,96,4096]{2,1,0:T(8,128)(2,1)}) %reduce-scatter.4.cloned.1.call-update) | async-done | bytes 786448
  351.8 1.4 copy.43
  353.2 1.1 copy.39
  354.3 5.3 %all-to-all-start = ((bf16[96,8,512]{2,0,1:T(8,128)(2,1)}), bf16[96,8,512]{2,0,1:T(8,128)(2,1)S(1)}, u32[]{:S(2)}, u32[]{:S(2)}) async-start(bf16[96,8,512]{2,0,1:T(8,128)(2,1)} %copy.39), calls=%async_computation | async-start | bytes 1572864 | tf_op jit(solution)/shard_map/all_to_all | solution.py:367
  359.7 0.8 slice_bitcast_fusion
  360.5 11.5 %all-to-all-done = bf16[96,8,512]{2,0,1:T(8,128)(2,1)S(1)} async-done(((bf16[96,8,512]{2,0,1:T(8,128)(2,1)}), bf16[96,8,512]{2,0,1:T(8,128)(2,1)S(1)}, u32[]{:S(2)}, u32[]{:S(2)}) %all-to-all-start) | async-done | bytes 786464 | tf_op jit(solution)/shard_map/all_to_all | solution.py:367
  371.9 0.5 copy.45
  372.4 1.0 gather_fusion.3
  373.4 0.3 reshape.130
  373.7 1.3 reduce_sum.29
  (62 shorter events, 0.4 us)
Async XLA Ops:
  7.2 210.0 %copy-start = (bf16[1,4096,16]{1,2,0:T(8,128)(2,1)S(1)}, bf16[1,4096,16]{1,2,0:T(8,128)(2,1)}, u32[]{:S(2)}) copy-start(bf16[1,4096,16]{1,2,0:T(8,128)(2,1)} %param.25) | copy-start | bytes 393220
  7.2 118.1 %all-gather.5.cloned.1.call-start = ((), (), s32[]{:S(2)}) async-start(), calls=%async_computation.3 | async-start | bytes 13369344 | tf_op jit(solution)/shard_map/all_gather | solution.py:351
  14.0 21.4 %copy-start.19 = (f32[128,2]{0,1:T(2,128)S(1)}, f32[128,2]{0,1:T(2,128)}, u32[]{:S(2)}) copy-start(f32[128,2]{0,1:T(2,128)} %param.16) | copy-start | bytes 3076
  35.4 5.4 %copy-start.15 = (bf16[128,512]{1,0:T(8,128)(2,1)S(1)}, bf16[128,512]{1,0:T(8,128)(2,1)}, u32[]{:S(2)}) copy-start(bf16[128,512]{1,0:T(8,128)(2,1)} %param.14) | copy-start | bytes 393220
  35.4 181.8 %all-gather.3.cloned.1.call-start = ((), (), s32[]{:S(2)}) async-start(), calls=%async_computation.2 | async-start | bytes 13369344 | tf_op jit(solution)/shard_map/all_gather | solution.py:353
  43.5 16.4 %copy-start.12 = (bf16[1,16,4096]{2,1,0:T(8,128)(2,1)S(1)}, bf16[1,16,4096]{2,1,0:T(8,128)(2,1)}, u32[]{:S(2)}) copy-start(bf16[1,16,4096]{2,1,0:T(8,128)(2,1)} %param.20) | copy-start | bytes 393220
  43.5 16.4 %copy-start.13 = (bf16[1,16,4096]{2,1,0:T(8,128)(2,1)S(1)}, bf16[1,16,4096]{2,1,0:T(8,128)(2,1)}, u32[]{:S(2)}) copy-start(bf16[1,16,4096]{2,1,0:T(8,128)(2,1)} %param.22) | copy-start | bytes 393220
  59.4 292.4 %reduce-scatter.4.cloned.1.call-start = ((), (), s32[]{:S(2)}) async-start(), calls=%async_computation.4 | async-start | bytes 13369344
  125.3 8.2 %copy-start.2 = (bf16[1536,4096]{1,0:T(8,128)(2,1)S(1)}, bf16[1536,4096]{1,0:T(8,128)(2,1)}, u32[]{:S(2)}) copy-start(bf16[1536,4096]{1,0:T(8,128)(2,1)} %all-gather.5.cloned.1.call-done) | copy-start | bytes 37748740
  133.5 8.0 %copy-start.16 = (bf16[1,448,16]{1,2,0:T(8,128)(2,1)S(1)}, bf16[1,448,16]{1,2,0:T(8,128)(2,1)}, u32[]{:S(2)}) copy-start(bf16[1,448,16]{1,2,0:T(8,128)(2,1)} %param.21) | copy-start | bytes 43012
  142.0 3.4 copy-start.20
  145.4 6.1 %copy-start.17 = (bf16[1,448,16]{1,2,0:T(8,128)(2,1)S(1)}, bf16[1,448,16]{1,2,0:T(8,128)(2,1)}, u32[]{:S(2)}) copy-start(bf16[1,448,16]{1,2,0:T(8,128)(2,1)} %param.23) | copy-start | bytes 43012
  151.5 5.5 %copy-start.18 = (bf16[1,16,448]{2,1,0:T(8,128)(2,1)S(1)}, bf16[1,16,448]{2,1,0:T(8,128)(2,1)}, u32[]{:S(2)}) copy-start(bf16[1,16,448]{2,1,0:T(8,128)(2,1)} %param.24) | copy-start | bytes 43012
  155.5 1.5 copy-start.10
  217.2 8.2 %copy-start.3 = (bf16[1536,4096]{1,0:T(8,128)(2,1)S(1)}, bf16[1536,4096]{1,0:T(8,128)(2,1)}, u32[]{:S(2)}) copy-start(bf16[1536,4096]{1,0:T(8,128)(2,1)} %all-gather.3.cloned.1.call-done) | copy-start | bytes 37748740
  225.3 8.3 %copy-start.14 = (bf16[1536,16]{0,1:T(8,128)(2,1)}, bf16[1536,16]{0,1:T(8,128)(2,1)S(1)}, u32[]{:S(2)}) copy-start(bf16[1536,16]{0,1:T(8,128)(2,1)S(1)} %convolution_convert_fusion.4) | copy-start | bytes 147460
  225.3 8.3 %copy-start.8 = (f32[448,1536]{1,0:T(8,128)S(1)}, f32[448,1536]{1,0:T(8,128)}, u32[]{:S(2)}) copy-start(f32[448,1536]{1,0:T(8,128)} %get-tuple-element.20) | copy-start | bytes 8257540
  225.4 8.4 %copy-start.9 = (f32[448,1536]{1,0:T(8,128)S(1)}, f32[448,1536]{1,0:T(8,128)}, u32[]{:S(2)}) copy-start(f32[448,1536]{1,0:T(8,128)} %get-tuple-element.18) | copy-start | bytes 8257540
  225.4 8.4 %copy-start.11 = (f32[448,1536]{1,0:T(8,128)S(1)}, f32[448,1536]{1,0:T(8,128)}, u32[]{:S(2)}) copy-start(f32[448,1536]{1,0:T(8,128)} %copy-done.10) | copy-start | bytes 8257540
  235.0 19.7 %copy-start.4 = (bf16[448,1536]{1,0:T(8,128)(2,1)}, bf16[448,1536]{1,0:T(8,128)(2,1)S(1)}, u32[]{:S(2)}) copy-start(bf16[448,1536]{1,0:T(8,128)(2,1)S(1)} %get-tuple-element.25) | copy-start | bytes 4128772
  235.0 19.7 %copy-start.6 = (bf16[448,1536]{1,0:T(8,128)(2,1)}, bf16[448,1536]{1,0:T(8,128)(2,1)S(1)}, u32[]{:S(2)}) copy-start(bf16[448,1536]{1,0:T(8,128)(2,1)S(1)} %get-tuple-element.26) | copy-start | bytes 4128772
  254.7 26.6 %copy-start.7 = (bf16[448,1536]{1,0:T(8,128)(2,1)S(1)}, bf16[448,1536]{1,0:T(8,128)(2,1)}, u32[]{:S(2)}) copy-start(bf16[448,1536]{1,0:T(8,128)(2,1)} %copy-done.6) | copy-start | bytes 4128772
  255.0 27.5 %copy-start.5 = (bf16[448,1536]{1,0:T(8,128)(2,1)S(1)}, bf16[448,1536]{1,0:T(8,128)(2,1)}, u32[]{:S(2)}) copy-start(bf16[448,1536]{1,0:T(8,128)(2,1)} %copy-done.4) | copy-start | bytes 4128772
  281.4 9.7 %slice-start = ((s8[12582912]{0:T(1024)(128)(4,1)}), s8[4194304]{0:T(1024)(128)(4,1)S(1)}, s32[]{:S(2)}) async-start(s8[12582912]{0:T(1024)(128)(4,1)} %bitcast.94), calls=%async_computation.5 | async-start | bytes 8388608
  283.6 7.5 %slice-start.1 = ((s8[12582912]{0:T(1024)(128)(4,1)}), s8[4194304]{0:T(1024)(128)(4,1)S(1)}, s32[]{:S(2)}) async-start(s8[12582912]{0:T(1024)(128)(4,1)} %bitcast.94), calls=%async_computation.6 | async-start | bytes 8388608
  283.6 7.7 %slice-start.2 = ((s8[12582912]{0:T(1024)(128)(4,1)}), s8[4194304]{0:T(1024)(128)(4,1)S(1)}, s32[]{:S(2)}) async-start(s8[12582912]{0:T(1024)(128)(4,1)} %bitcast.94), calls=%async_computation.7 | async-start | bytes 8388608
  354.3 17.6 %all-to-all-start = ((bf16[96,8,512]{2,0,1:T(8,128)(2,1)}), bf16[96,8,512]{2,0,1:T(8,128)(2,1)S(1)}, u32[]{:S(2)}, u32[]{:S(2)}) async-start(bf16[96,8,512]{2,0,1:T(8,128)(2,1)} %copy.39), calls=%async_computation | async-start | bytes 1572864 | tf_op jit(solution)/shard_map/all_to_all | solution.py:367
  372.4 2.6 copy-start.1
Sparse Core Ops, SparseCore 0:
  35.5 89.7 all-gather.4
  127.5 89.6 all-gather.2
  254.8 96.8 reduce-scatter.3

commit v12 on v11

--- a/solution.py
+++ b/solution.py
@@ -143,10 +143,14 @@
             up_projected_lower,
         )
     )
-    down_projected_lower = contract_pair(b_down, output_gradient_rows, 0, 1).astype(jnp.bfloat16)
-    hidden_gradient = contract_pair(
-        down_weight, output_gradient_rows, 1, 1
-    ) + ADAPTER_SCALE * contract_pair(down_adapter_lower, down_projected_lower, 0, 0)
+    hidden_here = down_weight.shape[0]
+    down_both = contract_pair(
+        jnp.concatenate([down_weight, b_down.T], 0), output_gradient_rows, 1, 1
+    )
+    down_projected_lower = down_both[hidden_here:].astype(jnp.bfloat16)
+    hidden_gradient = down_both[:hidden_here] + ADAPTER_SCALE * contract_pair(
+        down_adapter_lower, down_projected_lower, 0, 0
+    )
     gate_gradient = (
         hidden_gradient
         * up_preactivation

time: 387 us -> 383 us (0.990)
  waiting for transfers between devices: 194 us -> 183 us
  matrix products: 82.9 us -> 90.5 us
    all_gather x1, waiting for transfers between devices: 59.3 us -> 48.2 us  [local(): dy_rows = lax.all_gather(dy_block, 'dp', axis=0, tiled=True)]
    dot_general x17 -> x16, matrix products: 63.8 us -> 71.9 us  [contract_pair(): lax.dot_general(left, right, (((left_axis,), (right_axis,)), ((), ())), p...]
  transfers between devices with their start and end apart: 4 -> 4, of which waited for: 4 -> 4; matrix products, arithmetic and copies ran while one was open for 15% -> 18% of each run, Pallas kernels for 9% -> 9%
where the time goes in v12:
time: 383 us; the launch traced here: 378 us
  waiting for transfers between devices  183 us (48%)
  matrix products  90.5 us (24%)
  Pallas kernels  53.6 us (14%)
  local copies, waits for them, and re-layouts  25.8 us (7%)
  between operations  14.4 us (4%)
  starting transfers between devices  5.77 us (2%)
  other arithmetic  4.8 us (1%)
    dot_general x16, matrix products, contract_pair(): lax.dot_general(left, right, (((left_axis,), (right_axis,)), ((), ())), p...  71.9 us
    all_gather x1, waiting for transfers between devices, local(): x_rows = lax.all_gather(x_block, 'dp', axis=0, tiled=True)  65.5 us
    unnamed x4, waiting for transfers between devices  57.9 us
    all_gather x1, waiting for transfers between devices, local(): dy_rows = lax.all_gather(dy_block, 'dp', axis=0, tiled=True)  48.2 us
    pallas_call x2, Pallas kernels, a2a_expert(): pl.pallas_call(functools.partial(a2a_expert_kernel, n, width), out_shape=...  32.6 us
    dot_general x1, matrix products, rows_backward_parts(): lax.dot_general(lhs, extended, (((0,), (0,)), ((), ())), preferred_elemen...  18.6 us
    pallas_call x1, Pallas kernels, gather_dp(): pl.pallas_call(functools.partial(gather_dp_kernel, n), out_shape=jax.Shap...  11.6 us
    all_to_all x1, waiting for transfers between devices, local(): lax.all_to_all(summed.reshape(capacity, experts, feat_local), 'expert', s...  11.5 us
  transfers between devices with their start and end apart: 4, of which 4 were waited for; matrix products, arithmetic and copies ran while one was open for 18% of the time, Pallas kernels for 9%

profile of v12, /device:TPU:1, one launch (start us, length us, event | category | flops | bytes accessed | tf_op | source)
XLA Modules:
  0.0 377.9 jit_solution(15529369310140934652)
XLA Ops:
  7.2 0.0 all-gather.5.cloned.1.call-start
  7.2 0.7 convert_reduce_fusion
  7.9 0.1 copy.34
  8.0 0.2 reduce_window_sum.11
  8.3 0.7 select_reduce_fusion
  9.0 0.7 compare_select_fusion.3
  9.7 0.1 copy.37
  9.8 0.1 reshape.89
  9.9 0.1 reshape.137
  10.1 0.1 reshape.145
  10.2 1.4 scatter_custom_fusion.1
  11.6 1.4 scatter_custom_fusion
  13.1 0.9 concatenate.23
  14.0 3.3 gather_fusion.2
  17.3 18.0 %shard_map.181 = bf16[96,4096]{1,0:T(8,128)(2,1)} custom-call(bf16[8,96,512]{2,1,0:T(8,128)(2,1)} %bitcast.94), custom_call_target="tpu_custom_call" | custom-call | tf_op jit(solution)/shard_map/pallas_call | solution.py:251
  35.4 0.0 all-gather.3.cloned.1.call-start
  35.4 0.1 copy.38
  35.5 0.1 reshape.91
  35.7 5.0 %gather_fusion = f32[768]{0:T(1024)S(1)} fusion(f32[256]{0:T(256)S(1)} %reshape.91, s32[1024]{0:T(1024)S(1)} %get-tuple-element.38), kind=kCustom, calls=%fused_computation | custom fusion | bytes 9216 | tf_op jit(solution)/shard_map/gather | solution.py:343
  40.7 0.1 mul.108
  40.8 2.7 gather_fusion.1
  43.5 1.1 fusion.23.src_ref
  44.6 14.7 %shard_map.180 = bf16[96,4096]{1,0:T(8,128)(2,1)} custom-call(bf16[8,96,512]{2,1,0:T(8,128)(2,1)} %fusion.23.src_ref), custom_call_target="tpu_custom_call" | custom-call | tf_op jit(solution)/shard_map/pallas_call | solution.py:251
  59.3 0.0 all-gather.3.cloned.1.call-update
  59.3 0.4 reduce-scatter.4.cloned.1.call-start
  59.8 65.5 %all-gather.5.cloned.1.call-done = bf16[1536,4096]{1,0:T(8,128)(2,1)} async-done(((bf16[96,4096]{1,0:T(8,128)(2,1)}), bf16[1536,4096]{1,0:T(8,128)(2,1)}) %all-gather.5.cloned.1.call-update) | async-done | bytes 12582928 | tf_op jit(solution)/shard_map/all_gather | solution.py:355
  125.3 8.1 %convolution_convert_fusion.5 = bf16[1536,16]{0,1:T(8,128)(2,1)S(1)} fusion(bf16[1536,4096]{1,0:T(8,128)(2,1)} %all-gather.5.cloned.1.call-done, bf16[1,16,4096]{2,1,0:T(8,128)(2,1)S(1)} %copy-done.11), kind=kOutput, calls=%fused_computation.43 | convolution fusion | flops 201351168 | bytes 12763136 | tf_op jit(solution)/shard_map/dot_general | solution.py:18
  133.3 0.1 copy-done.1
  133.4 8.0 %fusion.45 = f32[1536,448]{0,1:T(8,128)S(1)} fusion(bf16[1536,4096]{1,0:T(8,128)(2,1)S(1)} %copy-done.1, bf16[1,448,4096]{2,1,0:T(8,128)(2,1)} %param.17), kind=kOutput, calls=%fused_computation.90 | convolution fusion | flops 5637144576 | bytes 19005440 | tf_op jit(solution)/shard_map/dot_general | solution.py:18
  141.4 0.6 fusion.14
  142.0 3.3 convolution_convert_fusion.4
  145.3 17.2 %fusion.43 = f32[1536,448]{0,1:T(8,128)S(1)} fusion(bf16[1536,4096]{1,0:T(8,128)(2,1)S(1)} %copy-done.1, bf16[1,448,4096]{2,1,0:T(8,128)(2,1)S(1)} %copy-done.17), kind=kOutput, calls=%fused_computation.88 | convolution fusion | flops 5637144576 | bytes 19005440 | tf_op jit(solution)/shard_map/dot_general | solution.py:18
  162.5 4.0 %multiply_convert_fusion.2 = (bf16[448,1536]{1,0:T(8,128)(2,1)}, f32[448,1536]{1,0:T(8,128)}, f32[448,1536]{1,0:T(8,128)}, f32[448,1536]{1,0:T(8,128)S(1)}) fusion(f32[448,1536]{1,0:T(8,128)S(1)} %fusion.14, f32[1536,448]{0,1:T(8,128)S(1)} %fusion.43, bf16[1536,16]{0,1:T(8,128)(2,1)S(1)} %convolution_convert_fusion.4, bf16[1,448,16]{1,2,0:T(8,128)(2,1)S(1)} %copy-done), kind=kOutput, calls=%fused_computation.37 | convolution fusion | flops 27525120 | bytes 15202304 | tf_op jit(solution)/shard_map/dot_general | solution.py:18
  166.6 1.5 copy-done.8
  168.0 0.9 convolution_convert_fusion.3
  168.9 48.2 %all-gather.3.cloned.1.call-done = bf16[1536,4096]{1,0:T(8,128)(2,1)} async-done(((bf16[96,4096]{1,0:T(8,128)(2,1)}), bf16[1536,4096]{1,0:T(8,128)(2,1)}) %all-gather.3.cloned.1.call-update) | async-done | bytes 12582928 | tf_op jit(solution)/shard_map/all_gather | solution.py:357
  217.1 11.5 %fusion.8 = f32[464,1536]{1,0:T(8,128)} fusion(bf16[1536,4096]{1,0:T(8,128)(2,1)} %all-gather.3.cloned.1.call-done, bf16[16,4096]{1,0:T(8,128)(2,1)} %bitcast.104, bf16[448,4096]{1,0:T(8,128)(2,1)} %bitcast.101), kind=kOutput, calls=%fused_computation.17 | convolution fusion | flops 5846073344 | bytes 19234816 | tf_op jit(solution)/shard_map/dot_general | solution.py:18
  228.7 3.1 multiply_convert_fusion.1
  231.9 0.3 convolution_convert_fusion.1
  232.2 0.3 convolution_convert_fusion.2
  232.5 18.6 %convolution_convert_fusion = bf16[1536,4096]{1,0:T(8,128)(2,1)} fusion(bf16[16,4096]{1,0:T(8,128)(2,1)S(1)} %get-tuple-element.39, bf16[16,4096]{1,0:T(8,128)(2,1)S(1)} %get-tuple-element.40, bf16[448,4096]{1,0:T(8,128)(2,1)} %bitcast.102, bf16[448,4096]{1,0:T(8,128)(2,1)} %bitcast.103, bf16[32,1536]{1,0:T(8,128)(2,1)S(1)} %maximum_bitcast_fusion, ...), kind=kOutput, calls=%fused_computation.6 | convolution fusion | flops 11722194944 | bytes 23035904 | tf_op jit(solution)/shard_map/dot_general | solution.py:174
  251.1 0.1 copy.41
  251.2 0.1 reshape.127
  251.4 0.2 copy.42
  251.6 1.2 reshape.96.src_ref
  252.9 9.4 %shard_map.182.src_ref = f32[36,128]{1,0:T(8,128)} custom-call(bf16[16,36,128]{2,1,0:T(8,128)(2,1)} %reshape.96.src_ref), custom_call_target="tpu_custom_call" | custom-call | tf_op jit(solution)/shard_map/pallas_call | solution.py:289
  262.3 11.6 %shard_map.183 = f32[16,36,128]{2,1,0:T(8,128)} custom-call(f32[36,128]{1,0:T(8,128)} %shard_map.182.src_ref), custom_call_target="tpu_custom_call" | custom-call | tf_op jit(solution)/shard_map/pallas_call | solution.py:212
  273.9 1.3 reshape.97
  275.3 1.1 fusion.25
  276.4 1.1 fusion.26
  277.5 2.3 fusion.24
  279.8 7.5 %convolution_multiply_fusion = f32[32,4096]{1,0:T(8,128)S(1)} fusion(bf16[1536,4096]{1,0:T(8,128)(2,1)} %all-gather.5.cloned.1.call-done, bf16[1536,48]{1,0:T(8,128)(2,1)S(1)} %reshape.97), kind=kOutput, calls=%fused_computation.14 | convolution fusion | flops 402784256 | bytes 13254656 | tf_op jit(solution)/shard_map/dot_general | solution.py:18
  287.3 0.2 slice-done.2
  287.6 2.6 fusion.7
  290.1 57.9 %reduce-scatter.4.cloned.1.call-done = bf16[1,96,4096]{2,1,0:T(8,128)(2,1)} async-done(((bf16[16,96,4096]{2,1,0:T(8,128)(2,1)}), bf16[1,96,4096]{2,1,0:T(8,128)(2,1)}) %reduce-scatter.4.cloned.1.call-update) | async-done | bytes 786448
  348.0 1.4 copy.43
  349.4 1.1 copy.39
  350.5 5.3 %all-to-all-start = ((bf16[96,8,512]{2,0,1:T(8,128)(2,1)}), bf16[96,8,512]{2,0,1:T(8,128)(2,1)S(1)}, u32[]{:S(2)}, u32[]{:S(2)}) async-start(bf16[96,8,512]{2,0,1:T(8,128)(2,1)} %copy.39), calls=%async_computation | async-start | bytes 1572864 | tf_op jit(solution)/shard_map/all_to_all | solution.py:371
  355.8 0.8 slice_bitcast_fusion
  356.6 11.5 %all-to-all-done = bf16[96,8,512]{2,0,1:T(8,128)(2,1)S(1)} async-done(((bf16[96,8,512]{2,0,1:T(8,128)(2,1)}), bf16[96,8,512]{2,0,1:T(8,128)(2,1)S(1)}, u32[]{:S(2)}, u32[]{:S(2)}) %all-to-all-start) | async-done | bytes 786464 | tf_op jit(solution)/shard_map/all_to_all | solution.py:371
  368.1 0.5 copy.45
  368.5 1.0 gather_fusion.3
  369.5 0.3 reshape.130
  369.8 1.3 reduce_sum.29
  (55 shorter events, 0.3 us)
Async XLA Ops:
  7.2 155.3 %copy-start = (bf16[1,448,16]{1,2,0:T(8,128)(2,1)S(1)}, bf16[1,448,16]{1,2,0:T(8,128)(2,1)}, u32[]{:S(2)}) copy-start(bf16[1,448,16]{1,2,0:T(8,128)(2,1)} %param.23) | copy-start | bytes 43012
  7.2 118.1 %all-gather.5.cloned.1.call-start = ((), (), s32[]{:S(2)}) async-start(), calls=%async_computation.3 | async-start | bytes 13369344 | tf_op jit(solution)/shard_map/all_gather | solution.py:355
  14.0 21.4 %copy-start.16 = (f32[128,2]{0,1:T(2,128)S(1)}, f32[128,2]{0,1:T(2,128)}, u32[]{:S(2)}) copy-start(f32[128,2]{0,1:T(2,128)} %param.16) | copy-start | bytes 3076
  35.3 5.4 %copy-start.13 = (bf16[128,512]{1,0:T(8,128)(2,1)S(1)}, bf16[128,512]{1,0:T(8,128)(2,1)}, u32[]{:S(2)}) copy-start(bf16[128,512]{1,0:T(8,128)(2,1)} %param.14) | copy-start | bytes 393220
  35.4 181.8 %all-gather.3.cloned.1.call-start = ((), (), s32[]{:S(2)}) async-start(), calls=%async_computation.2 | async-start | bytes 13369344 | tf_op jit(solution)/shard_map/all_gather | solution.py:357
  43.5 16.3 %copy-start.11 = (bf16[1,16,4096]{2,1,0:T(8,128)(2,1)S(1)}, bf16[1,16,4096]{2,1,0:T(8,128)(2,1)}, u32[]{:S(2)}) copy-start(bf16[1,16,4096]{2,1,0:T(8,128)(2,1)} %param.20) | copy-start | bytes 393220
  43.5 16.3 %copy-start.12 = (bf16[1,16,4096]{2,1,0:T(8,128)(2,1)S(1)}, bf16[1,16,4096]{2,1,0:T(8,128)(2,1)}, u32[]{:S(2)}) copy-start(bf16[1,16,4096]{2,1,0:T(8,128)(2,1)} %param.22) | copy-start | bytes 393220
  59.3 288.7 %reduce-scatter.4.cloned.1.call-start = ((), (), s32[]{:S(2)}) async-start(), calls=%async_computation.4 | async-start | bytes 13369344
  125.3 8.2 %copy-start.1 = (bf16[1536,4096]{1,0:T(8,128)(2,1)S(1)}, bf16[1536,4096]{1,0:T(8,128)(2,1)}, u32[]{:S(2)}) copy-start(bf16[1536,4096]{1,0:T(8,128)(2,1)} %all-gather.5.cloned.1.call-done) | copy-start | bytes 37748740
  133.4 8.0 %copy-start.14 = (bf16[1,448,16]{1,2,0:T(8,128)(2,1)S(1)}, bf16[1,448,16]{1,2,0:T(8,128)(2,1)}, u32[]{:S(2)}) copy-start(bf16[1,448,16]{1,2,0:T(8,128)(2,1)} %param.21) | copy-start | bytes 43012
  142.0 3.4 copy-start.17
  162.5 5.5 %copy-start.15 = (bf16[1,16,448]{2,1,0:T(8,128)(2,1)S(1)}, bf16[1,16,448]{2,1,0:T(8,128)(2,1)}, u32[]{:S(2)}) copy-start(bf16[1,16,448]{2,1,0:T(8,128)(2,1)} %param.24) | copy-start | bytes 43012
  166.5 1.5 copy-start.8
  217.1 11.6 %copy-start.6 = (f32[448,1536]{1,0:T(8,128)S(1)}, f32[448,1536]{1,0:T(8,128)}, u32[]{:S(2)}) copy-start(f32[448,1536]{1,0:T(8,128)} %get-tuple-element.20) | copy-start | bytes 8257540
  217.1 11.6 %copy-start.7 = (f32[448,1536]{1,0:T(8,128)S(1)}, f32[448,1536]{1,0:T(8,128)}, u32[]{:S(2)}) copy-start(f32[448,1536]{1,0:T(8,128)} %get-tuple-element.18) | copy-start | bytes 8257540
  217.1 11.6 %copy-start.9 = (f32[448,1536]{1,0:T(8,128)S(1)}, f32[448,1536]{1,0:T(8,128)}, u32[]{:S(2)}) copy-start(f32[448,1536]{1,0:T(8,128)} %copy-done.8) | copy-start | bytes 8257540
  231.9 19.2 %copy-start.2 = (bf16[448,1536]{1,0:T(8,128)(2,1)}, bf16[448,1536]{1,0:T(8,128)(2,1)S(1)}, u32[]{:S(2)}) copy-start(bf16[448,1536]{1,0:T(8,128)(2,1)S(1)} %get-tuple-element.25) | copy-start | bytes 4128772
  231.9 19.2 %copy-start.4 = (bf16[448,1536]{1,0:T(8,128)(2,1)}, bf16[448,1536]{1,0:T(8,128)(2,1)S(1)}, u32[]{:S(2)}) copy-start(bf16[448,1536]{1,0:T(8,128)(2,1)S(1)} %get-tuple-element.26) | copy-start | bytes 4128772
  251.1 24.1 %copy-start.5 = (bf16[448,1536]{1,0:T(8,128)(2,1)S(1)}, bf16[448,1536]{1,0:T(8,128)(2,1)}, u32[]{:S(2)}) copy-start(bf16[448,1536]{1,0:T(8,128)(2,1)} %copy-done.4) | copy-start | bytes 4128772
  251.1 25.2 %copy-start.3 = (bf16[448,1536]{1,0:T(8,128)(2,1)S(1)}, bf16[448,1536]{1,0:T(8,128)(2,1)}, u32[]{:S(2)}) copy-start(bf16[448,1536]{1,0:T(8,128)(2,1)} %copy-done.2) | copy-start | bytes 4128772
  275.3 2.2 copy-start.10
  276.4 10.9 %slice-start = ((s8[12582912]{0:T(1024)(128)(4,1)}), s8[4194304]{0:T(1024)(128)(4,1)S(1)}, s32[]{:S(2)}) async-start(s8[12582912]{0:T(1024)(128)(4,1)} %bitcast.90), calls=%async_computation.5 | async-start | bytes 8388608
  279.8 7.5 %slice-start.1 = ((s8[12582912]{0:T(1024)(128)(4,1)}), s8[4194304]{0:T(1024)(128)(4,1)S(1)}, s32[]{:S(2)}) async-start(s8[12582912]{0:T(1024)(128)(4,1)} %bitcast.90), calls=%async_computation.6 | async-start | bytes 8388608
  279.8 7.7 %slice-start.2 = ((s8[12582912]{0:T(1024)(128)(4,1)}), s8[4194304]{0:T(1024)(128)(4,1)S(1)}, s32[]{:S(2)}) async-start(s8[12582912]{0:T(1024)(128)(4,1)} %bitcast.90), calls=%async_computation.7 | async-start | bytes 8388608
  350.5 17.6 %all-to-all-start = ((bf16[96,8,512]{2,0,1:T(8,128)(2,1)}), bf16[96,8,512]{2,0,1:T(8,128)(2,1)S(1)}, u32[]{:S(2)}, u32[]{:S(2)}) async-start(bf16[96,8,512]{2,0,1:T(8,128)(2,1)} %copy.39), calls=%async_computation | async-start | bytes 1572864 | tf_op jit(solution)/shard_map/all_to_all | solution.py:371
Sparse Core Ops, SparseCore 0:
  35.5 89.7 all-gather.4
  127.5 89.6 all-gather.2
  251.2 96.7 reduce-scatter.3

commit v13 on v12

--- a/solution.py
+++ b/solution.py
@@ -368,12 +368,8 @@
     grad_b_down = ADAPTER_SCALE * contract_pair(
         dy_rows, parts_sum[:, 2 * adapter_rank:3 * adapter_rank], 0, 0
     )
-    returned_rows = lax.all_to_all(
-        summed.reshape(capacity, experts, feat_local),
-        "expert",
-        split_axis=1,
-        concat_axis=1,
-        tiled=True,
+    returned_rows = a2a_expert(
+        summed.reshape(capacity, experts, feat_local).transpose(1, 0, 2), 4
     ).astype(jnp.float32)
     lookup = positions * experts + routing
     grad_x = jnp.sum(returned_rows.reshape(capacity * experts, feat_local)[lookup], axis=1).astype(

time: 383 us -> 382 us (level)
  Pallas kernels: 53.6 us -> 69.8 us
  waiting for transfers between devices: 183 us -> 171 us
  starting transfers between devices: 5.77 us -> 0.5 us
    pallas_call x2 -> x3, Pallas kernels: 32.6 us -> 48.8 us  [a2a_expert(): pl.pallas_call(functools.partial(a2a_expert_kernel, n, width), out_shape=...]
    all_to_all x1 -> x0, waiting for transfers between devices: 11.5 us -> none  [local(): lax.all_to_all(summed.reshape(capacity, experts, feat_local), 'expert', s...]
    all_to_all x1 -> x0, starting transfers between devices: 5.28 us -> none  [local(): lax.all_to_all(summed.reshape(capacity, experts, feat_local), 'expert', s...]
  transfers between devices with their start and end apart: 4 -> 3, of which waited for: 4 -> 3; matrix products, arithmetic and copies ran while one was open for 18% -> 18% of each run, Pallas kernels for 9% -> 9%
where the time goes in v13:
time: 382 us; the launch traced here: 377 us
  waiting for transfers between devices  171 us (45%)
  matrix products  90.3 us (24%)
  Pallas kernels  69.8 us (18%)
  local copies, waits for them, and re-layouts  26.5 us (7%)
  between operations  14.4 us (4%)
  other arithmetic  4.79 us (1%)
    dot_general x16, matrix products, contract_pair(): lax.dot_general(left, right, (((left_axis,), (right_axis,)), ((), ())), p...  71.8 us
    all_gather x1, waiting for transfers between devices, local(): x_rows = lax.all_gather(x_block, 'dp', axis=0, tiled=True)  65.5 us
    unnamed x4, waiting for transfers between devices  57.5 us
    pallas_call x3, Pallas kernels, a2a_expert(): pl.pallas_call(functools.partial(a2a_expert_kernel, n, width), out_shape=...  48.8 us
    all_gather x1, waiting for transfers between devices, local(): dy_rows = lax.all_gather(dy_block, 'dp', axis=0, tiled=True)  48.2 us
    dot_general x1, matrix products, rows_backward_parts(): lax.dot_general(lhs, extended, (((0,), (0,)), ((), ())), preferred_elemen...  18.5 us
    pallas_call x1, Pallas kernels, gather_dp(): pl.pallas_call(functools.partial(gather_dp_kernel, n), out_shape=jax.Shap...  11.6 us
    pallas_call x1, Pallas kernels, reduce_dp(): pl.pallas_call(functools.partial(reduce_dp_kernel, n), out_shape=jax.Shap...  9.41 us
  transfers between devices with their start and end apart: 3, of which 3 were waited for; matrix products, arithmetic and copies ran while one was open for 18% of the time, Pallas kernels for 9%

profile of v13, /device:TPU:1, one launch (start us, length us, event | category | flops | bytes accessed | tf_op | source)
XLA Modules:
  0.0 377.4 jit_solution(13156719728615943712)
XLA Ops:
  7.2 0.0 all-gather.5.cloned.1.call-start
  7.2 0.7 convert_reduce_fusion
  7.9 0.1 copy.34
  8.0 0.2 reduce_window_sum.11
  8.3 0.7 select_reduce_fusion
  9.0 0.7 compare_select_fusion.3
  9.7 0.1 copy.37
  9.8 0.1 reshape.89
  9.9 0.1 reshape.137
  10.1 0.1 reshape.145
  10.2 1.4 scatter_custom_fusion.1
  11.6 1.4 scatter_custom_fusion
  13.1 0.9 concatenate.23
  14.0 3.3 gather_fusion.2
  17.3 18.0 %shard_map.181 = bf16[96,4096]{1,0:T(8,128)(2,1)} custom-call(bf16[8,96,512]{2,1,0:T(8,128)(2,1)} %bitcast.93), custom_call_target="tpu_custom_call" | custom-call | tf_op jit(solution)/shard_map/pallas_call | solution.py:251
  35.3 0.0 all-gather.5.cloned.1.call-update
  35.4 0.0 all-gather.3.cloned.1.call-start
  35.4 0.1 copy.38
  35.5 0.1 reshape.91
  35.7 5.0 %gather_fusion = f32[768]{0:T(1024)S(1)} fusion(f32[256]{0:T(256)S(1)} %reshape.91, s32[1024]{0:T(1024)S(1)} %get-tuple-element.38), kind=kCustom, calls=%fused_computation | custom fusion | bytes 9216 | tf_op jit(solution)/shard_map/gather | solution.py:343
  40.7 0.1 mul.108
  40.8 2.7 gather_fusion.1
  43.5 1.1 fusion.23.src_ref
  44.6 14.7 %shard_map.180 = bf16[96,4096]{1,0:T(8,128)(2,1)} custom-call(bf16[8,96,512]{2,1,0:T(8,128)(2,1)} %fusion.23.src_ref), custom_call_target="tpu_custom_call" | custom-call | tf_op jit(solution)/shard_map/pallas_call | solution.py:251
  59.2 0.0 all-gather.3.cloned.1.call-update
  59.3 0.4 reduce-scatter.4.cloned.1.call-start
  59.8 65.5 %all-gather.5.cloned.1.call-done = bf16[1536,4096]{1,0:T(8,128)(2,1)} async-done(((bf16[96,4096]{1,0:T(8,128)(2,1)}), bf16[1536,4096]{1,0:T(8,128)(2,1)}) %all-gather.5.cloned.1.call-update) | async-done | bytes 12582928 | tf_op jit(solution)/shard_map/all_gather | solution.py:355
  125.3 8.1 %convolution_convert_fusion.5 = bf16[1536,16]{0,1:T(8,128)(2,1)S(1)} fusion(bf16[1536,4096]{1,0:T(8,128)(2,1)} %all-gather.5.cloned.1.call-done, bf16[1,16,4096]{2,1,0:T(8,128)(2,1)S(1)} %copy-done.11), kind=kOutput, calls=%fused_computation.43 | convolution fusion | flops 201351168 | bytes 12763136 | tf_op jit(solution)/shard_map/dot_general | solution.py:18
  133.3 0.1 copy-done.1
  133.4 8.0 %fusion.45 = f32[1536,448]{0,1:T(8,128)S(1)} fusion(bf16[1536,4096]{1,0:T(8,128)(2,1)S(1)} %copy-done.1, bf16[1,448,4096]{2,1,0:T(8,128)(2,1)} %param.17), kind=kOutput, calls=%fused_computation.90 | convolution fusion | flops 5637144576 | bytes 19005440 | tf_op jit(solution)/shard_map/dot_general | solution.py:18
  141.4 0.6 fusion.14
  142.0 3.3 convolution_convert_fusion.4
  145.3 17.2 %fusion.43 = f32[1536,448]{0,1:T(8,128)S(1)} fusion(bf16[1536,4096]{1,0:T(8,128)(2,1)S(1)} %copy-done.1, bf16[1,448,4096]{2,1,0:T(8,128)(2,1)S(1)} %copy-done.17), kind=kOutput, calls=%fused_computation.88 | convolution fusion | flops 5637144576 | bytes 19005440 | tf_op jit(solution)/shard_map/dot_general | solution.py:18
  162.5 4.0 %multiply_convert_fusion.2 = (bf16[448,1536]{1,0:T(8,128)(2,1)}, f32[448,1536]{1,0:T(8,128)}, f32[448,1536]{1,0:T(8,128)}, f32[448,1536]{1,0:T(8,128)S(1)}) fusion(f32[448,1536]{1,0:T(8,128)S(1)} %fusion.14, f32[1536,448]{0,1:T(8,128)S(1)} %fusion.43, bf16[1536,16]{0,1:T(8,128)(2,1)S(1)} %convolution_convert_fusion.4, bf16[1,448,16]{1,2,0:T(8,128)(2,1)S(1)} %copy-done), kind=kOutput, calls=%fused_computation.37 | convolution fusion | flops 27525120 | bytes 15202304 | tf_op jit(solution)/shard_map/dot_general | solution.py:18
  166.6 1.5 copy-done.8
  168.1 0.9 convolution_convert_fusion.3
  168.9 48.2 %all-gather.3.cloned.1.call-done = bf16[1536,4096]{1,0:T(8,128)(2,1)} async-done(((bf16[96,4096]{1,0:T(8,128)(2,1)}), bf16[1536,4096]{1,0:T(8,128)(2,1)}) %all-gather.3.cloned.1.call-update) | async-done | bytes 12582928 | tf_op jit(solution)/shard_map/all_gather | solution.py:357
  217.1 11.5 %fusion.8 = f32[464,1536]{1,0:T(8,128)} fusion(bf16[1536,4096]{1,0:T(8,128)(2,1)} %all-gather.3.cloned.1.call-done, bf16[16,4096]{1,0:T(8,128)(2,1)} %bitcast.104, bf16[448,4096]{1,0:T(8,128)(2,1)} %bitcast.101), kind=kOutput, calls=%fused_computation.17 | convolution fusion | flops 5846073344 | bytes 19234816 | tf_op jit(solution)/shard_map/dot_general | solution.py:18
  228.7 3.1 multiply_convert_fusion.1
  231.8 0.3 convolution_convert_fusion.1
  232.1 0.3 convolution_convert_fusion.2
  232.4 18.5 %convolution_convert_fusion = bf16[1536,4096]{1,0:T(8,128)(2,1)} fusion(bf16[16,4096]{1,0:T(8,128)(2,1)S(1)} %get-tuple-element.39, bf16[16,4096]{1,0:T(8,128)(2,1)S(1)} %get-tuple-element.40, bf16[448,4096]{1,0:T(8,128)(2,1)} %bitcast.102, bf16[448,4096]{1,0:T(8,128)(2,1)} %bitcast.103, bf16[32,1536]{1,0:T(8,128)(2,1)S(1)} %maximum_bitcast_fusion, ...), kind=kOutput, calls=%fused_computation.6 | convolution fusion | flops 11722194944 | bytes 23035904 | tf_op jit(solution)/shard_map/dot_general | solution.py:174
  250.9 0.0 reduce-scatter.4.cloned.1.call-update
  250.9 0.1 copy.40
  251.1 0.1 reshape.127
  251.2 0.2 copy.41
  251.5 1.2 reshape.96.src_ref
  252.7 9.4 %shard_map.183.src_ref = f32[36,128]{1,0:T(8,128)} custom-call(bf16[16,36,128]{2,1,0:T(8,128)(2,1)} %reshape.96.src_ref), custom_call_target="tpu_custom_call" | custom-call | tf_op jit(solution)/shard_map/pallas_call | solution.py:289
  262.1 11.6 %shard_map.184 = f32[16,36,128]{2,1,0:T(8,128)} custom-call(f32[36,128]{1,0:T(8,128)} %shard_map.183.src_ref), custom_call_target="tpu_custom_call" | custom-call | tf_op jit(solution)/shard_map/pallas_call | solution.py:212
  273.7 1.3 reshape.97
  275.1 1.1 fusion.25
  276.2 1.1 fusion.26
  277.3 2.3 fusion.24
  279.6 7.5 %convolution_multiply_fusion = f32[32,4096]{1,0:T(8,128)S(1)} fusion(bf16[1536,4096]{1,0:T(8,128)(2,1)} %all-gather.5.cloned.1.call-done, bf16[1536,48]{1,0:T(8,128)(2,1)S(1)} %reshape.97), kind=kOutput, calls=%fused_computation.14 | convolution fusion | flops 402784256 | bytes 13254656 | tf_op jit(solution)/shard_map/dot_general | solution.py:18
  287.1 0.8 slice_bitcast_fusion
  288.0 2.6 fusion.7
  290.5 57.4 %reduce-scatter.4.cloned.1.call-done = bf16[1,96,4096]{2,1,0:T(8,128)(2,1)} async-done(((bf16[16,96,4096]{2,1,0:T(8,128)(2,1)}), bf16[1,96,4096]{2,1,0:T(8,128)(2,1)}) %reduce-scatter.4.cloned.1.call-update) | async-done | bytes 786448
  347.9 1.4 copy.42
  349.3 1.1 copy.44
  350.5 16.2 %shard_map.182 = bf16[96,4096]{1,0:T(8,128)(2,1)} custom-call(bf16[8,96,512]{2,1,0:T(8,128)(2,1)} %bitcast.95), custom_call_target="tpu_custom_call" | custom-call | tf_op jit(solution)/shard_map/pallas_call | solution.py:251
  366.7 1.4 reshape.100
  368.1 1.0 gather_fusion.3
  369.0 0.3 reshape.130
  369.4 1.3 reduce_sum.29
  (54 shorter events, 0.3 us)
Async XLA Ops:
  7.2 155.3 %copy-start = (bf16[1,448,16]{1,2,0:T(8,128)(2,1)S(1)}, bf16[1,448,16]{1,2,0:T(8,128)(2,1)}, u32[]{:S(2)}) copy-start(bf16[1,448,16]{1,2,0:T(8,128)(2,1)} %param.23) | copy-start | bytes 43012
  7.2 118.1 %all-gather.5.cloned.1.call-start = ((), (), s32[]{:S(2)}) async-start(), calls=%async_computation.2 | async-start | bytes 13369344 | tf_op jit(solution)/shard_map/all_gather | solution.py:355
  14.0 21.4 %copy-start.16 = (f32[128,2]{0,1:T(2,128)S(1)}, f32[128,2]{0,1:T(2,128)}, u32[]{:S(2)}) copy-start(f32[128,2]{0,1:T(2,128)} %param.16) | copy-start | bytes 3076
  35.3 5.4 %copy-start.13 = (bf16[128,512]{1,0:T(8,128)(2,1)S(1)}, bf16[128,512]{1,0:T(8,128)(2,1)}, u32[]{:S(2)}) copy-start(bf16[128,512]{1,0:T(8,128)(2,1)} %param.14) | copy-start | bytes 393220
  35.4 181.8 %all-gather.3.cloned.1.call-start = ((), (), s32[]{:S(2)}) async-start(), calls=%async_computation.1 | async-start | bytes 13369344 | tf_op jit(solution)/shard_map/all_gather | solution.py:357
  43.5 16.2 %copy-start.11 = (bf16[1,16,4096]{2,1,0:T(8,128)(2,1)S(1)}, bf16[1,16,4096]{2,1,0:T(8,128)(2,1)}, u32[]{:S(2)}) copy-start(bf16[1,16,4096]{2,1,0:T(8,128)(2,1)} %param.20) | copy-start | bytes 393220
  43.5 16.2 %copy-start.12 = (bf16[1,16,4096]{2,1,0:T(8,128)(2,1)S(1)}, bf16[1,16,4096]{2,1,0:T(8,128)(2,1)}, u32[]{:S(2)}) copy-start(bf16[1,16,4096]{2,1,0:T(8,128)(2,1)} %param.22) | copy-start | bytes 393220
  59.3 288.7 %reduce-scatter.4.cloned.1.call-start = ((), (), s32[]{:S(2)}) async-start(), calls=%async_computation.3 | async-start | bytes 13369344
  125.3 8.2 %copy-start.1 = (bf16[1536,4096]{1,0:T(8,128)(2,1)S(1)}, bf16[1536,4096]{1,0:T(8,128)(2,1)}, u32[]{:S(2)}) copy-start(bf16[1536,4096]{1,0:T(8,128)(2,1)} %all-gather.5.cloned.1.call-done) | copy-start | bytes 37748740
  133.4 8.0 %copy-start.14 = (bf16[1,448,16]{1,2,0:T(8,128)(2,1)S(1)}, bf16[1,448,16]{1,2,0:T(8,128)(2,1)}, u32[]{:S(2)}) copy-start(bf16[1,448,16]{1,2,0:T(8,128)(2,1)} %param.21) | copy-start | bytes 43012
  142.0 3.4 copy-start.17
  162.5 5.5 %copy-start.15 = (bf16[1,16,448]{2,1,0:T(8,128)(2,1)S(1)}, bf16[1,16,448]{2,1,0:T(8,128)(2,1)}, u32[]{:S(2)}) copy-start(bf16[1,16,448]{2,1,0:T(8,128)(2,1)} %param.24) | copy-start | bytes 43012
  166.6 1.5 copy-start.8
  217.1 11.5 %copy-start.6 = (f32[448,1536]{1,0:T(8,128)S(1)}, f32[448,1536]{1,0:T(8,128)}, u32[]{:S(2)}) copy-start(f32[448,1536]{1,0:T(8,128)} %get-tuple-element.20) | copy-start | bytes 8257540
  217.1 11.5 %copy-start.7 = (f32[448,1536]{1,0:T(8,128)S(1)}, f32[448,1536]{1,0:T(8,128)}, u32[]{:S(2)}) copy-start(f32[448,1536]{1,0:T(8,128)} %get-tuple-element.18) | copy-start | bytes 8257540
  217.1 11.5 %copy-start.9 = (f32[448,1536]{1,0:T(8,128)S(1)}, f32[448,1536]{1,0:T(8,128)}, u32[]{:S(2)}) copy-start(f32[448,1536]{1,0:T(8,128)} %copy-done.8) | copy-start | bytes 8257540
  231.8 19.1 %copy-start.2 = (bf16[448,1536]{1,0:T(8,128)(2,1)}, bf16[448,1536]{1,0:T(8,128)(2,1)S(1)}, u32[]{:S(2)}) copy-start(bf16[448,1536]{1,0:T(8,128)(2,1)S(1)} %get-tuple-element.25) | copy-start | bytes 4128772
  231.8 19.1 %copy-start.4 = (bf16[448,1536]{1,0:T(8,128)(2,1)}, bf16[448,1536]{1,0:T(8,128)(2,1)S(1)}, u32[]{:S(2)}) copy-start(bf16[448,1536]{1,0:T(8,128)(2,1)S(1)} %get-tuple-element.26) | copy-start | bytes 4128772
  250.9 24.1 %copy-start.5 = (bf16[448,1536]{1,0:T(8,128)(2,1)S(1)}, bf16[448,1536]{1,0:T(8,128)(2,1)}, u32[]{:S(2)}) copy-start(bf16[448,1536]{1,0:T(8,128)(2,1)} %copy-done.4) | copy-start | bytes 4128772
  250.9 25.2 %copy-start.3 = (bf16[448,1536]{1,0:T(8,128)(2,1)S(1)}, bf16[448,1536]{1,0:T(8,128)(2,1)}, u32[]{:S(2)}) copy-start(bf16[448,1536]{1,0:T(8,128)(2,1)} %copy-done.2) | copy-start | bytes 4128772
  275.1 2.2 copy-start.10
  276.2 11.8 %slice-start = ((s8[12582912]{0:T(1024)(128)(4,1)}), s8[4194304]{0:T(1024)(128)(4,1)S(1)}, s32[]{:S(2)}) async-start(s8[12582912]{0:T(1024)(128)(4,1)} %bitcast.89), calls=%async_computation.4 | async-start | bytes 8388608
  279.6 8.3 %slice-start.1 = ((s8[12582912]{0:T(1024)(128)(4,1)}), s8[4194304]{0:T(1024)(128)(4,1)S(1)}, s32[]{:S(2)}) async-start(s8[12582912]{0:T(1024)(128)(4,1)} %bitcast.89), calls=%async_computation.5 | async-start | bytes 8388608
  279.6 8.3 %slice-start.2 = ((s8[12582912]{0:T(1024)(128)(4,1)}), s8[4194304]{0:T(1024)(128)(4,1)S(1)}, s32[]{:S(2)}) async-start(s8[12582912]{0:T(1024)(128)(4,1)} %bitcast.89), calls=%async_computation.6 | async-start | bytes 8388608
Sparse Core Ops, SparseCore 0:
  35.5 89.7 all-gather.4
  127.5 89.6 all-gather.2
  251.0 96.8 reduce-scatter.3

commit v14 on v13

--- a/solution.py
+++ b/solution.py
@@ -219,7 +219,7 @@
     )(block)
 
 
-def a2a_expert_kernel(n, width, src_ref, out_ref, send_sem, recv_sem):
+def a2a_expert_kernel(n, width, sliced, src_ref, out_ref, send_sem, recv_sem):
     me = lax.axis_index("expert")
     row = lax.axis_index("dp")
     barrier = pltpu.get_barrier_semaphore()
@@ -231,8 +231,12 @@
     copies = []
     for k in range(1, n):
         peer = lax.rem(me + k, n)
+        if sliced:
+            block = src_ref.at[:, pl.ds(pl.multiple_of(peer * width, width), width)]
+        else:
+            block = src_ref.at[peer]
         cp = pltpu.make_async_remote_copy(
-            src_ref.at[peer],
+            block,
             out_ref.at[:, mine],
             send_sem.at[k],
             recv_sem.at[k],
@@ -241,15 +245,22 @@
         )
         cp.start()
         copies.append(cp)
-    out_ref[:, mine] = src_ref[me]
+    if sliced:
+        out_ref[:, mine] = src_ref[:, mine]
+    else:
+        out_ref[:, mine] = src_ref[me]
     for cp in copies:
         cp.wait()
 
 
-def a2a_expert(send, exchange_id):
-    n, rows, width = send.shape
+def a2a_expert(send, exchange_id, n=None):
+    sliced = n is not None
+    if sliced:
+        rows, width = send.shape[0], send.shape[1] // n
+    else:
+        n, rows, width = send.shape
     return pl.pallas_call(
-        functools.partial(a2a_expert_kernel, n, width),
+        functools.partial(a2a_expert_kernel, n, width, sliced),
         out_shape=jax.ShapeDtypeStruct((rows, n * width), send.dtype),
         in_specs=[pl.BlockSpec(memory_space=pltpu.VMEM)],
         out_specs=pl.BlockSpec(memory_space=pltpu.VMEM),
@@ -368,9 +379,7 @@
     grad_b_down = ADAPTER_SCALE * contract_pair(
         dy_rows, parts_sum[:, 2 * adapter_rank:3 * adapter_rank], 0, 0
     )
-    returned_rows = a2a_expert(
-        summed.reshape(capacity, experts, feat_local).transpose(1, 0, 2), 4
-    ).astype(jnp.float32)
+    returned_rows = a2a_expert(summed, 4, experts).astype(jnp.float32)
     lookup = positions * experts + routing
     grad_x = jnp.sum(returned_rows.reshape(capacity * experts, feat_local)[lookup], axis=1).astype(
         jnp.bfloat16

time: 382 us -> 380 us (level)
  waiting for transfers between devices: 171 us -> 182 us
  matrix products: 90.3 us -> 79.5 us
    all_gather x1, waiting for transfers between devices: 48.2 us -> 59.2 us  [local(): dy_rows = lax.all_gather(dy_block, 'dp', axis=0, tiled=True)]
    dot_general x16, matrix products: 71.8 us -> 60.9 us  [contract_pair(): lax.dot_general(left, right, (((left_axis,), (right_axis,)), ((), ())), p...]
  transfers between devices with their start and end apart: 3 -> 3, of which waited for: 3 -> 3; matrix products, arithmetic and copies ran while one was open for 18% -> 16% of each run, Pallas kernels for 9% -> 10%
where the time goes in v14:
time: 380 us; the launch traced here: 375 us
  waiting for transfers between devices  182 us (48%)
  matrix products  79.5 us (21%)
  Pallas kernels  69.8 us (18%)
  local copies, waits for them, and re-layouts  24 us (6%)
  between operations  14.4 us (4%)
  other arithmetic  4.79 us (1%)
    all_gather x1, waiting for transfers between devices, local(): x_rows = lax.all_gather(x_block, 'dp', axis=0, tiled=True)  65.7 us
    dot_general x16, matrix products, contract_pair(): lax.dot_general(left, right, (((left_axis,), (right_axis,)), ((), ())), p...  60.9 us
    all_gather x1, waiting for transfers between devices, local(): dy_rows = lax.all_gather(dy_block, 'dp', axis=0, tiled=True)  59.2 us
    unnamed x4, waiting for transfers between devices  57.4 us
    pallas_call x3, Pallas kernels, a2a_expert(): pl.pallas_call(functools.partial(a2a_expert_kernel, n, width, sliced), ou...  48.8 us
    dot_general x1, matrix products, rows_backward_parts(): lax.dot_general(lhs, extended, (((0,), (0,)), ((), ())), preferred_elemen...  18.6 us
    pallas_call x1, Pallas kernels, gather_dp(): pl.pallas_call(functools.partial(gather_dp_kernel, n), out_shape=jax.Shap...  11.6 us
    pallas_call x1, Pallas kernels, reduce_dp(): pl.pallas_call(functools.partial(reduce_dp_kernel, n), out_shape=jax.Shap...  9.42 us
  transfers between devices with their start and end apart: 3, of which 3 were waited for; matrix products, arithmetic and copies ran while one was open for 16% of the time, Pallas kernels for 10%

profile of v14, /device:TPU:1, one launch (start us, length us, event | category | flops | bytes accessed | tf_op | source)
XLA Modules:
  0.0 375.0 jit_solution(9837249032260780710)
XLA Ops:
  7.2 0.0 copy-start
  7.2 0.0 all-gather.5.cloned.1.call-start
  7.2 0.7 convert_reduce_fusion
  7.9 0.1 copy.32
  8.0 0.2 reduce_window_sum.11
  8.3 0.7 select_reduce_fusion
  9.0 0.7 compare_select_fusion.3
  9.7 0.1 copy.35
  9.8 0.1 reshape.89
  9.9 0.1 reshape.137
  10.1 0.1 reshape.145
  10.2 1.4 scatter_custom_fusion.1
  11.6 1.4 scatter_custom_fusion
  13.1 0.9 concatenate.23
  14.0 3.3 gather_fusion.2
  17.3 18.0 %shard_map.181 = bf16[96,4096]{1,0:T(8,128)(2,1)} custom-call(bf16[8,96,512]{2,1,0:T(8,128)(2,1)} %bitcast.88), custom_call_target="tpu_custom_call" | custom-call | tf_op jit(solution)/shard_map/pallas_call | solution.py:262
  35.3 0.0 copy-start.13
  35.3 0.0 all-gather.5.cloned.1.call-update
  35.4 0.0 all-gather.3.cloned.1.call-start
  35.4 0.1 copy.36
  35.5 0.1 reshape.91
  35.7 5.0 %gather_fusion = f32[768]{0:T(1024)S(1)} fusion(f32[256]{0:T(256)S(1)} %reshape.91, s32[1024]{0:T(1024)S(1)} %get-tuple-element.38), kind=kCustom, calls=%fused_computation | custom fusion | bytes 9216 | tf_op jit(solution)/shard_map/gather | solution.py:354
  40.7 0.1 mul.108
  40.8 2.7 gather_fusion.1
  43.5 1.1 fusion.23.src_ref
  44.6 14.7 %shard_map.180 = bf16[96,4096]{1,0:T(8,128)(2,1)} custom-call(bf16[8,96,512]{2,1,0:T(8,128)(2,1)} %fusion.23.src_ref), custom_call_target="tpu_custom_call" | custom-call | tf_op jit(solution)/shard_map/pallas_call | solution.py:262
  59.2 0.0 all-gather.3.cloned.1.call-update
  59.3 0.2 reduce-scatter.4.cloned.1.call-start
  59.6 65.7 %all-gather.5.cloned.1.call-done = bf16[1536,4096]{1,0:T(8,128)(2,1)} async-done(((bf16[96,4096]{1,0:T(8,128)(2,1)}), bf16[1536,4096]{1,0:T(8,128)(2,1)}) %all-gather.5.cloned.1.call-update) | async-done | bytes 12582928 | tf_op jit(solution)/shard_map/all_gather | solution.py:366
  125.3 8.1 %convolution_convert_fusion.5 = bf16[1536,16]{0,1:T(8,128)(2,1)S(1)} fusion(bf16[1536,4096]{1,0:T(8,128)(2,1)} %all-gather.5.cloned.1.call-done, bf16[1,16,4096]{2,1,0:T(8,128)(2,1)S(1)} %copy-done.11), kind=kOutput, calls=%fused_computation.43 | convolution fusion | flops 201351168 | bytes 12763136 | tf_op jit(solution)/shard_map/dot_general | solution.py:18
  133.3 0.1 copy-done.1
  133.4 8.0 %fusion.45 = f32[1536,448]{0,1:T(8,128)S(1)} fusion(bf16[1536,4096]{1,0:T(8,128)(2,1)S(1)} %copy-done.1, bf16[1,448,4096]{2,1,0:T(8,128)(2,1)} %param.17), kind=kOutput, calls=%fused_computation.89 | convolution fusion | flops 5637144576 | bytes 19005440 | tf_op jit(solution)/shard_map/dot_general | solution.py:18
  141.4 0.6 fusion.14
  142.0 3.3 convolution_convert_fusion.4
  145.3 6.3 %fusion.43 = f32[1536,448]{0,1:T(8,128)S(1)} fusion(bf16[1536,4096]{1,0:T(8,128)(2,1)S(1)} %copy-done.1, bf16[1,448,4096]{2,1,0:T(8,128)(2,1)S(1)} %copy-done.17), kind=kOutput, calls=%fused_computation.87 | convolution fusion | flops 5637144576 | bytes 19005440 | tf_op jit(solution)/shard_map/dot_general | solution.py:18
  151.7 3.9 %multiply_convert_fusion.2 = (bf16[448,1536]{1,0:T(8,128)(2,1)}, f32[448,1536]{1,0:T(8,128)}, f32[448,1536]{1,0:T(8,128)}, f32[448,1536]{1,0:T(8,128)S(1)}) fusion(f32[448,1536]{1,0:T(8,128)S(1)} %fusion.14, f32[1536,448]{0,1:T(8,128)S(1)} %fusion.43, bf16[1536,16]{0,1:T(8,128)(2,1)S(1)} %convolution_convert_fusion.4, bf16[1,448,16]{1,2,0:T(8,128)(2,1)S(1)} %copy-done), kind=kOutput, calls=%fused_computation.37 | convolution fusion | flops 27525120 | bytes 15202304 | tf_op jit(solution)/shard_map/dot_general | solution.py:18
  155.6 1.5 copy-done.8
  157.1 0.9 convolution_convert_fusion.3
  157.9 59.2 %all-gather.3.cloned.1.call-done = bf16[1536,4096]{1,0:T(8,128)(2,1)} async-done(((bf16[96,4096]{1,0:T(8,128)(2,1)}), bf16[1536,4096]{1,0:T(8,128)(2,1)}) %all-gather.3.cloned.1.call-update) | async-done | bytes 12582928 | tf_op jit(solution)/shard_map/all_gather | solution.py:368
  217.2 11.5 %fusion.8 = f32[464,1536]{1,0:T(8,128)} fusion(bf16[1536,4096]{1,0:T(8,128)(2,1)} %all-gather.3.cloned.1.call-done, bf16[16,4096]{1,0:T(8,128)(2,1)} %bitcast.97, bf16[448,4096]{1,0:T(8,128)(2,1)} %bitcast.94), kind=kOutput, calls=%fused_computation.17 | convolution fusion | flops 5846073344 | bytes 19234816 | tf_op jit(solution)/shard_map/dot_general | solution.py:18
  228.7 3.2 multiply_convert_fusion.1
  231.8 0.3 convolution_convert_fusion.1
  232.1 0.3 convolution_convert_fusion.2
  232.4 18.6 %convolution_convert_fusion = bf16[1536,4096]{1,0:T(8,128)(2,1)} fusion(bf16[16,4096]{1,0:T(8,128)(2,1)S(1)} %get-tuple-element.39, bf16[16,4096]{1,0:T(8,128)(2,1)S(1)} %get-tuple-element.40, bf16[448,4096]{1,0:T(8,128)(2,1)} %bitcast.95, bf16[448,4096]{1,0:T(8,128)(2,1)} %bitcast.96, bf16[32,1536]{1,0:T(8,128)(2,1)S(1)} %maximum_bitcast_fusion, ...), kind=kOutput, calls=%fused_computation.6 | convolution fusion | flops 11722194944 | bytes 23035904 | tf_op jit(solution)/shard_map/dot_general | solution.py:174
  251.1 0.0 reduce-scatter.4.cloned.1.call-update
  251.1 0.1 copy.37
  251.2 0.1 reshape.127
  251.4 0.2 copy.38
  251.6 1.2 reshape.96.src_ref
  252.9 9.4 %shard_map.183.src_ref = f32[36,128]{1,0:T(8,128)} custom-call(bf16[16,36,128]{2,1,0:T(8,128)(2,1)} %reshape.96.src_ref), custom_call_target="tpu_custom_call" | custom-call | tf_op jit(solution)/shard_map/pallas_call | solution.py:300
  262.3 11.6 %shard_map.184 = f32[16,36,128]{2,1,0:T(8,128)} custom-call(f32[36,128]{1,0:T(8,128)} %shard_map.183.src_ref), custom_call_target="tpu_custom_call" | custom-call | tf_op jit(solution)/shard_map/pallas_call | solution.py:212
  273.9 1.3 reshape.97
  275.2 1.1 fusion.25
  276.4 1.1 fusion.26
  277.5 2.3 fusion.24
  279.8 7.5 %convolution_multiply_fusion = f32[32,4096]{1,0:T(8,128)S(1)} fusion(bf16[1536,4096]{1,0:T(8,128)(2,1)} %all-gather.5.cloned.1.call-done, bf16[1536,48]{1,0:T(8,128)(2,1)S(1)} %reshape.97), kind=kOutput, calls=%fused_computation.14 | convolution fusion | flops 402784256 | bytes 13254656 | tf_op jit(solution)/shard_map/dot_general | solution.py:18
  287.3 0.8 slice_bitcast_fusion
  288.2 2.6 fusion.7
  290.7 57.3 %reduce-scatter.4.cloned.1.call-done = bf16[1,96,4096]{2,1,0:T(8,128)(2,1)} async-done(((bf16[16,96,4096]{2,1,0:T(8,128)(2,1)}), bf16[1,96,4096]{2,1,0:T(8,128)(2,1)}) %reduce-scatter.4.cloned.1.call-update) | async-done | bytes 786448
  348.0 16.2 %shard_map.182 = bf16[96,4096]{1,0:T(8,128)(2,1)} custom-call(bf16[96,4096]{1,0:T(8,128)(2,1)} %bitcast.89), custom_call_target="tpu_custom_call" | custom-call | tf_op jit(solution)/shard_map/pallas_call | solution.py:262
  364.2 1.4 reshape.100
  365.7 1.0 gather_fusion.3
  366.6 0.3 reshape.130
  366.9 1.3 reduce_sum.29
  (52 shorter events, 0.3 us)
Async XLA Ops:
  7.2 144.5 %copy-start = (bf16[1,448,16]{1,2,0:T(8,128)(2,1)S(1)}, bf16[1,448,16]{1,2,0:T(8,128)(2,1)}, u32[]{:S(2)}) copy-start(bf16[1,448,16]{1,2,0:T(8,128)(2,1)} %param.23) | copy-start | bytes 43012
  7.2 118.1 %all-gather.5.cloned.1.call-start = ((), (), s32[]{:S(2)}) async-start(), calls=%async_computation.2 | async-start | bytes 13369344 | tf_op jit(solution)/shard_map/all_gather | solution.py:366
  14.0 21.4 %copy-start.16 = (f32[128,2]{0,1:T(2,128)S(1)}, f32[128,2]{0,1:T(2,128)}, u32[]{:S(2)}) copy-start(f32[128,2]{0,1:T(2,128)} %param.16) | copy-start | bytes 3076
  35.3 5.4 %copy-start.13 = (bf16[128,512]{1,0:T(8,128)(2,1)S(1)}, bf16[128,512]{1,0:T(8,128)(2,1)}, u32[]{:S(2)}) copy-start(bf16[128,512]{1,0:T(8,128)(2,1)} %param.14) | copy-start | bytes 393220
  35.4 181.8 %all-gather.3.cloned.1.call-start = ((), (), s32[]{:S(2)}) async-start(), calls=%async_computation.1 | async-start | bytes 13369344 | tf_op jit(solution)/shard_map/all_gather | solution.py:368
  43.5 16.0 %copy-start.11 = (bf16[1,16,4096]{2,1,0:T(8,128)(2,1)S(1)}, bf16[1,16,4096]{2,1,0:T(8,128)(2,1)}, u32[]{:S(2)}) copy-start(bf16[1,16,4096]{2,1,0:T(8,128)(2,1)} %param.20) | copy-start | bytes 393220
  43.5 16.0 %copy-start.12 = (bf16[1,16,4096]{2,1,0:T(8,128)(2,1)S(1)}, bf16[1,16,4096]{2,1,0:T(8,128)(2,1)}, u32[]{:S(2)}) copy-start(bf16[1,16,4096]{2,1,0:T(8,128)(2,1)} %param.22) | copy-start | bytes 393220
  59.3 288.8 %reduce-scatter.4.cloned.1.call-start = ((), (), s32[]{:S(2)}) async-start(), calls=%async_computation.3 | async-start | bytes 13369344
  125.3 8.2 %copy-start.1 = (bf16[1536,4096]{1,0:T(8,128)(2,1)S(1)}, bf16[1536,4096]{1,0:T(8,128)(2,1)}, u32[]{:S(2)}) copy-start(bf16[1536,4096]{1,0:T(8,128)(2,1)} %all-gather.5.cloned.1.call-done) | copy-start | bytes 37748740
  133.4 8.0 %copy-start.14 = (bf16[1,448,16]{1,2,0:T(8,128)(2,1)S(1)}, bf16[1,448,16]{1,2,0:T(8,128)(2,1)}, u32[]{:S(2)}) copy-start(bf16[1,448,16]{1,2,0:T(8,128)(2,1)} %param.21) | copy-start | bytes 43012
  142.0 3.4 copy-start.17
  151.7 5.4 %copy-start.15 = (bf16[1,16,448]{2,1,0:T(8,128)(2,1)S(1)}, bf16[1,16,448]{2,1,0:T(8,128)(2,1)}, u32[]{:S(2)}) copy-start(bf16[1,16,448]{2,1,0:T(8,128)(2,1)} %param.24) | copy-start | bytes 43012
  155.6 1.5 copy-start.8
  217.1 11.5 %copy-start.6 = (f32[448,1536]{1,0:T(8,128)S(1)}, f32[448,1536]{1,0:T(8,128)}, u32[]{:S(2)}) copy-start(f32[448,1536]{1,0:T(8,128)} %get-tuple-element.20) | copy-start | bytes 8257540
  217.1 11.5 %copy-start.7 = (f32[448,1536]{1,0:T(8,128)S(1)}, f32[448,1536]{1,0:T(8,128)}, u32[]{:S(2)}) copy-start(f32[448,1536]{1,0:T(8,128)} %get-tuple-element.18) | copy-start | bytes 8257540
  217.2 11.5 %copy-start.9 = (f32[448,1536]{1,0:T(8,128)S(1)}, f32[448,1536]{1,0:T(8,128)}, u32[]{:S(2)}) copy-start(f32[448,1536]{1,0:T(8,128)} %copy-done.8) | copy-start | bytes 8257540
  231.8 19.2 %copy-start.2 = (bf16[448,1536]{1,0:T(8,128)(2,1)}, bf16[448,1536]{1,0:T(8,128)(2,1)S(1)}, u32[]{:S(2)}) copy-start(bf16[448,1536]{1,0:T(8,128)(2,1)S(1)} %get-tuple-element.25) | copy-start | bytes 4128772
  231.8 19.2 %copy-start.4 = (bf16[448,1536]{1,0:T(8,128)(2,1)}, bf16[448,1536]{1,0:T(8,128)(2,1)S(1)}, u32[]{:S(2)}) copy-start(bf16[448,1536]{1,0:T(8,128)(2,1)S(1)} %get-tuple-element.26) | copy-start | bytes 4128772
  251.1 24.1 %copy-start.5 = (bf16[448,1536]{1,0:T(8,128)(2,1)S(1)}, bf16[448,1536]{1,0:T(8,128)(2,1)}, u32[]{:S(2)}) copy-start(bf16[448,1536]{1,0:T(8,128)(2,1)} %copy-done.4) | copy-start | bytes 4128772
  251.1 25.2 %copy-start.3 = (bf16[448,1536]{1,0:T(8,128)(2,1)S(1)}, bf16[448,1536]{1,0:T(8,128)(2,1)}, u32[]{:S(2)}) copy-start(bf16[448,1536]{1,0:T(8,128)(2,1)} %copy-done.2) | copy-start | bytes 4128772
  275.2 2.2 copy-start.10
  276.4 11.8 %slice-start = ((s8[12582912]{0:T(1024)(128)(4,1)}), s8[4194304]{0:T(1024)(128)(4,1)S(1)}, s32[]{:S(2)}) async-start(s8[12582912]{0:T(1024)(128)(4,1)} %bitcast.84), calls=%async_computation.4 | async-start | bytes 8388608
  279.8 8.3 %slice-start.1 = ((s8[12582912]{0:T(1024)(128)(4,1)}), s8[4194304]{0:T(1024)(128)(4,1)S(1)}, s32[]{:S(2)}) async-start(s8[12582912]{0:T(1024)(128)(4,1)} %bitcast.84), calls=%async_computation.5 | async-start | bytes 8388608
  279.8 8.3 %slice-start.2 = ((s8[12582912]{0:T(1024)(128)(4,1)}), s8[4194304]{0:T(1024)(128)(4,1)S(1)}, s32[]{:S(2)}) async-start(s8[12582912]{0:T(1024)(128)(4,1)} %bitcast.84), calls=%async_computation.6 | async-start | bytes 8388608
Sparse Core Ops, SparseCore 0:
  35.5 89.7 all-gather.4
  127.5 89.6 all-gather.2
  251.2 96.7 reduce-scatter.3
